TPU v7x, 32 devices: a whole 2x2x4 slice. The times are simulated.
32 devices in a mesh: gx: 4 (over z), gy: 2 (over y), gz: 4 (over x, core).
Axes of the slice: x: 2, y: 2, z: 4, core: 2. Of those that a mesh axis runs over, the one named last changes fastest.
Arguments:
- pop_ratio: float32 [19, 8, 32, 512], P(None, 'gx', 'gy', 'gz'), may hold values from 0.7 to 1.3
- solid_flags: int32 [8, 32, 512], P('gx', 'gy', 'gz'), may hold values 0 or 1
- class_ids: int32 [8, 32, 512], P('gx', 'gy', 'gz'), may hold values from 0 to 7
- drag_table: float32 [8], replicated, may hold values from 0.05 to 1
- row_map: int32 [8, 32, 512], P('gx', 'gy', 'gz'), may hold values from 0 to 4095, as said below
- old_basis: float32 [32, 16384], P(None, ('gx', 'gy', 'gz')), may hold values from -6 to 6
- old_sigma: float32 [32], replicated, may hold values from 1 to 10
Outputs:
- final_populations: float32 [19, 8, 32, 512], P(None, 'gx', 'gy', 'gz')
- new_basis: float32 [44, 16384], P(None, ('gx', 'gy', 'gz'))
- triangle: float32 [44, 44], replicated
Inputs may be any that keep to these rules, and one draw needn't show every extreme that they name: `row_map`: within each slab along the first dimension every snapshot row is named by exactly 8 voxels, and the voxels of one device name rows of each block of 512 rows exactly 512 times.
All inputs are finite; a program needn't handle non-finite values. No bound on the sum of `solid_flags` on one device may be relied on, other than what follows from the above.
Results may differ from a plain program's by a relative error of at most 0.0003.
Values sent between devices are 32-bit elements; how exact they have to be, the bound alone decides.
No kernel may reach another device: no remote copies, remote signals or barrier semaphores. Data moves between devices by JAX's collectives and lax.ppermute only.
A program may use at most 64 MiB of HBM per device.

v0:
```python
import functools

import jax
import jax.numpy as jnp
import numpy as np
from jax import lax
from jax.experimental import pallas as pl
from jax.experimental.pallas import tpu as pltpu
from jax.sharding import PartitionSpec as P


STEPS = 4
VOX_ROW = 8
LATTICE = np.array(
    [
        [0, 0, 0],
        [1, 0, 0],
        [-1, 0, 0],
        [0, 1, 0],
        [0, -1, 0],
        [0, 0, 1],
        [0, 0, -1],
        [1, 1, 0],
        [-1, -1, 0],
        [1, -1, 0],
        [-1, 1, 0],
        [1, 0, 1],
        [-1, 0, -1],
        [1, 0, -1],
        [-1, 0, 1],
        [0, 1, 1],
        [0, -1, -1],
        [0, 1, -1],
        [0, -1, 1],
    ]
)
OPPOSITE = [0, 2, 1, 4, 3, 6, 5, 8, 7, 10, 9, 12, 11, 14, 13, 16, 15, 18, 17]
WEIGHTS = [1.0 / 3.0] + [1.0 / 18.0] * 6 + [1.0 / 36.0] * 12
PAIRS = [(q, OPPOSITE[q]) for q in range(1, 19) if q < OPPOSITE[q]]
PLUS_X = [q for q in range(19) if LATTICE[q, 0] == 1]
MINUS_X = [q for q in range(19) if LATTICE[q, 0] == -1]
relax_time = 0.9
vel_scale = 16.0

FIELDS = 20
LOW = 256


def lanes(shape=(8, 128)):
    return lax.broadcasted_iota(jnp.int32, shape, len(shape) - 1)


def subs(shape=(8, 128)):
    return lax.broadcasted_iota(jnp.int32, shape, len(shape) - 2)


def roll(value, shift, axis):
    size = value.shape[axis]
    shift = shift % size
    return value if shift == 0 else pltpu.roll(value, shift, axis)


def init_kernel(table, ratio, solid, cls, g_ref, zr_ref, zl_ref, y_ref, cr_ref, cl_ref):
    lane, sub = lanes(), subs()
    blank = jnp.zeros((8, 128), jnp.float32)
    zr, zl = [blank] * 3, [blank] * 3
    cr, cl = [blank] * 2, [blank] * 2
    for f in range(FIELDS):
        tiles = {}
        for x in range(2):
            for yt in range(2):
                rows = pl.ds(8 * yt, 8)
                if f < 19:
                    tile = ratio[f, x, rows, :] * WEIGHTS[f]
                else:
                    ids = cls[x, rows, :]
                    drag = jnp.zeros((8, 128), jnp.float32)
                    for c in range(table.shape[0]):
                        drag = jnp.where(ids == c, table[c], drag)
                    tile = jnp.where(solid[x, rows, :] == 1, -1.0, 1.0 + 0.5 * drag)
                    g_ref[x, rows, :] = tile
                tiles[x, yt] = tile
                at, k = divmod(f * 4 + x * 2 + yt, 32)
                here = (lane >= 4 * k) & (lane < 4 * k + 4)
                zr[at] = jnp.where(here, roll(tile, 4 * k - 124, 1), zr[at])
                zl[at] = jnp.where(here, roll(tile, 4 * k, 1), zl[at])
        up = jnp.where(sub < 4, roll(tiles[0, 1], 4, 0), tiles[1, 1])
        down = jnp.where(sub < 4, tiles[0, 0], roll(tiles[1, 0], 4, 0))
        y_ref[f] = up
        y_ref[FIELDS + f] = down
        here = (lane >= 4 * f) & (lane < 4 * f + 4)
        for i, tile in enumerate((up, down)):
            cr[i] = jnp.where(here, roll(tile, 4 * f - 124, 1), cr[i])
            cl[i] = jnp.where(here, roll(tile, 4 * f, 1), cl[i])
    for at in range(3):
        zr_ref[at] = zr[at]
        zl_ref[at] = zl[at]
    for at in range(2):
        cr_ref[at] = cr[at]
        cl_ref[at] = cl[at]


def collide(pops, g):
    density = pops[0]
    for q in range(1, 19):
        density = density + pops[q]
    scale = 1.0 / (density * jnp.abs(g))
    speeds = []
    for a in range(3):
        total = None
        for q in range(19):
            c = LATTICE[q, a]
            if c == 1:
                total = pops[q] if total is None else total + pops[q]
            elif c == -1:
                total = total - pops[q]
        speeds.append(total * scale)
    square = speeds[0] * speeds[0] + speeds[1] * speeds[1] + speeds[2] * speeds[2]
    solid = g < 0.0
    keep = 1.0 - 1.0 / relax_time
    base = 1.0 - 1.5 * square
    part = {w: density * (w / relax_time) for w in sorted(set(WEIGHTS))}
    relaxed = [None] * 19
    rest = pops[0] * keep + part[WEIGHTS[0]] * base
    relaxed[0] = jnp.where(solid, pops[0], rest)
    for q, o in PAIRS:
        along = None
        for a in range(3):
            c = LATTICE[q, a]
            if c == 1:
                along = speeds[a] if along is None else along + speeds[a]
            elif c == -1:
                along = -speeds[a] if along is None else along - speeds[a]
        even = part[WEIGHTS[q]] * (base + 4.5 * along * along)
        odd = part[WEIGHTS[q]] * (3.0 * along)
        relaxed[q] = jnp.where(solid, pops[o], pops[q] * keep + (even + odd))
        relaxed[o] = jnp.where(solid, pops[q], pops[o] * keep + (even - odd))
    factor = jnp.where(solid, 0.0, vel_scale / VOX_ROW)
    return relaxed, [s * factor for s in speeds]


def collide_all(source, g_of, out, vel_ref, tiles=range(3)):
    for x in range(2):
        for yt in tiles:
            for lt in range(2):
                rows, cols = pl.ds(8 * yt, 8), pl.ds(128 * lt, 128)
                pops = [source[q, x, rows, cols] for q in range(19)]
                relaxed, vel = collide(pops, g_of[x, rows, cols])
                for q in range(19):
                    out[q, x, rows, cols] = relaxed[q]
                if yt < 2 and lt == 0:
                    for a in range(3):
                        vel_ref[a, x, rows, :] = vel[a]


def pack_x(out, xr_ref, xl_ref):
    lane = lanes()
    for ref, directions, x in ((xr_ref, PLUS_X, 1), (xl_ref, MINUS_X, 0)):
        extra = jnp.zeros((8, 128), jnp.float32)
        for i, q in enumerate(directions):
            for yt in range(3):
                j = 3 * i + yt
                ref[j] = out[q, x, pl.ds(8 * yt, 8), pl.ds(0, 128)]
                tile = out[q, x, pl.ds(8 * yt, 8), pl.ds(128, 128)]
                here = (lane >= 8 * j) & (lane < 8 * j + 8)
                extra = jnp.where(here, roll(tile, 4 + 8 * j, 1), extra)
        ref[15] = extra


def inner_kernel(ratio, g_in, left, right, out, g_ref, vel_ref, wide):
    lane = lanes()
    for f in range(FIELDS):
        ref = wide.at[f] if f < 19 else g_ref
        for x in range(2):
            for yt in range(2):
                rows = pl.ds(8 * yt, 8)
                own = ratio[f, x, rows, :] * WEIGHTS[f] if f < 19 else g_in[x, rows, :]
                at, k = divmod(f * 4 + x * 2 + yt, 32)
                tile = jnp.where(lane < 4, roll(right[at], -4 * k, 1), own)
                tile = jnp.where(lane >= 124, roll(left[at], 124 - 4 * k, 1), tile)
                ref[x, rows, pl.ds(0, 128)] = own
                ref[x, rows, pl.ds(128, 128)] = tile
    collide_all(wide, g_ref, out, vel_ref, range(2))


def outer_kernel(out_in, g_in, y, cr, cl, out, g_ref, xr_ref, xl_ref, wide):
    lane, sub = lanes(), subs()
    for f in range(FIELDS):
        ref = wide.at[f] if f < 19 else g_ref
        pairs = []
        for i in range(2):
            own = y[FIELDS * i + f]
            tile = jnp.where(lane < 4, roll(cl[i], -4 * f, 1), own)
            pairs.append((own, jnp.where(lane >= 124, roll(cr[i], 124 - 4 * f, 1), tile)))
        high, low = pairs
        for lt in range(2):
            cols = pl.ds(128 * lt, 128)
            ref[0, pl.ds(16, 8), cols] = jnp.where(sub < 4, low[lt], roll(high[lt], 4, 0))
            ref[1, pl.ds(16, 8), cols] = jnp.where(sub < 4, roll(low[lt], 4, 0), high[lt])
    collide_all(wide, g_ref, out, None, (2,))
    pack_x(out, xr_ref, xl_ref)


def unpack_x(xr, xl, side):
    for s, ref in enumerate((xr, xl)):
        for i in range(5):
            for yt in range(3):
                j = 3 * i + yt
                side[s, i, pl.ds(8 * yt, 8), pl.ds(0, 128)] = ref[j]
                side[s, i, pl.ds(8 * yt, 8), pl.ds(128, 128)] = roll(ref[15], -(8 * j + 4), 1)


def streamed(prev, side, q, x):
    c = [int(v) for v in LATTICE[q]]
    if c[0] == 1 and x == 0:
        value = side[0, PLUS_X.index(q)]
    elif c[0] == -1 and x == 1:
        value = side[1, MINUS_X.index(q)]
    else:
        value = prev[q, x - c[0]]
    return roll(roll(value, c[1], 0), c[2], 1)


def step_kernel(prev, g_ref, xr, xl, out, vel_ref, xr_ref, xl_ref, wide, side):
    unpack_x(xr, xl, side)
    for q in range(19):
        for x in range(2):
            wide[q, x] = streamed(prev, side, q, x)
    collide_all(wide, g_ref, out, vel_ref)
    pack_x(out, xr_ref, xl_ref)


def last_kernel(prev, xr, xl, out, side):
    unpack_x(xr, xl, side)
    for q in range(19):
        for x in range(2):
            out[q, x] = streamed(prev, side, q, x)[:16, :128]


def split(value):
    big = value.astype(jnp.bfloat16).astype(jnp.float32)
    return big, value - big


def onehot_kernel(row_map, right):
    low_at = lax.broadcasted_iota(jnp.int32, (LOW, 128), 0)
    for x in range(2):
        for y in range(16):
            rows = row_map[x, pl.ds(y, 1), :]
            low = rows - (rows // LOW) * LOW
            cols = pl.ds(128 * (16 * x + y), 128)
            right[:, cols] = jnp.where(low_at == low, 1.0, 0.0).astype(jnp.bfloat16)


def times_onehot(left, right):
    return lax.dot_general(
        left[...], right[...], (((1,), (1,)), ((), ())), preferred_element_type=jnp.float32
    )


def early_kernel(v0, v1, v2, row_map, right, out, left):
    highs = out.shape[0]
    vels = (v0, v1, v2)

    def row(i, carry):
        x, y = i // 16, i % 16
        cols = pl.ds(pl.multiple_of(128 * i, 128), 128)
        high = row_map[x, pl.ds(y, 1), :] // LOW
        vals = [v[a, x, pl.ds(y, 1), :] for v in vels for a in range(3)]
        vals = jnp.concatenate(vals + [jnp.zeros((7, 128), jnp.float32)], 0)
        big, rest = split(vals)
        for h in range(highs):
            here = high == h
            left[pl.ds(16 * h, 16), cols] = jnp.where(here, big, 0.0).astype(jnp.bfloat16)
            left[pl.ds(16 * (highs + h), 16), cols] = jnp.where(here, rest, 0.0).astype(jnp.bfloat16)
        return carry

    lax.fori_loop(0, 32, row, 0)
    both = times_onehot(left, right)
    half = 16 * highs
    for h in range(highs):
        out[h] = both[16 * h : 16 * h + 16] + both[half + 16 * h : half + 16 * h + 16]


def late_kernel(v3, row_map, right, early, out, left):
    highs = out.shape[0]
    high_at = lax.broadcasted_iota(jnp.int32, (highs, 128), 0)
    for x in range(2):
        for y in range(16):
            cols = pl.ds(128 * (16 * x + y), 128)
            here = high_at == row_map[x, pl.ds(y, 1), :] // LOW
            for a in range(3):
                for i, part in enumerate(split(v3[a, x, pl.ds(y, 1), :])):
                    left[pl.ds(highs * (3 * i + a), highs), cols] = jnp.where(here, part, 0.0).astype(jnp.bfloat16)
    both = times_onehot(left, right)
    half = 3 * highs
    both = both[:half] + both[half:]
    out[...] = early[...]
    for a in range(3):
        for h in range(highs):
            out[h, pl.ds(9 + a, 1), :] = both[highs * a + h : highs * a + h + 1]


def gram_kernel(total_rows, parts, basis, sigma, aug_ref, out, gram):
    owners = parts.shape[0] // 32
    total = parts[pl.ds(0, 32), :]
    for o in range(1, owners):
        total = total + parts[pl.ds(32 * o, 32), :]
    aug_ref[pl.ds(0, 32), :] = basis[...] * sigma[...]
    aug_ref[pl.ds(32, 16), pl.ds(0, LOW)] = total[:16]
    aug_ref[pl.ds(32, 16), pl.ds(LOW, LOW)] = total[16:]
    aug = aug_ref[...]
    product = lax.dot_general(
        aug,
        aug,
        (((1,), (1,)), ((), ())),
        precision=lax.Precision.HIGHEST,
        preferred_element_type=jnp.float32,
    ) * (1.0 / total_rows)
    gram[...] = jnp.zeros((48, 128), jnp.float32)
    gram[:, pl.ds(0, 48)] = product
    lane = lanes()
    first = gram[pl.ds(0, 8), :]
    for k in range(1, 4):
        here = (lane >= 32 * k) & (lane < 32 * k + 32)
        first = jnp.where(here, roll(gram[pl.ds(8 * k, 8), :], 32 * k, 1), first)
    second = jnp.where(lane < 64, gram[pl.ds(32, 8), :], roll(gram[pl.ds(40, 8), :], 64, 1))
    for d in range(out.shape[0]):
        out[d, pl.ds(0, 8), :] = first
        out[d, pl.ds(8, 8), :] = second


def factor_kernel(parts, aug_ref, basis_ref, tri_ref, work):
    lane = lanes()
    total = parts[0]
    for d in range(1, parts.shape[0]):
        total = total + parts[d]
    first, second = total[:8], total[8:]
    low = jnp.concatenate([jnp.where(lane < 64, second, 0.0), jnp.where(lane < 64, roll(second, -64, 1), 0.0)], 0)
    turned = low.T
    for k in range(4):
        own = jnp.where(lane < 32, roll(first, -32 * k, 1), 0.0)
        work[pl.ds(8 * k, 8), :] = own
        work[pl.ds(8 * k, 8), pl.ds(32, 16)] = turned[8 * k : 8 * k + 8]
    work[pl.ds(32, 16), :] = low
    tiles = []
    for t in range(6):
        row = lax.broadcasted_iota(jnp.int32, (8, 128), 0) + 8 * t
        tiles.append(work[pl.ds(8 * t, 8), :] + jnp.where(lane == row + 64, 1.0, 0.0))
    done = list(tiles)
    sub = subs()
    for k in range(44):
        t, r = divmod(k, 8)
        pivot_row = jnp.broadcast_to(tiles[t][r : r + 1, :], (8, 128))
        pivot = jnp.broadcast_to(pivot_row[:, k : k + 1], (8, 128))
        inv = 1.0 / jnp.sqrt(pivot)
        scaled = pivot_row * inv
        for u in range(t, 6):
            column = jnp.broadcast_to(tiles[u][:, k : k + 1], (8, 128))
            update = tiles[u] - (column * inv) * scaled
            if u == t:
                done[t] = jnp.where(sub == r, scaled, done[t])
                tiles[t] = jnp.where(sub > r, update, tiles[t])
            else:
                tiles[u] = update
    for t in range(6):
        row = sub + 8 * t
        work[pl.ds(8 * t, 8), :] = jnp.where(lane >= 64, done[t], jnp.where(lane >= row, done[t], 0.0))
        if t == 5:
            work[pl.ds(40, 8), :] = jnp.where(sub < 4, work[pl.ds(40, 8), :], 0.0)
    both = work[...]
    tri_ref[...] = both[:44, :44]
    inverse = both[:, 64:112]
    basis_ref[...] = lax.dot_general(
        inverse,
        aug_ref[...],
        (((1,), (0,)), ((), ())),
        precision=lax.Precision.HIGHEST,
        preferred_element_type=jnp.float32,
    )[:44]


def f32(*shape):
    return jax.ShapeDtypeStruct(shape, jnp.float32)


def vmem(*shape):
    return pltpu.VMEM(shape, jnp.float32)


def held(value):
    return pltpu.with_memory_space_constraint(value, pltpu.VMEM)


def call(kernel, outs, scratch=(), smem=(), count=None, aliases=None, limit=16):
    specs = [
        pl.BlockSpec(memory_space=pltpu.SMEM) if i in smem else pl.BlockSpec(memory_space=pltpu.VMEM)
        for i in range(count)
    ]
    many = isinstance(outs, (tuple, list))
    out_specs = [pl.BlockSpec(memory_space=pltpu.VMEM)] * len(outs) if many else pl.BlockSpec(memory_space=pltpu.VMEM)
    return pl.pallas_call(
        kernel, out_shape=outs, in_specs=specs, out_specs=out_specs, scratch_shapes=list(scratch),
        input_output_aliases=aliases or {},
        compiler_params=pltpu.CompilerParams(vmem_limit_bytes=limit * 2**20),
    )


def shift(value, axis, step):
    count = lax.axis_size(axis)
    return lax.ppermute(value, axis, [(i, (i + step) % count) for i in range(count)])


def shift_both(value, step_y, step_z):
    ny, nz = lax.axis_size("gy"), lax.axis_size("gz")
    pairs = [
        (y * nz + z, (y + step_y) % ny * nz + (z + step_z) % nz) for y in range(ny) for z in range(nz)
    ]
    return lax.ppermute(value, ("gy", "gz"), pairs)


def across(value, step_z):
    if lax.axis_size("gy") == 2:
        return shift_both(value, 1, step_z)
    half = value.shape[0] // 2
    return jnp.concatenate([shift_both(value[:half], 1, step_z), shift_both(value[half:], -1, step_z)], 0)


def on_device(pop_ratio, solid_flags, class_ids, drag_table, row_map, old_basis, old_sigma):
    slab = ("gy", "gz")
    everyone = ("gx", "gy", "gz")
    owners = lax.axis_size(slab)
    devices = lax.axis_size(everyone)
    rows_local = old_basis.shape[1]
    highs = owners * rows_local // LOW
    cells = 4096
    tile = (8, 128)

    g, zr, zl, y, cr, cl = call(
        init_kernel,
        (vmem(2, 16, 128), vmem(3, *tile), vmem(3, *tile), vmem(2 * FIELDS, *tile), vmem(2, *tile), vmem(2, *tile)),
        smem=(0,),
        count=4,
    )(drag_table, pop_ratio, solid_flags, class_ids)
    y = across(y, 0)
    left, right = shift(zr, "gz", 1), shift(zl, "gz", -1)
    cr, cl = across(cr, 1), across(cl, -1)

    wide = pltpu.VMEM((19, 2, 24, 256), jnp.float32)
    side = pltpu.VMEM((2, 5, 24, 256), jnp.float32)
    big, wall, vel, face = vmem(19, 2, 24, 256), vmem(2, 24, 256), vmem(3, 2, 16, 128), vmem(16, *tile)
    relaxed, g_wide, v0 = call(inner_kernel, (big, wall, vel), (wide,), count=4)(
        pop_ratio, *map(held, (g, left, right))
    )
    relaxed, g_wide, xr, xl = call(
        outer_kernel, (big, wall, face, face), (wide,), count=5, aliases={0: 0, 1: 1}
    )(*map(held, (relaxed, g_wide, y, cr, cl)))
    vels = [v0]
    step = jax.jit(call(step_kernel, (big, vel, face, face), (wide, side), count=4))
    onehot = call(onehot_kernel, pltpu.VMEM((LOW, cells), jnp.bfloat16), count=1)(row_map)
    for _ in range(1, STEPS):
        xr, xl = shift(xr, "gx", 1), shift(xl, "gx", -1)
        relaxed, vel_s, xr, xl = step(*map(held, (relaxed, g_wide, xr, xl)))
        vels.append(vel_s)
    xr, xl = shift(xr, "gx", 1), shift(xl, "gx", -1)

    early = call(
        early_kernel, vmem(highs, 16, LOW), (pltpu.VMEM((32 * highs, cells), jnp.bfloat16),), count=5,
        limit=8 + highs // 2,
    )(*map(held, vels[:3]), row_map, held(onehot))
    term = call(
        late_kernel, f32(highs, 16, LOW), (pltpu.VMEM((6 * highs, cells), jnp.bfloat16),), count=4,
        limit=8 + highs // 2,
    )(held(vels[3]), row_map, held(onehot), held(early))
    parts = lax.all_to_all(term.reshape(16 * highs, LOW), slab, 0, 0, tiled=True)
    aug, gram = call(
        functools.partial(gram_kernel, float(rows_local * devices)),
        (vmem(48, rows_local), f32(devices, 16, 128)),
        (pltpu.VMEM((48, 128), jnp.float32),),
        count=3,
    )(held(parts), old_basis, old_sigma[:, None])
    grams = lax.all_to_all(gram, everyone, 0, 0, tiled=True)
    new_basis, upper = call(
        factor_kernel, (f32(44, rows_local), f32(44, 44)), (pltpu.VMEM((48, 128), jnp.float32),), count=2
    )(held(grams), held(aug))
    populations = call(last_kernel, f32(19, 2, 16, 128), (side,), count=3)(*map(held, (relaxed, xr, xl)))
    return (populations, new_basis, upper)


def solution(mesh):
    in_specs = (
        P(None, "gx", "gy", "gz"),
        P("gx", "gy", "gz"),
        P("gx", "gy", "gz"),
        P(),
        P("gx", "gy", "gz"),
        P(None, ("gx", "gy", "gz")),
        P(),
    )
    out_specs = (P(None, "gx", "gy", "gz"), P(None, ("gx", "gy", "gz")), P())

    return jax.shard_map(on_device, mesh=mesh, in_specs=in_specs, out_specs=out_specs, check_vma=False)
```

profile of v0, /device:TPU:0, one launch (start us, length us, event | category | flops | bytes accessed | tf_op | source)
XLA Modules:
  0.0 72.4 jit_solution(3555908378340380480)
XLA Ops:
  0.6 1.0 %copy-done = f32[19,2,16,128]{3,2,1,0:T(8,128)S(1)} copy-done((f32[19,2,16,128]{3,2,1,0:T(8,128)S(1)}, f32[19,2,16,128]{3,2,1,0:T(8,128)}, u32[]{:S(2)}) %copy-start) | copy-done | bytes 311320
  4.6 3.1 %collective-permute-start.2 = (f32[40,8,128]{2,1,0:T(8,128)S(1)}, f32[40,8,128]{2,1,0:T(8,128)S(1)}, u32[]{:S(2)}, u32[]{:S(2)}) collective-permute-start(f32[40,8,128]{2,1,0:T(8,128)S(1)} %get-tuple-element.37), channel_id=1, source_target_pairs={{0,4},{1,5},{2,6},{3,7},{4,0},{5,1},{6,2},{7,3},{8,12},{9,13},{10,... | collective-permute-start | bytes 491528 | tf_op jit(solution)/shard_map/ppermute | solution.py:419
  7.6 1.7 %collective-permute-start.1 = (f32[3,8,128]{2,1,0:T(8,128)S(1)}, f32[3,8,128]{2,1,0:T(8,128)S(1)}, u32[]{:S(2)}, u32[]{:S(2)}) collective-permute-start(f32[3,8,128]{2,1,0:T(8,128)S(1)} %get-tuple-element.34), channel_id=1, source_target_pairs={{0,3},{1,0},{2,1},{3,2},{4,7},{5,4},{6,5},{7,6},{8,11},{9,8},{10,9... | collective-permute-start | bytes 36872 | tf_op jit(solution)/shard_map/ppermute | solution.py:411
  9.4 2.6 %collective-permute-start.4 = (f32[2,8,128]{2,1,0:T(8,128)S(1)}, f32[2,8,128]{2,1,0:T(8,128)S(1)}, u32[]{:S(2)}, u32[]{:S(2)}) collective-permute-start(f32[2,8,128]{2,1,0:T(8,128)S(1)} %get-tuple-element.39), channel_id=1, source_target_pairs={{0,7},{1,4},{2,5},{3,6},{4,3},{5,0},{6,1},{7,2},{8,15},{9,12},{10,... | collective-permute-start | bytes 24584 | tf_op jit(solution)/shard_map/ppermute | solution.py:419
  12.0 1.0 %copy-done.1 = f32[19,2,16,128]{3,2,1,0:T(8,128)S(1)} copy-done((f32[19,2,16,128]{3,2,1,0:T(8,128)S(1)}, f32[19,2,16,128]{3,2,1,0:T(8,128)}, u32[]{:S(2)}) %copy-start.1) | copy-done | bytes 311320
  13.7 1.6 %collective-permute-start.5 = (f32[16,8,128]{2,1,0:T(8,128)S(1)}, f32[16,8,128]{2,1,0:T(8,128)S(1)}, u32[]{:S(2)}, u32[]{:S(2)}) collective-permute-start(f32[16,8,128]{2,1,0:T(8,128)S(1)} %get-tuple-element.42), channel_id=1, source_target_pairs={{0,8},{8,16},{16,24},{24,0},{1,9},{9,17},{17,25},{25,1},{2,10},{10... | collective-permute-start | bytes 196616 | tf_op jit(solution)/shard_map/ppermute | solution.py:411
  15.3 2.2 %collective-permute-start.6 = (f32[16,8,128]{2,1,0:T(8,128)S(1)}, f32[16,8,128]{2,1,0:T(8,128)S(1)}, u32[]{:S(2)}, u32[]{:S(2)}) collective-permute-start(f32[16,8,128]{2,1,0:T(8,128)S(1)} %get-tuple-element.43), channel_id=1, source_target_pairs={{0,24},{8,0},{16,8},{24,16},{1,25},{9,1},{17,9},{25,17},{2,26},{10... | collective-permute-start | bytes 196616 | tf_op jit(solution)/shard_map/ppermute | solution.py:411
  17.6 2.5 %collective-permute-done.5.xr = f32[16,8,128]{2,1,0:T(8,128)S(1)} collective-permute-done((f32[16,8,128]{2,1,0:T(8,128)S(1)}, f32[16,8,128]{2,1,0:T(8,128)S(1)}, u32[]{:S(2)}, u32[]{:S(2)}) %collective-permute-start.5) | collective-permute-done | bytes 65568 | tf_op jit(solution)/shard_map/ppermute | solution.py:411
  20.1 1.4 %collective-permute-done.6.xl = f32[16,8,128]{2,1,0:T(8,128)S(1)} collective-permute-done((f32[16,8,128]{2,1,0:T(8,128)S(1)}, f32[16,8,128]{2,1,0:T(8,128)S(1)}, u32[]{:S(2)}, u32[]{:S(2)}) %collective-permute-start.6) | collective-permute-done | bytes 65568 | tf_op jit(solution)/shard_map/ppermute | solution.py:411
  22.1 1.0 %collective-permute-start.7 = (f32[16,8,128]{2,1,0:T(8,128)S(1)}, f32[16,8,128]{2,1,0:T(8,128)S(1)}, u32[]{:S(2)}, u32[]{:S(2)}) collective-permute-start(f32[16,8,128]{2,1,0:T(8,128)S(1)} %get-tuple-element.45), channel_id=1, source_target_pairs={{0,8},{8,16},{16,24},{24,0},{1,9},{9,17},{17,25},{25,1},{2,10},{10... | collective-permute-start | bytes 196616 | tf_op jit(solution)/shard_map/ppermute | solution.py:411
  23.1 2.9 %collective-permute-start.8 = (f32[16,8,128]{2,1,0:T(8,128)S(1)}, f32[16,8,128]{2,1,0:T(8,128)S(1)}, u32[]{:S(2)}, u32[]{:S(2)}) collective-permute-start(f32[16,8,128]{2,1,0:T(8,128)S(1)} %get-tuple-element.46), channel_id=1, source_target_pairs={{0,24},{8,0},{16,8},{24,16},{1,25},{9,1},{17,9},{25,17},{2,26},{10... | collective-permute-start | bytes 196616 | tf_op jit(solution)/shard_map/ppermute | solution.py:411
  26.0 2.8 %collective-permute-done.7.xr = f32[16,8,128]{2,1,0:T(8,128)S(1)} collective-permute-done((f32[16,8,128]{2,1,0:T(8,128)S(1)}, f32[16,8,128]{2,1,0:T(8,128)S(1)}, u32[]{:S(2)}, u32[]{:S(2)}) %collective-permute-start.7) | collective-permute-done | bytes 65568 | tf_op jit(solution)/shard_map/ppermute | solution.py:411
  29.8 3.4 %collective-permute-start.10 = (f32[16,8,128]{2,1,0:T(8,128)S(1)}, f32[16,8,128]{2,1,0:T(8,128)S(1)}, u32[]{:S(2)}, u32[]{:S(2)}) collective-permute-start(f32[16,8,128]{2,1,0:T(8,128)S(1)} %get-tuple-element.49), channel_id=1, source_target_pairs={{0,24},{8,0},{16,8},{24,16},{1,25},{9,1},{17,9},{25,17},{2,26},{10... | collective-permute-start | bytes 196616 | tf_op jit(solution)/shard_map/ppermute | solution.py:411
  33.9 2.9 %shard_map.102.early = f32[16,16,256]{2,1,0:T(8,128)S(1)} custom-call(f32[3,2,16,128]{3,2,1,0:T(8,128)S(1)} %get-tuple-element.54.v0, f32[3,2,16,128]{3,2,1,0:T(8,128)S(1)} %get-tuple-element.55.v1, f32[3,2,16,128]{3,2,1,0:T(8,128)S(1)} %get-tuple-element.56.v2, s32[2,16,128]{2,1,0:T(8,128)S(1)} %copy-done.2, bf16[256,4096]{1,0:T(8,128)(2,1)S(1)} %shard_map.101.right), custom_call_target="tpu_custom_call" | custom-call | tf_op jit(solution)/shard_map/pallas_call | solution.py:467
  37.4 1.6 %shard_map.103 = f32[16,16,256]{2,1,0:T(8,128)} custom-call(f32[3,2,16,128]{3,2,1,0:T(8,128)S(1)} %get-tuple-element.53.v3, s32[2,16,128]{2,1,0:T(8,128)S(1)} %copy-done.2, bf16[256,4096]{1,0:T(8,128)(2,1)S(1)} %shard_map.101.right, f32[16,16,256]{2,1,0:T(8,128)S(1)} %shard_map.102.early), custom_call_target="tpu_custom_call" | custom-call | tf_op jit(solution)/shard_map/pallas_call | solution.py:471
  39.0 3.4 %all-to-all-start = ((f32[8,32,256]{2,1,0:T(8,128)}), f32[8,32,256]{2,1,0:T(8,128)S(1)}, u32[]{:S(2)}, u32[]{:S(2)}) async-start(f32[8,32,256]{2,1,0:T(8,128)} %bitcast), calls=%async_computation | async-start | bytes 524288 | tf_op jit(solution)/shard_map/all_to_all | solution.py:475
  42.5 6.7 %all-to-all-done = f32[8,32,256]{2,1,0:T(8,128)S(1)} async-done(((f32[8,32,256]{2,1,0:T(8,128)}), f32[8,32,256]{2,1,0:T(8,128)S(1)}, u32[]{:S(2)}, u32[]{:S(2)}) %all-to-all-start) | async-done | bytes 262176 | tf_op jit(solution)/shard_map/all_to_all | solution.py:475
  49.2 1.1 %shard_map.104 = (f32[48,512]{1,0:T(8,128)S(1)}, f32[32,16,128]{2,1,0:T(8,128)}) custom-call(f32[256,256]{1,0:T(8,128)S(1)} %bitcast.3, f32[32,512]{1,0:T(8,128)S(1)} %copy-done.3, f32[32,1]{1,0:T(8,128)S(1)} %copy.12.sigma), custom_call_target="tpu_custom_call" | custom-call | tf_op jit(solution)/shard_map/pallas_call | solution.py:476
  50.3 2.9 %all-to-all-start.1 = ((f32[32,16,128]{2,1,0:T(8,128)}), f32[32,16,128]{2,1,0:T(8,128)S(1)}, u32[]{:S(2)}, u32[]{:S(2)}) async-start(f32[32,16,128]{2,1,0:T(8,128)} %get-tuple-element.57), calls=%async_computation.1 | async-start | bytes 524288 | tf_op jit(solution)/shard_map/all_to_all | solution.py:482
  53.2 1.8 %collective-permute-start.11 = (f32[16,8,128]{2,1,0:T(8,128)S(1)}, f32[16,8,128]{2,1,0:T(8,128)S(1)}, u32[]{:S(2)}, u32[]{:S(2)}) collective-permute-start(f32[16,8,128]{2,1,0:T(8,128)S(1)} %get-tuple-element.51), channel_id=1, source_target_pairs={{0,8},{8,16},{16,24},{24,0},{1,9},{9,17},{17,25},{25,1},{2,10},{10... | collective-permute-start | bytes 196616 | tf_op jit(solution)/shard_map/ppermute | solution.py:411
  55.0 2.1 %collective-permute-start.12 = (f32[16,8,128]{2,1,0:T(8,128)S(1)}, f32[16,8,128]{2,1,0:T(8,128)S(1)}, u32[]{:S(2)}, u32[]{:S(2)}) collective-permute-start(f32[16,8,128]{2,1,0:T(8,128)S(1)} %get-tuple-element.52), channel_id=1, source_target_pairs={{0,24},{8,0},{16,8},{24,16},{1,25},{9,1},{17,9},{25,17},{2,26},{10... | collective-permute-start | bytes 196616 | tf_op jit(solution)/shard_map/ppermute | solution.py:411
  57.1 7.0 %collective-permute-done.11.xr = f32[16,8,128]{2,1,0:T(8,128)S(1)} collective-permute-done((f32[16,8,128]{2,1,0:T(8,128)S(1)}, f32[16,8,128]{2,1,0:T(8,128)S(1)}, u32[]{:S(2)}, u32[]{:S(2)}) %collective-permute-start.11) | collective-permute-done | bytes 65568 | tf_op jit(solution)/shard_map/ppermute | solution.py:411
  64.1 0.9 %shard_map.100 = f32[19,2,16,128]{3,2,1,0:T(8,128)} custom-call(f32[19,2,24,256]{3,2,1,0:T(8,128)S(1)} %get-tuple-element.50.prev, f32[16,8,128]{2,1,0:T(8,128)S(1)} %collective-permute-done.11.xr, f32[16,8,128]{2,1,0:T(8,128)S(1)} %collective-permute-done.12.xl), custom_call_target="tpu_custom_call" | custom-call | tf_op jit(solution)/shard_map/pallas_call | solution.py:486
  65.0 7.3 %shard_map.105 = (f32[44,512]{1,0:T(8,128)}, f32[44,44]{1,0:T(8,128)}) custom-call(f32[32,16,128]{2,1,0:T(8,128)S(1)} %all-to-all-done.1.parts, f32[48,512]{1,0:T(8,128)S(1)} %get-tuple-element.58.aug_ref), custom_call_target="tpu_custom_call" | custom-call | tf_op jit(solution)/shard_map/pallas_call | solution.py:483
  (35 shorter events, 6.7 us)
Async XLA Ops:
  0.6 1.0 %copy-start = (f32[19,2,16,128]{3,2,1,0:T(8,128)S(1)}, f32[19,2,16,128]{3,2,1,0:T(8,128)}, u32[]{:S(2)}) copy-start(f32[19,2,16,128]{3,2,1,0:T(8,128)} %ratio.3) | copy-start | bytes 933892
  1.6 0.7 copy-start.4
  2.3 0.7 copy-start.5
  3.0 0.7 copy-start.6
  3.7 29.6 %copy-start.2 = (s32[2,16,128]{2,1,0:T(8,128)S(1)}, s32[2,16,128]{2,1,0:T(8,128)}, u32[]{:S(2)}) copy-start(s32[2,16,128]{2,1,0:T(8,128)} %row_map.5) | copy-start | bytes 49156
  4.6 8.9 %collective-permute-start.2 = (f32[40,8,128]{2,1,0:T(8,128)S(1)}, f32[40,8,128]{2,1,0:T(8,128)S(1)}, u32[]{:S(2)}, u32[]{:S(2)}) collective-permute-start(f32[40,8,128]{2,1,0:T(8,128)S(1)} %get-tuple-element.37), channel_id=1, source_target_pairs={{0,4},{1,5},{2,6},{3,7},{4,0},{5,1},{6,2},{7,3},{8,12},{9,13},{10,... | collective-permute-start | bytes 491528 | tf_op jit(solution)/shard_map/ppermute | solution.py:419
  7.6 4.4 %collective-permute-start = (f32[3,8,128]{2,1,0:T(8,128)S(1)}, f32[3,8,128]{2,1,0:T(8,128)S(1)}, u32[]{:S(2)}, u32[]{:S(2)}) collective-permute-start(f32[3,8,128]{2,1,0:T(8,128)S(1)} %get-tuple-element.33), channel_id=1, source_target_pairs={{0,1},{1,2},{2,3},{3,0},{4,5},{5,6},{6,7},{7,4},{8,9},{9,10},{10,1... | collective-permute-start | bytes 36872 | tf_op jit(solution)/shard_map/ppermute | solution.py:411
  7.6 4.4 %collective-permute-start.1 = (f32[3,8,128]{2,1,0:T(8,128)S(1)}, f32[3,8,128]{2,1,0:T(8,128)S(1)}, u32[]{:S(2)}, u32[]{:S(2)}) collective-permute-start(f32[3,8,128]{2,1,0:T(8,128)S(1)} %get-tuple-element.34), channel_id=1, source_target_pairs={{0,3},{1,0},{2,1},{3,2},{4,7},{5,4},{6,5},{7,6},{8,11},{9,8},{10,9... | collective-permute-start | bytes 36872 | tf_op jit(solution)/shard_map/ppermute | solution.py:411
  9.4 4.0 %collective-permute-start.3 = (f32[2,8,128]{2,1,0:T(8,128)S(1)}, f32[2,8,128]{2,1,0:T(8,128)S(1)}, u32[]{:S(2)}, u32[]{:S(2)}) collective-permute-start(f32[2,8,128]{2,1,0:T(8,128)S(1)} %get-tuple-element.38), channel_id=1, source_target_pairs={{0,5},{1,6},{2,7},{3,4},{4,1},{5,2},{6,3},{7,0},{8,13},{9,14},{10,... | collective-permute-start | bytes 24584 | tf_op jit(solution)/shard_map/ppermute | solution.py:419
  9.4 4.1 %collective-permute-start.4 = (f32[2,8,128]{2,1,0:T(8,128)S(1)}, f32[2,8,128]{2,1,0:T(8,128)S(1)}, u32[]{:S(2)}, u32[]{:S(2)}) collective-permute-start(f32[2,8,128]{2,1,0:T(8,128)S(1)} %get-tuple-element.39), channel_id=1, source_target_pairs={{0,7},{1,4},{2,5},{3,6},{4,3},{5,0},{6,1},{7,2},{8,15},{9,12},{10,... | collective-permute-start | bytes 24584 | tf_op jit(solution)/shard_map/ppermute | solution.py:419
  12.0 1.0 %copy-start.1 = (f32[19,2,16,128]{3,2,1,0:T(8,128)S(1)}, f32[19,2,16,128]{3,2,1,0:T(8,128)}, u32[]{:S(2)}) copy-start(f32[19,2,16,128]{3,2,1,0:T(8,128)} %ratio.3) | copy-start | bytes 933892
  13.7 6.4 %collective-permute-start.5 = (f32[16,8,128]{2,1,0:T(8,128)S(1)}, f32[16,8,128]{2,1,0:T(8,128)S(1)}, u32[]{:S(2)}, u32[]{:S(2)}) collective-permute-start(f32[16,8,128]{2,1,0:T(8,128)S(1)} %get-tuple-element.42), channel_id=1, source_target_pairs={{0,8},{8,16},{16,24},{24,0},{1,9},{9,17},{17,25},{25,1},{2,10},{10... | collective-permute-start | bytes 196616 | tf_op jit(solution)/shard_map/ppermute | solution.py:411
  15.3 6.2 %collective-permute-start.6 = (f32[16,8,128]{2,1,0:T(8,128)S(1)}, f32[16,8,128]{2,1,0:T(8,128)S(1)}, u32[]{:S(2)}, u32[]{:S(2)}) collective-permute-start(f32[16,8,128]{2,1,0:T(8,128)S(1)} %get-tuple-element.43), channel_id=1, source_target_pairs={{0,24},{8,0},{16,8},{24,16},{1,25},{9,1},{17,9},{25,17},{2,26},{10... | collective-permute-start | bytes 196616 | tf_op jit(solution)/shard_map/ppermute | solution.py:411
  22.1 6.7 %collective-permute-start.7 = (f32[16,8,128]{2,1,0:T(8,128)S(1)}, f32[16,8,128]{2,1,0:T(8,128)S(1)}, u32[]{:S(2)}, u32[]{:S(2)}) collective-permute-start(f32[16,8,128]{2,1,0:T(8,128)S(1)} %get-tuple-element.45), channel_id=1, source_target_pairs={{0,8},{8,16},{16,24},{24,0},{1,9},{9,17},{17,25},{25,1},{2,10},{10... | collective-permute-start | bytes 196616 | tf_op jit(solution)/shard_map/ppermute | solution.py:411
  23.1 5.7 %collective-permute-start.8 = (f32[16,8,128]{2,1,0:T(8,128)S(1)}, f32[16,8,128]{2,1,0:T(8,128)S(1)}, u32[]{:S(2)}, u32[]{:S(2)}) collective-permute-start(f32[16,8,128]{2,1,0:T(8,128)S(1)} %get-tuple-element.46), channel_id=1, source_target_pairs={{0,24},{8,0},{16,8},{24,16},{1,25},{9,1},{17,9},{25,17},{2,26},{10... | collective-permute-start | bytes 196616 | tf_op jit(solution)/shard_map/ppermute | solution.py:411
  29.4 7.4 %collective-permute-start.9 = (f32[16,8,128]{2,1,0:T(8,128)S(1)}, f32[16,8,128]{2,1,0:T(8,128)S(1)}, u32[]{:S(2)}, u32[]{:S(2)}) collective-permute-start(f32[16,8,128]{2,1,0:T(8,128)S(1)} %get-tuple-element.48), channel_id=1, source_target_pairs={{0,8},{8,16},{16,24},{24,0},{1,9},{9,17},{17,25},{25,1},{2,10},{10... | collective-permute-start | bytes 196616 | tf_op jit(solution)/shard_map/ppermute | solution.py:411
  29.8 7.0 %collective-permute-start.10 = (f32[16,8,128]{2,1,0:T(8,128)S(1)}, f32[16,8,128]{2,1,0:T(8,128)S(1)}, u32[]{:S(2)}, u32[]{:S(2)}) collective-permute-start(f32[16,8,128]{2,1,0:T(8,128)S(1)} %get-tuple-element.49), channel_id=1, source_target_pairs={{0,24},{8,0},{16,8},{24,16},{1,25},{9,1},{17,9},{25,17},{2,26},{10... | collective-permute-start | bytes 196616 | tf_op jit(solution)/shard_map/ppermute | solution.py:411
  36.8 5.6 %copy-start.7 = (f32[32]{0:T(128)S(1)}, f32[32]{0:T(128)}, u32[]{:S(2)}) copy-start(f32[32]{0:T(128)} %param.13) | copy-start | bytes 388
  36.8 12.4 %copy-start.3 = (f32[32,512]{1,0:T(8,128)S(1)}, f32[32,512]{1,0:T(8,128)}, u32[]{:S(2)}) copy-start(f32[32,512]{1,0:T(8,128)} %basis.1) | copy-start | bytes 196612
  39.0 10.3 %all-to-all-start = ((f32[8,32,256]{2,1,0:T(8,128)}), f32[8,32,256]{2,1,0:T(8,128)S(1)}, u32[]{:S(2)}, u32[]{:S(2)}) async-start(f32[8,32,256]{2,1,0:T(8,128)} %bitcast), calls=%async_computation | async-start | bytes 524288 | tf_op jit(solution)/shard_map/all_to_all | solution.py:475
  50.3 14.7 %all-to-all-start.1 = ((f32[32,16,128]{2,1,0:T(8,128)}), f32[32,16,128]{2,1,0:T(8,128)S(1)}, u32[]{:S(2)}, u32[]{:S(2)}) async-start(f32[32,16,128]{2,1,0:T(8,128)} %get-tuple-element.57), calls=%async_computation.1 | async-start | bytes 524288 | tf_op jit(solution)/shard_map/all_to_all | solution.py:482
  53.2 10.9 %collective-permute-start.11 = (f32[16,8,128]{2,1,0:T(8,128)S(1)}, f32[16,8,128]{2,1,0:T(8,128)S(1)}, u32[]{:S(2)}, u32[]{:S(2)}) collective-permute-start(f32[16,8,128]{2,1,0:T(8,128)S(1)} %get-tuple-element.51), channel_id=1, source_target_pairs={{0,8},{8,16},{16,24},{24,0},{1,9},{9,17},{17,25},{25,1},{2,10},{10... | collective-permute-start | bytes 196616 | tf_op jit(solution)/shard_map/ppermute | solution.py:411
  55.0 9.0 %collective-permute-start.12 = (f32[16,8,128]{2,1,0:T(8,128)S(1)}, f32[16,8,128]{2,1,0:T(8,128)S(1)}, u32[]{:S(2)}, u32[]{:S(2)}) collective-permute-start(f32[16,8,128]{2,1,0:T(8,128)S(1)} %get-tuple-element.52), channel_id=1, source_target_pairs={{0,24},{8,0},{16,8},{24,16},{1,25},{9,1},{17,9},{25,17},{2,26},{10... | collective-permute-start | bytes 196616 | tf_op jit(solution)/shard_map/ppermute | solution.py:411
where the time goes:
time: 72.8 us; the launch traced here: 72.4 us
  starting transfers between devices  29.2 us (40%)
  waiting for transfers between devices  20.5 us (28%)
  Pallas kernels  17.7 us (24%)
  local copies, waits for them, and re-layouts  4.12 us (6%)
  between operations  0.77 us (1%)
    ppermute x10, starting transfers between devices, shift(): lax.ppermute(value, axis, [(i, (i + step) % count) for i in range(count)])  17.3 us
    ppermute x10, waiting for transfers between devices, shift(): lax.ppermute(value, axis, [(i, (i + step) % count) for i in range(count)])  13.7 us
    pallas_call x1, Pallas kernels, on_device(): call(factor_kernel, (f32(44, rows_local), f32(44, 44)), (pltpu.VMEM((48,...  7.33 us
    all_to_all x1, waiting for transfers between devices, on_device(): lax.all_to_all(term.reshape(16 * highs, LOW), slab, 0, 0, tiled=True)  6.74 us
    ppermute x3, starting transfers between devices, shift_both(): return lax.ppermute(value, ('gy', 'gz'), pairs)  5.71 us
    unnamed x16, local copies, waits for them, and re-layouts  4.03 us
    all_to_all x1, starting transfers between devices, on_device(): lax.all_to_all(term.reshape(16 * highs, LOW), slab, 0, 0, tiled=True)  3.41 us
    pallas_call x1, Pallas kernels, on_device(): call(early_kernel, vmem(highs, 16, LOW), (pltpu.VMEM((32 * highs, cells),...  2.86 us
  transfers between devices with their start and end apart: 15, of which 6 were waited for; matrix products, arithmetic and copies ran while one was open for 0% of the time, Pallas kernels for 7%

commit v1 on v0

--- a/solution.py
+++ b/solution.py
@@ -60,7 +60,17 @@
     return value if shift == 0 else pltpu.roll(value, shift, axis)
 
 
-def init_kernel(table, ratio, solid, cls, g_ref, zr_ref, zl_ref, y_ref, cr_ref, cl_ref):
+def init_kernel(
+    table_hbm, ratio_hbm, solid_hbm, cls_hbm,
+    pops_ref, g_ref, zr_ref, zl_ref, y_ref, cr_ref, cl_ref,
+    table, ratio, solid, cls, sems,
+):
+    pairs = ((ratio_hbm, ratio), (table_hbm, table), (solid_hbm, solid), (cls_hbm, cls))
+    copies = [pltpu.make_async_copy(src, dst, sems.at[i]) for i, (src, dst) in enumerate(pairs)]
+    for copy in copies:
+        copy.start()
+    for copy in copies:
+        copy.wait()
     lane, sub = lanes(), subs()
     blank = jnp.zeros((8, 128), jnp.float32)
     zr, zl = [blank] * 3, [blank] * 3
@@ -72,6 +82,7 @@
                 rows = pl.ds(8 * yt, 8)
                 if f < 19:
                     tile = ratio[f, x, rows, :] * WEIGHTS[f]
+                    pops_ref[f, x, rows, :] = tile
                 else:
                     ids = cls[x, rows, :]
                     drag = jnp.zeros((8, 128), jnp.float32)
@@ -167,14 +178,14 @@
         ref[15] = extra
 
 
-def inner_kernel(ratio, g_in, left, right, out, g_ref, vel_ref, wide):
+def inner_kernel(pops, g_in, left, right, out, g_ref, vel_ref, wide):
     lane = lanes()
     for f in range(FIELDS):
         ref = wide.at[f] if f < 19 else g_ref
         for x in range(2):
             for yt in range(2):
                 rows = pl.ds(8 * yt, 8)
-                own = ratio[f, x, rows, :] * WEIGHTS[f] if f < 19 else g_in[x, rows, :]
+                own = pops[f, x, rows, :] if f < 19 else g_in[x, rows, :]
                 at, k = divmod(f * 4 + x * 2 + yt, 32)
                 tile = jnp.where(lane < 4, roll(right[at], -4 * k, 1), own)
                 tile = jnp.where(lane >= 124, roll(left[at], 124 - 4 * k, 1), tile)
@@ -221,13 +232,15 @@
     return roll(roll(value, c[1], 0), c[2], 1)
 
 
-def step_kernel(prev, g_ref, xr, xl, out, vel_ref, xr_ref, xl_ref, wide, side):
+def step_kernel(prev, g_ref, xr, xl, rider_r, rider_l, out, vel_ref, xr_ref, xl_ref, wide, side):
     unpack_x(xr, xl, side)
     for q in range(19):
         for x in range(2):
             wide[q, x] = streamed(prev, side, q, x)
     collide_all(wide, g_ref, out, vel_ref)
     pack_x(out, xr_ref, xl_ref)
+    xr_ref[16] = rider_r[...]
+    xl_ref[16] = rider_l[...]
 
 
 def last_kernel(prev, xr, xl, out, side):
@@ -282,7 +295,30 @@
         out[h] = both[16 * h : 16 * h + 16] + both[half + 16 * h : half + 16 * h + 16]
 
 
-def late_kernel(v3, row_map, right, early, out, left):
+def old_kernel(total_rows, basis, sigma, scaled_ref, tile_ref, work):
+    scaled = basis[...] * sigma[...]
+    scaled_ref[...] = scaled
+    work[...] = jnp.zeros((32, 128), jnp.float32)
+    work[:, pl.ds(0, 32)] = dot(scaled, scaled, 1) * (1.0 / total_rows)
+    lane = lanes()
+    tile = work[pl.ds(0, 8), :]
+    for k in range(1, 4):
+        here = (lane >= 32 * k) & (lane < 32 * k + 32)
+        tile = jnp.where(here, roll(work[pl.ds(8 * k, 8), :], 32 * k, 1), tile)
+    tile_ref[...] = tile
+
+
+def dot(a, b, dim):
+    return lax.dot_general(
+        a,
+        b,
+        (((1,), (dim,)), ((), ())),
+        precision=lax.Precision.HIGHEST,
+        preferred_element_type=jnp.float32,
+    )
+
+
+def late_kernel(v3, row_map, right, early, own, near_r, near_l, far, out, left):
     highs = out.shape[0]
     high_at = lax.broadcasted_iota(jnp.int32, (highs, 128), 0)
     for x in range(2):
@@ -296,66 +332,45 @@
     half = 3 * highs
     both = both[:half] + both[half:]
     out[...] = early[...]
-    for a in range(3):
-        for h in range(highs):
+    old = (own[...] + far[...]) + (near_r[...] + near_l[...])
+    for h in range(highs):
+        for a in range(3):
             out[h, pl.ds(9 + a, 1), :] = both[highs * a + h : highs * a + h + 1]
-
-
-def gram_kernel(total_rows, parts, basis, sigma, aug_ref, out, gram):
+        if h % 2 == 0:
+            out[h, pl.ds(12, 4), pl.ds(0, 128)] = old[:4]
+            out[h, pl.ds(12, 4), pl.ds(128, 128)] = old[4:]
+
+
+def gram_kernel(total_rows, parts, scaled, snap_ref, tile_ref, out, aug):
     owners = parts.shape[0] // 32
     total = parts[pl.ds(0, 32), :]
     for o in range(1, owners):
         total = total + parts[pl.ds(32 * o, 32), :]
-    aug_ref[pl.ds(0, 32), :] = basis[...] * sigma[...]
-    aug_ref[pl.ds(32, 16), pl.ds(0, LOW)] = total[:16]
-    aug_ref[pl.ds(32, 16), pl.ds(LOW, LOW)] = total[16:]
-    aug = aug_ref[...]
-    product = lax.dot_general(
-        aug,
-        aug,
-        (((1,), (1,)), ((), ())),
-        precision=lax.Precision.HIGHEST,
-        preferred_element_type=jnp.float32,
-    ) * (1.0 / total_rows)
-    gram[...] = jnp.zeros((48, 128), jnp.float32)
-    gram[:, pl.ds(0, 48)] = product
-    lane = lanes()
-    first = gram[pl.ds(0, 8), :]
-    for k in range(1, 4):
-        here = (lane >= 32 * k) & (lane < 32 * k + 32)
-        first = jnp.where(here, roll(gram[pl.ds(8 * k, 8), :], 32 * k, 1), first)
-    second = jnp.where(lane < 64, gram[pl.ds(32, 8), :], roll(gram[pl.ds(40, 8), :], 64, 1))
+    tile_ref[pl.ds(0, 4), :] = total[12:16, :128]
+    tile_ref[pl.ds(4, 4), :] = total[12:16, 128:]
+    used = lax.broadcasted_iota(jnp.int32, (16, LOW), 0) < 12
+    aug[pl.ds(0, 32), :] = scaled[...]
+    aug[pl.ds(32, 16), pl.ds(0, LOW)] = jnp.where(used, total[:16], 0.0)
+    aug[pl.ds(32, 16), pl.ds(LOW, LOW)] = jnp.where(used, total[16:], 0.0)
+    aug[pl.ds(48, 80), :] = jnp.zeros((80, 2 * LOW), jnp.float32)
+    snap = aug[pl.ds(32, 16), :]
+    snap_ref[...] = snap
+    product = dot(snap, aug[...], 1) * (1.0 / total_rows)
+    packed = jnp.where(lanes() < 64, product[:8], roll(product[8:], 64, 1))
     for d in range(out.shape[0]):
-        out[d, pl.ds(0, 8), :] = first
-        out[d, pl.ds(8, 8), :] = second
-
-
-def factor_kernel(parts, aug_ref, basis_ref, tri_ref, work):
-    lane = lanes()
-    total = parts[0]
-    for d in range(1, parts.shape[0]):
-        total = total + parts[d]
-    first, second = total[:8], total[8:]
-    low = jnp.concatenate([jnp.where(lane < 64, second, 0.0), jnp.where(lane < 64, roll(second, -64, 1), 0.0)], 0)
-    turned = low.T
-    for k in range(4):
-        own = jnp.where(lane < 32, roll(first, -32 * k, 1), 0.0)
-        work[pl.ds(8 * k, 8), :] = own
-        work[pl.ds(8 * k, 8), pl.ds(32, 16)] = turned[8 * k : 8 * k + 8]
-    work[pl.ds(32, 16), :] = low
-    tiles = []
-    for t in range(6):
-        row = lax.broadcasted_iota(jnp.int32, (8, 128), 0) + 8 * t
-        tiles.append(work[pl.ds(8 * t, 8), :] + jnp.where(lane == row + 64, 1.0, 0.0))
+        out[d] = packed
+
+
+def eliminate(tiles, count):
+    sub = subs()
     done = list(tiles)
-    sub = subs()
-    for k in range(44):
+    for k in range(count):
         t, r = divmod(k, 8)
         pivot_row = jnp.broadcast_to(tiles[t][r : r + 1, :], (8, 128))
         pivot = jnp.broadcast_to(pivot_row[:, k : k + 1], (8, 128))
         inv = 1.0 / jnp.sqrt(pivot)
         scaled = pivot_row * inv
-        for u in range(t, 6):
+        for u in range(t, len(tiles)):
             column = jnp.broadcast_to(tiles[u][:, k : k + 1], (8, 128))
             update = tiles[u] - (column * inv) * scaled
             if u == t:
@@ -363,21 +378,44 @@
                 tiles[t] = jnp.where(sub > r, update, tiles[t])
             else:
                 tiles[u] = update
-    for t in range(6):
-        row = sub + 8 * t
-        work[pl.ds(8 * t, 8), :] = jnp.where(lane >= 64, done[t], jnp.where(lane >= row, done[t], 0.0))
-        if t == 5:
-            work[pl.ds(40, 8), :] = jnp.where(sub < 4, work[pl.ds(40, 8), :], 0.0)
-    both = work[...]
-    tri_ref[...] = both[:44, :44]
-    inverse = both[:, 64:112]
-    basis_ref[...] = lax.dot_general(
-        inverse,
-        aug_ref[...],
-        (((1,), (0,)), ((), ())),
-        precision=lax.Precision.HIGHEST,
-        preferred_element_type=jnp.float32,
-    )[:44]
+    return [jnp.where((lanes() >= 64) | (lanes() >= sub + 8 * t), tile, 0.0) for t, tile in enumerate(done)]
+
+
+def old_factor_kernel(tile, scaled, work, head_ref):
+    lane, sub = lanes(), subs()
+    tiles = []
+    for k in range(4):
+        own = jnp.where(lane < 32, roll(tile[...], -32 * k, 1), 0.0)
+        tiles.append(own + jnp.where(lane == sub + 8 * k + 64, 1.0, 0.0))
+    for k, value in enumerate(eliminate(tiles, 32)):
+        work[pl.ds(8 * k, 8), :] = value
+    head_ref[...] = dot(work[:, pl.ds(64, 32)], scaled[...], 0)
+
+
+def factor_kernel(parts, factor, head, snap, basis_ref, tri_ref, work):
+    lane, sub = lanes(), subs()
+    total = parts[0]
+    for d in range(1, parts.shape[0]):
+        total = total + parts[d]
+    work[pl.ds(0, 8), :] = jnp.where(lane < 64, total, 0.0)
+    work[pl.ds(8, 8), :] = jnp.where(lane < 64, roll(total, -64, 1), 0.0)
+    cross = work[:, pl.ds(0, 32)]
+    inner = work[:, pl.ds(32, 16)]
+    inverse = factor[:, pl.ds(64, 32)]
+    below = dot(cross, inverse, 1)
+    rest = snap[...] - dot(below, head[...], 0)
+    inner = inner - dot(below, below, 1)
+    work[...] = jnp.zeros((16, 128), jnp.float32)
+    work[:, pl.ds(0, 16)] = inner
+    tiles = [work[pl.ds(8 * t, 8), :] + jnp.where(lane == sub + 8 * t + 64, 1.0, 0.0) for t in range(2)]
+    for t, value in enumerate(eliminate(tiles, 12)):
+        work[pl.ds(8 * t, 8), :] = value
+    tri_ref[pl.ds(0, 32), pl.ds(0, 32)] = factor[:, pl.ds(0, 32)]
+    tri_ref[pl.ds(0, 32), pl.ds(32, 12)] = dot(inverse, cross, 1)[:, :12]
+    tri_ref[pl.ds(32, 12), pl.ds(0, 32)] = jnp.zeros((12, 32), jnp.float32)
+    tri_ref[pl.ds(32, 12), pl.ds(32, 12)] = work[pl.ds(0, 12), pl.ds(0, 12)]
+    basis_ref[pl.ds(0, 32), :] = head[...]
+    basis_ref[pl.ds(32, 12), :] = dot(work[:, pl.ds(64, 16)], rest, 0)[:12]
 
 
 def f32(*shape):
@@ -392,11 +430,8 @@
     return pltpu.with_memory_space_constraint(value, pltpu.VMEM)
 
 
-def call(kernel, outs, scratch=(), smem=(), count=None, aliases=None, limit=16):
-    specs = [
-        pl.BlockSpec(memory_space=pltpu.SMEM) if i in smem else pl.BlockSpec(memory_space=pltpu.VMEM)
-        for i in range(count)
-    ]
+def call(kernel, outs, scratch=(), count=None, aliases=None, limit=16, space=pltpu.VMEM):
+    specs = [pl.BlockSpec(memory_space=space) for _ in range(count)]
     many = isinstance(outs, (tuple, list))
     out_specs = [pl.BlockSpec(memory_space=pltpu.VMEM)] * len(outs) if many else pl.BlockSpec(memory_space=pltpu.VMEM)
     return pl.pallas_call(
@@ -436,12 +471,20 @@
     cells = 4096
     tile = (8, 128)
 
-    g, zr, zl, y, cr, cl = call(
+    pops, g, zr, zl, y, cr, cl = call(
         init_kernel,
-        (vmem(2, 16, 128), vmem(3, *tile), vmem(3, *tile), vmem(2 * FIELDS, *tile), vmem(2, *tile), vmem(2, *tile)),
-        smem=(0,),
+        (vmem(19, 2, 16, 128), vmem(2, 16, 128), vmem(3, *tile), vmem(3, *tile))
+        + (vmem(2 * FIELDS, *tile), vmem(2, *tile), vmem(2, *tile)),
+        (
+            pltpu.SMEM(drag_table.shape, jnp.float32),
+            pltpu.VMEM((19, 2, 16, 128), jnp.float32),
+            pltpu.VMEM((2, 16, 128), jnp.int32),
+            pltpu.VMEM((2, 16, 128), jnp.int32),
+            pltpu.SemaphoreType.DMA((4,)),
+        ),
         count=4,
-    )(drag_table, pop_ratio, solid_flags, class_ids)
+        space=pltpu.HBM,
+    )(*(pltpu.with_memory_space_constraint(v, pltpu.HBM) for v in (drag_table, pop_ratio, solid_flags, class_ids)))
     y = across(y, 0)
     left, right = shift(zr, "gz", 1), shift(zl, "gz", -1)
     cr, cl = across(cr, 1), across(cl, -1)
@@ -449,18 +492,36 @@
     wide = pltpu.VMEM((19, 2, 24, 256), jnp.float32)
     side = pltpu.VMEM((2, 5, 24, 256), jnp.float32)
     big, wall, vel, face = vmem(19, 2, 24, 256), vmem(2, 24, 256), vmem(3, 2, 16, 128), vmem(16, *tile)
+    loaded = vmem(17, *tile)
     relaxed, g_wide, v0 = call(inner_kernel, (big, wall, vel), (wide,), count=4)(
-        pop_ratio, *map(held, (g, left, right))
+        *map(held, (pops, g, left, right))
     )
     relaxed, g_wide, xr, xl = call(
         outer_kernel, (big, wall, face, face), (wide,), count=5, aliases={0: 0, 1: 1}
     )(*map(held, (relaxed, g_wide, y, cr, cl)))
     vels = [v0]
-    step = jax.jit(call(step_kernel, (big, vel, face, face), (wide, side), count=4))
+    old, own = call(
+        functools.partial(old_kernel, float(rows_local * devices)),
+        (vmem(32, rows_local), vmem(*tile)),
+        (pltpu.VMEM((32, 128), jnp.float32),),
+        count=2,
+    )(old_basis, old_sigma[:, None])
+    ring = lax.axis_size("gx") == 4
+    if not ring:
+        own = lax.psum(own, "gx")
+    none = jnp.zeros(tile, jnp.float32)
+    step = jax.jit(call(step_kernel, (big, vel, loaded, loaded), (wide, side), count=6))
     onehot = call(onehot_kernel, pltpu.VMEM((LOW, cells), jnp.bfloat16), count=1)(row_map)
-    for _ in range(1, STEPS):
+    riders, got = (own, own), [none] * 3
+    for s in range(1, STEPS):
         xr, xl = shift(xr, "gx", 1), shift(xl, "gx", -1)
-        relaxed, vel_s, xr, xl = step(*map(held, (relaxed, g_wide, xr, xl)))
+        if s == 2 and ring:
+            got[0], got[1] = xr[16], xl[16]
+            riders = (xr[16], none)
+        if s == 3 and ring:
+            got[2] = xr[16]
+            riders = (none, none)
+        relaxed, vel_s, xr, xl = step(*map(held, (relaxed, g_wide, xr, xl, *riders)))
         vels.append(vel_s)
     xr, xl = shift(xr, "gx", 1), shift(xl, "gx", -1)
 
@@ -469,20 +530,21 @@
         limit=8 + highs // 2,
     )(*map(held, vels[:3]), row_map, held(onehot))
     term = call(
-        late_kernel, f32(highs, 16, LOW), (pltpu.VMEM((6 * highs, cells), jnp.bfloat16),), count=4,
+        late_kernel, f32(highs, 16, LOW), (pltpu.VMEM((6 * highs, cells), jnp.bfloat16),), count=8,
         limit=8 + highs // 2,
-    )(held(vels[3]), row_map, held(onehot), held(early))
+    )(held(vels[3]), row_map, *map(held, (onehot, early, own, *got)))
     parts = lax.all_to_all(term.reshape(16 * highs, LOW), slab, 0, 0, tiled=True)
-    aug, gram = call(
+    snap, old_tile, gram = call(
         functools.partial(gram_kernel, float(rows_local * devices)),
-        (vmem(48, rows_local), f32(devices, 16, 128)),
-        (pltpu.VMEM((48, 128), jnp.float32),),
-        count=3,
-    )(held(parts), old_basis, old_sigma[:, None])
+        (vmem(16, rows_local), vmem(*tile), f32(devices, *tile)),
+        (pltpu.VMEM((128, rows_local), jnp.float32),),
+        count=2,
+    )(held(parts), held(old))
     grams = lax.all_to_all(gram, everyone, 0, 0, tiled=True)
+    factor, head = call(old_factor_kernel, (vmem(32, 128), vmem(32, rows_local)), count=2)(held(old_tile), held(old))
     new_basis, upper = call(
-        factor_kernel, (f32(44, rows_local), f32(44, 44)), (pltpu.VMEM((48, 128), jnp.float32),), count=2
-    )(held(grams), held(aug))
+        factor_kernel, (f32(44, rows_local), f32(44, 44)), (pltpu.VMEM((16, 128), jnp.float32),), count=4
+    )(*map(held, (grams, factor, head, snap)))
     populations = call(last_kernel, f32(19, 2, 16, 128), (side,), count=3)(*map(held, (relaxed, xr, xl)))
     return (populations, new_basis, upper)
 

time: 72.8 us -> 66.8 us (0.918)
  waiting for transfers between devices: 20.5 us -> 10.6 us
  blocking collectives: 0 us -> 9.34 us
  starting transfers between devices: 29.2 us -> 26.6 us
  local copies, waits for them, and re-layouts: 4.12 us -> 1.59 us
    all_to_all x0 -> x1, blocking collectives: none -> 9.34 us  [on_device(): lax.all_to_all(term.reshape(16 * highs, LOW), slab, 0, 0, tiled=True)]
    all_to_all x1 -> x0, waiting for transfers between devices: 6.74 us -> none  [on_device(): lax.all_to_all(term.reshape(16 * highs, LOW), slab, 0, 0, tiled=True)]
    ppermute x10, waiting for transfers between devices: 13.7 us -> 9.53 us  [shift(): lax.ppermute(value, axis, [(i, (i + step) % count) for i in range(count)])]
    all_to_all x1 -> x0, starting transfers between devices: 3.41 us -> none  [on_device(): lax.all_to_all(term.reshape(16 * highs, LOW), slab, 0, 0, tiled=True)]
    unnamed x16 -> x4, local copies, waits for them, and re-layouts: 4.03 us -> 0.84 us
    ppermute x3, waiting for transfers between devices: 0.02 us -> 1.04 us  [shift_both(): return lax.ppermute(value, ('gy', 'gz'), pairs)]
    pallas_call x6 -> x8, Pallas kernels: 11.1 us -> 11.8 us  [the longest x1 4.53 us: on_device(): call(old_factor_kernel, (vmem(32, 128), vmem(32, rows_local)), count=2)]
  transfers between devices with their start and end apart: 15 -> 14, of which waited for: 6 -> 7; matrix products, arithmetic and copies ran while one was open for 0% -> 1% of each run, Pallas kernels for 7% -> 14%
where the time goes in v1:
time: 66.8 us; the launch traced here: 66.5 us
  starting transfers between devices  26.6 us (40%)
  Pallas kernels  17.7 us (26%)
  waiting for transfers between devices  10.6 us (16%)
  blocking collectives  9.34 us (14%)
  local copies, waits for them, and re-layouts  1.59 us (2%)
  between operations  0.75 us (1%)
    ppermute x10, starting transfers between devices, shift(): lax.ppermute(value, axis, [(i, (i + step) % count) for i in range(count)])  17.3 us
    ppermute x10, waiting for transfers between devices, shift(): lax.ppermute(value, axis, [(i, (i + step) % count) for i in range(count)])  9.53 us
    all_to_all x1, blocking collectives, on_device(): lax.all_to_all(term.reshape(16 * highs, LOW), slab, 0, 0, tiled=True)  9.34 us
    ppermute x3, starting transfers between devices, shift_both(): return lax.ppermute(value, ('gy', 'gz'), pairs)  5.71 us
    pallas_call x1, Pallas kernels, on_device(): call(old_factor_kernel, (vmem(32, 128), vmem(32, rows_local)), count=2)  4.53 us
    all_to_all x1, starting transfers between devices, on_device(): grams = lax.all_to_all(gram, everyone, 0, 0, tiled=True)  3.57 us
    pallas_call x1, Pallas kernels, on_device(): call(factor_kernel, (f32(44, rows_local), f32(44, 44)), (pltpu.VMEM((16,...  2.89 us
    pallas_call x1, Pallas kernels, on_device(): call(early_kernel, vmem(highs, 16, LOW), (pltpu.VMEM((32 * highs, cells),...  2.86 us
  transfers between devices with their start and end apart: 14, of which 7 were waited for; matrix products, arithmetic and copies ran while one was open for 1% of the time, Pallas kernels for 14%

profile of v1, /device:TPU:0, one launch (start us, length us, event | category | flops | bytes accessed | tf_op | source)
XLA Modules:
  0.0 66.5 jit_solution(7635446712039886216)
XLA Ops:
  0.6 1.3 %shard_map.94 = (f32[19,2,16,128]{3,2,1,0:T(8,128)S(1)}, f32[2,16,128]{2,1,0:T(8,128)S(1)}, f32[3,8,128]{2,1,0:T(8,128)S(1)}, f32[3,8,128]{2,1,0:T(8,128)S(1)}, ...) custom-call(f32[8]{0:T(128)} %table_hbm.1, f32[19,2,16,128]{3,2,1,0:T(8,128)} %ratio_hbm.1, ...), custom_call_target="tpu_custom_call" | custom-call | tf_op jit(solution)/shard_map/pallas_call | solution.py:474
  2.0 3.1 %collective-permute-start.2 = (f32[40,8,128]{2,1,0:T(8,128)S(1)}, f32[40,8,128]{2,1,0:T(8,128)S(1)}, u32[]{:S(2)}, u32[]{:S(2)}) collective-permute-start(f32[40,8,128]{2,1,0:T(8,128)S(1)} %get-tuple-element.44), channel_id=1, source_target_pairs={{0,4},{1,5},{2,6},{3,7},{4,0},{5,1},{6,2},{7,3},{8,12},{9,13},{10,... | collective-permute-start | bytes 491528 | tf_op jit(solution)/shard_map/ppermute | solution.py:454
  5.1 1.7 %collective-permute-start.1 = (f32[3,8,128]{2,1,0:T(8,128)S(1)}, f32[3,8,128]{2,1,0:T(8,128)S(1)}, u32[]{:S(2)}, u32[]{:S(2)}) collective-permute-start(f32[3,8,128]{2,1,0:T(8,128)S(1)} %get-tuple-element.41), channel_id=1, source_target_pairs={{0,3},{1,0},{2,1},{3,2},{4,7},{5,4},{6,5},{7,6},{8,11},{9,8},{10,9... | collective-permute-start | bytes 36872 | tf_op jit(solution)/shard_map/ppermute | solution.py:446
  6.8 2.6 %collective-permute-start.4 = (f32[2,8,128]{2,1,0:T(8,128)S(1)}, f32[2,8,128]{2,1,0:T(8,128)S(1)}, u32[]{:S(2)}, u32[]{:S(2)}) collective-permute-start(f32[2,8,128]{2,1,0:T(8,128)S(1)} %get-tuple-element.46), channel_id=1, source_target_pairs={{0,7},{1,4},{2,5},{3,6},{4,3},{5,0},{6,1},{7,2},{8,15},{9,12},{10,... | collective-permute-start | bytes 24584 | tf_op jit(solution)/shard_map/ppermute | solution.py:454
  9.8 0.9 %collective-permute-done.3.cr = f32[2,8,128]{2,1,0:T(8,128)S(1)} collective-permute-done((f32[2,8,128]{2,1,0:T(8,128)S(1)}, f32[2,8,128]{2,1,0:T(8,128)S(1)}, u32[]{:S(2)}, u32[]{:S(2)}) %collective-permute-start.3) | collective-permute-done | bytes 8224 | tf_op jit(solution)/shard_map/ppermute | solution.py:454
  11.1 1.6 %collective-permute-start.5 = (f32[16,8,128]{2,1,0:T(8,128)S(1)}, f32[16,8,128]{2,1,0:T(8,128)S(1)}, u32[]{:S(2)}, u32[]{:S(2)}) collective-permute-start(f32[16,8,128]{2,1,0:T(8,128)S(1)} %get-tuple-element.49), channel_id=1, source_target_pairs={{0,8},{8,16},{16,24},{24,0},{1,9},{9,17},{17,25},{25,1},{2,10},{10... | collective-permute-start | bytes 196616 | tf_op jit(solution)/shard_map/ppermute | solution.py:446
  12.8 2.2 %collective-permute-start.6 = (f32[16,8,128]{2,1,0:T(8,128)S(1)}, f32[16,8,128]{2,1,0:T(8,128)S(1)}, u32[]{:S(2)}, u32[]{:S(2)}) collective-permute-start(f32[16,8,128]{2,1,0:T(8,128)S(1)} %get-tuple-element.50), channel_id=1, source_target_pairs={{0,24},{8,0},{16,8},{24,16},{1,25},{9,1},{17,9},{25,17},{2,26},{10... | collective-permute-start | bytes 196616 | tf_op jit(solution)/shard_map/ppermute | solution.py:446
  17.5 1.4 %collective-permute-done.6.xl = f32[16,8,128]{2,1,0:T(8,128)S(1)} collective-permute-done((f32[16,8,128]{2,1,0:T(8,128)S(1)}, f32[16,8,128]{2,1,0:T(8,128)S(1)}, u32[]{:S(2)}, u32[]{:S(2)}) %collective-permute-start.6) | collective-permute-done | bytes 65568 | tf_op jit(solution)/shard_map/ppermute | solution.py:446
  19.5 1.0 %collective-permute-start.7 = (f32[17,8,128]{2,1,0:T(8,128)S(1)}, f32[17,8,128]{2,1,0:T(8,128)S(1)}, u32[]{:S(2)}, u32[]{:S(2)}) collective-permute-start(f32[17,8,128]{2,1,0:T(8,128)S(1)} %get-tuple-element.53), channel_id=1, source_target_pairs={{0,8},{8,16},{16,24},{24,0},{1,9},{9,17},{17,25},{25,1},{2,10},{10... | collective-permute-start | bytes 208904 | tf_op jit(solution)/shard_map/ppermute | solution.py:446
  21.2 2.9 %collective-permute-start.8 = (f32[17,8,128]{2,1,0:T(8,128)S(1)}, f32[17,8,128]{2,1,0:T(8,128)S(1)}, u32[]{:S(2)}, u32[]{:S(2)}) collective-permute-start(f32[17,8,128]{2,1,0:T(8,128)S(1)} %get-tuple-element.54), channel_id=1, source_target_pairs={{0,24},{8,0},{16,8},{24,16},{1,25},{9,1},{17,9},{25,17},{2,26},{10... | collective-permute-start | bytes 208904 | tf_op jit(solution)/shard_map/ppermute | solution.py:446
  24.1 2.0 %collective-permute-done.7.xr = f32[17,8,128]{2,1,0:T(8,128)S(1)} collective-permute-done((f32[17,8,128]{2,1,0:T(8,128)S(1)}, f32[17,8,128]{2,1,0:T(8,128)S(1)}, u32[]{:S(2)}, u32[]{:S(2)}) %collective-permute-start.7) | collective-permute-done | bytes 69664 | tf_op jit(solution)/shard_map/ppermute | solution.py:446
  27.3 1.0 %collective-permute-start.9 = (f32[17,8,128]{2,1,0:T(8,128)S(1)}, f32[17,8,128]{2,1,0:T(8,128)S(1)}, u32[]{:S(2)}, u32[]{:S(2)}) collective-permute-start(f32[17,8,128]{2,1,0:T(8,128)S(1)} %get-tuple-element.56), channel_id=1, source_target_pairs={{0,8},{8,16},{16,24},{24,0},{1,9},{9,17},{17,25},{25,1},{2,10},{10... | collective-permute-start | bytes 208904 | tf_op jit(solution)/shard_map/ppermute | solution.py:446
  28.3 2.8 %collective-permute-start.10 = (f32[17,8,128]{2,1,0:T(8,128)S(1)}, f32[17,8,128]{2,1,0:T(8,128)S(1)}, u32[]{:S(2)}, u32[]{:S(2)}) collective-permute-start(f32[17,8,128]{2,1,0:T(8,128)S(1)} %get-tuple-element.57), channel_id=1, source_target_pairs={{0,24},{8,0},{16,8},{24,16},{1,25},{9,1},{17,9},{25,17},{2,26},{10... | collective-permute-start | bytes 208904 | tf_op jit(solution)/shard_map/ppermute | solution.py:446
  31.1 2.9 %shard_map.103.early = f32[16,16,256]{2,1,0:T(8,128)S(1)} custom-call(f32[3,2,16,128]{3,2,1,0:T(8,128)S(1)} %get-tuple-element.62.v0, f32[3,2,16,128]{3,2,1,0:T(8,128)S(1)} %get-tuple-element.63.v1, f32[3,2,16,128]{3,2,1,0:T(8,128)S(1)} %get-tuple-element.64.v2, s32[2,16,128]{2,1,0:T(8,128)S(1)} %copy-done, bf16[256,4096]{1,0:T(8,128)(2,1)S(1)} %shard_map.102.right), custom_call_target="tpu_custom_call" | custom-call | tf_op jit(solution)/shard_map/pallas_call | solution.py:528
  34.6 0.9 %shard_map.104 = f32[16,16,256]{2,1,0:T(8,128)S(1)} custom-call(f32[3,2,16,128]{3,2,1,0:T(8,128)S(1)} %get-tuple-element.61.v3, s32[2,16,128]{2,1,0:T(8,128)S(1)} %copy-done, bf16[256,4096]{1,0:T(8,128)(2,1)S(1)} %shard_map.102.right, f32[16,16,256]{2,1,0:T(8,128)S(1)} %shard_map.103.early, f32[8,128]{1,0:T(8,128)S(1)} %get-tuple-element.51.rider_r.rider_l.own, ...), custom_call_target="tpu_custom_call" | custom-call | tf_op jit(solution)/shard_map/pallas_call | solution.py:532
  35.5 9.3 %all_to_all.16 = f32[8,32,256]{2,1,0:T(8,128)S(1)} all-to-all(f32[8,32,256]{2,1,0:T(8,128)S(1)} %bitcast.10), channel_id=1, replica_groups=mesh['gx'=4,'gy'=2,'gz'=4] {'gy','gz'}, dimensions={0} | all-to-all | bytes 524288 | tf_op jit(solution)/shard_map/all_to_all | solution.py:536
  44.8 0.9 %shard_map.105 = (f32[16,512]{1,0:T(8,128)S(1)}, f32[8,128]{1,0:T(8,128)S(1)}, f32[32,8,128]{2,1,0:T(8,128)}) custom-call(f32[256,256]{1,0:T(8,128)S(1)} %bitcast.9, f32[32,512]{1,0:T(8,128)S(1)} %get-tuple-element.65.scaled), custom_call_target="tpu_custom_call" | custom-call | tf_op jit(solution)/shard_map/pallas_call | solution.py:537
  45.8 3.6 %all-to-all-start.1 = ((f32[32,8,128]{2,1,0:T(8,128)}), f32[32,8,128]{2,1,0:T(8,128)S(1)}, u32[]{:S(2)}, u32[]{:S(2)}) async-start(f32[32,8,128]{2,1,0:T(8,128)} %get-tuple-element.66), calls=%async_computation.1 | async-start | bytes 262144 | tf_op jit(solution)/shard_map/all_to_all | solution.py:543
  49.3 1.8 %collective-permute-start.11 = (f32[17,8,128]{2,1,0:T(8,128)S(1)}, f32[17,8,128]{2,1,0:T(8,128)S(1)}, u32[]{:S(2)}, u32[]{:S(2)}) collective-permute-start(f32[17,8,128]{2,1,0:T(8,128)S(1)} %get-tuple-element.59), channel_id=1, source_target_pairs={{0,8},{8,16},{16,24},{24,0},{1,9},{9,17},{17,25},{25,1},{2,10},{10... | collective-permute-start | bytes 208904 | tf_op jit(solution)/shard_map/ppermute | solution.py:446
  51.2 2.1 %collective-permute-start.12 = (f32[17,8,128]{2,1,0:T(8,128)S(1)}, f32[17,8,128]{2,1,0:T(8,128)S(1)}, u32[]{:S(2)}, u32[]{:S(2)}) collective-permute-start(f32[17,8,128]{2,1,0:T(8,128)S(1)} %get-tuple-element.60), channel_id=1, source_target_pairs={{0,24},{8,0},{16,8},{24,16},{1,25},{9,1},{17,9},{25,17},{2,26},{10... | collective-permute-start | bytes 208904 | tf_op jit(solution)/shard_map/ppermute | solution.py:446
  53.2 5.0 %collective-permute-done.11.xr = f32[17,8,128]{2,1,0:T(8,128)S(1)} collective-permute-done((f32[17,8,128]{2,1,0:T(8,128)S(1)}, f32[17,8,128]{2,1,0:T(8,128)S(1)}, u32[]{:S(2)}, u32[]{:S(2)}) %collective-permute-start.11) | collective-permute-done | bytes 69664 | tf_op jit(solution)/shard_map/ppermute | solution.py:446
  58.2 0.9 %shard_map.101 = f32[19,2,16,128]{3,2,1,0:T(8,128)} custom-call(f32[19,2,24,256]{3,2,1,0:T(8,128)S(1)} %get-tuple-element.58.prev, f32[17,8,128]{2,1,0:T(8,128)S(1)} %collective-permute-done.11.xr, f32[17,8,128]{2,1,0:T(8,128)S(1)} %collective-permute-done.12.xl), custom_call_target="tpu_custom_call" | custom-call | tf_op jit(solution)/shard_map/pallas_call | solution.py:548
  59.1 4.5 %shard_map.106 = (f32[32,128]{1,0:T(8,128)S(1)}, f32[32,512]{1,0:T(8,128)S(1)}) custom-call(f32[8,128]{1,0:T(8,128)S(1)} %get-tuple-element.67.tile, f32[32,512]{1,0:T(8,128)S(1)} %get-tuple-element.65.scaled), custom_call_target="tpu_custom_call" | custom-call | tf_op jit(solution)/shard_map/pallas_call | solution.py:544
  63.6 2.9 %shard_map.107 = (f32[44,512]{1,0:T(8,128)}, f32[44,44]{1,0:T(8,128)}) custom-call(f32[32,8,128]{2,1,0:T(8,128)S(1)} %all-to-all-done.1.parts, f32[32,128]{1,0:T(8,128)S(1)} %get-tuple-element.68.factor, f32[32,512]{1,0:T(8,128)S(1)} %get-tuple-element.69.head, f32[16,512]{1,0:T(8,128)S(1)} %get-tuple-element.70.snap), custom_call_target="tpu_custom_call" | custom-call | tf_op jit(solution)/shard_map/pallas_call | solution.py:545
  (28 shorter events, 6.2 us)
Async XLA Ops:
  0.6 19.9 %copy-start = (s32[2,16,128]{2,1,0:T(8,128)S(1)}, s32[2,16,128]{2,1,0:T(8,128)}, u32[]{:S(2)}) copy-start(s32[2,16,128]{2,1,0:T(8,128)} %row_map.5) | copy-start | bytes 49156
  2.0 8.9 %collective-permute-start.2 = (f32[40,8,128]{2,1,0:T(8,128)S(1)}, f32[40,8,128]{2,1,0:T(8,128)S(1)}, u32[]{:S(2)}, u32[]{:S(2)}) collective-permute-start(f32[40,8,128]{2,1,0:T(8,128)S(1)} %get-tuple-element.44), channel_id=1, source_target_pairs={{0,4},{1,5},{2,6},{3,7},{4,0},{5,1},{6,2},{7,3},{8,12},{9,13},{10,... | collective-permute-start | bytes 491528 | tf_op jit(solution)/shard_map/ppermute | solution.py:454
  5.0 4.4 %collective-permute-start = (f32[3,8,128]{2,1,0:T(8,128)S(1)}, f32[3,8,128]{2,1,0:T(8,128)S(1)}, u32[]{:S(2)}, u32[]{:S(2)}) collective-permute-start(f32[3,8,128]{2,1,0:T(8,128)S(1)} %get-tuple-element.40), channel_id=1, source_target_pairs={{0,1},{1,2},{2,3},{3,0},{4,5},{5,6},{6,7},{7,4},{8,9},{9,10},{10,1... | collective-permute-start | bytes 36872 | tf_op jit(solution)/shard_map/ppermute | solution.py:446
  5.1 4.4 %collective-permute-start.1 = (f32[3,8,128]{2,1,0:T(8,128)S(1)}, f32[3,8,128]{2,1,0:T(8,128)S(1)}, u32[]{:S(2)}, u32[]{:S(2)}) collective-permute-start(f32[3,8,128]{2,1,0:T(8,128)S(1)} %get-tuple-element.41), channel_id=1, source_target_pairs={{0,3},{1,0},{2,1},{3,2},{4,7},{5,4},{6,5},{7,6},{8,11},{9,8},{10,9... | collective-permute-start | bytes 36872 | tf_op jit(solution)/shard_map/ppermute | solution.py:446
  6.8 4.0 %collective-permute-start.3 = (f32[2,8,128]{2,1,0:T(8,128)S(1)}, f32[2,8,128]{2,1,0:T(8,128)S(1)}, u32[]{:S(2)}, u32[]{:S(2)}) collective-permute-start(f32[2,8,128]{2,1,0:T(8,128)S(1)} %get-tuple-element.45), channel_id=1, source_target_pairs={{0,5},{1,6},{2,7},{3,4},{4,1},{5,2},{6,3},{7,0},{8,13},{9,14},{10,... | collective-permute-start | bytes 24584 | tf_op jit(solution)/shard_map/ppermute | solution.py:454
  6.8 4.1 %collective-permute-start.4 = (f32[2,8,128]{2,1,0:T(8,128)S(1)}, f32[2,8,128]{2,1,0:T(8,128)S(1)}, u32[]{:S(2)}, u32[]{:S(2)}) collective-permute-start(f32[2,8,128]{2,1,0:T(8,128)S(1)} %get-tuple-element.46), channel_id=1, source_target_pairs={{0,7},{1,4},{2,5},{3,6},{4,3},{5,0},{6,1},{7,2},{8,15},{9,12},{10,... | collective-permute-start | bytes 24584 | tf_op jit(solution)/shard_map/ppermute | solution.py:454
  11.1 6.4 %collective-permute-start.5 = (f32[16,8,128]{2,1,0:T(8,128)S(1)}, f32[16,8,128]{2,1,0:T(8,128)S(1)}, u32[]{:S(2)}, u32[]{:S(2)}) collective-permute-start(f32[16,8,128]{2,1,0:T(8,128)S(1)} %get-tuple-element.49), channel_id=1, source_target_pairs={{0,8},{8,16},{16,24},{24,0},{1,9},{9,17},{17,25},{25,1},{2,10},{10... | collective-permute-start | bytes 196616 | tf_op jit(solution)/shard_map/ppermute | solution.py:446
  12.8 6.2 %collective-permute-start.6 = (f32[16,8,128]{2,1,0:T(8,128)S(1)}, f32[16,8,128]{2,1,0:T(8,128)S(1)}, u32[]{:S(2)}, u32[]{:S(2)}) collective-permute-start(f32[16,8,128]{2,1,0:T(8,128)S(1)} %get-tuple-element.50), channel_id=1, source_target_pairs={{0,24},{8,0},{16,8},{24,16},{1,25},{9,1},{17,9},{25,17},{2,26},{10... | collective-permute-start | bytes 196616 | tf_op jit(solution)/shard_map/ppermute | solution.py:446
  15.8 0.8 %copy-start.1 = (f32[32,512]{1,0:T(8,128)S(1)}, f32[32,512]{1,0:T(8,128)}, u32[]{:S(2)}) copy-start(f32[32,512]{1,0:T(8,128)} %basis.1) | copy-start | bytes 196612
  19.5 6.6 %collective-permute-start.7 = (f32[17,8,128]{2,1,0:T(8,128)S(1)}, f32[17,8,128]{2,1,0:T(8,128)S(1)}, u32[]{:S(2)}, u32[]{:S(2)}) collective-permute-start(f32[17,8,128]{2,1,0:T(8,128)S(1)} %get-tuple-element.53), channel_id=1, source_target_pairs={{0,8},{8,16},{16,24},{24,0},{1,9},{9,17},{17,25},{25,1},{2,10},{10... | collective-permute-start | bytes 208904 | tf_op jit(solution)/shard_map/ppermute | solution.py:446
  21.2 5.5 %collective-permute-start.8 = (f32[17,8,128]{2,1,0:T(8,128)S(1)}, f32[17,8,128]{2,1,0:T(8,128)S(1)}, u32[]{:S(2)}, u32[]{:S(2)}) collective-permute-start(f32[17,8,128]{2,1,0:T(8,128)S(1)} %get-tuple-element.54), channel_id=1, source_target_pairs={{0,24},{8,0},{16,8},{24,16},{1,25},{9,1},{17,9},{25,17},{2,26},{10... | collective-permute-start | bytes 208904 | tf_op jit(solution)/shard_map/ppermute | solution.py:446
  27.3 6.7 %collective-permute-start.9 = (f32[17,8,128]{2,1,0:T(8,128)S(1)}, f32[17,8,128]{2,1,0:T(8,128)S(1)}, u32[]{:S(2)}, u32[]{:S(2)}) collective-permute-start(f32[17,8,128]{2,1,0:T(8,128)S(1)} %get-tuple-element.56), channel_id=1, source_target_pairs={{0,8},{8,16},{16,24},{24,0},{1,9},{9,17},{17,25},{25,1},{2,10},{10... | collective-permute-start | bytes 208904 | tf_op jit(solution)/shard_map/ppermute | solution.py:446
  28.3 5.7 %collective-permute-start.10 = (f32[17,8,128]{2,1,0:T(8,128)S(1)}, f32[17,8,128]{2,1,0:T(8,128)S(1)}, u32[]{:S(2)}, u32[]{:S(2)}) collective-permute-start(f32[17,8,128]{2,1,0:T(8,128)S(1)} %get-tuple-element.57), channel_id=1, source_target_pairs={{0,24},{8,0},{16,8},{24,16},{1,25},{9,1},{17,9},{25,17},{2,26},{10... | collective-permute-start | bytes 208904 | tf_op jit(solution)/shard_map/ppermute | solution.py:446
  45.8 17.9 %all-to-all-start.1 = ((f32[32,8,128]{2,1,0:T(8,128)}), f32[32,8,128]{2,1,0:T(8,128)S(1)}, u32[]{:S(2)}, u32[]{:S(2)}) async-start(f32[32,8,128]{2,1,0:T(8,128)} %get-tuple-element.66), calls=%async_computation.1 | async-start | bytes 262144 | tf_op jit(solution)/shard_map/all_to_all | solution.py:543
  49.3 8.9 %collective-permute-start.11 = (f32[17,8,128]{2,1,0:T(8,128)S(1)}, f32[17,8,128]{2,1,0:T(8,128)S(1)}, u32[]{:S(2)}, u32[]{:S(2)}) collective-permute-start(f32[17,8,128]{2,1,0:T(8,128)S(1)} %get-tuple-element.59), channel_id=1, source_target_pairs={{0,8},{8,16},{16,24},{24,0},{1,9},{9,17},{17,25},{25,1},{2,10},{10... | collective-permute-start | bytes 208904 | tf_op jit(solution)/shard_map/ppermute | solution.py:446
  51.2 7.0 %collective-permute-start.12 = (f32[17,8,128]{2,1,0:T(8,128)S(1)}, f32[17,8,128]{2,1,0:T(8,128)S(1)}, u32[]{:S(2)}, u32[]{:S(2)}) collective-permute-start(f32[17,8,128]{2,1,0:T(8,128)S(1)} %get-tuple-element.60), channel_id=1, source_target_pairs={{0,24},{8,0},{16,8},{24,16},{1,25},{9,1},{17,9},{25,17},{2,26},{10... | collective-permute-start | bytes 208904 | tf_op jit(solution)/shard_map/ppermute | solution.py:446

commit v2 on v1

--- a/solution.py
+++ b/solution.py
@@ -356,28 +356,38 @@
     snap = aug[pl.ds(32, 16), :]
     snap_ref[...] = snap
     product = dot(snap, aug[...], 1) * (1.0 / total_rows)
-    packed = jnp.where(lanes() < 64, product[:8], roll(product[8:], 64, 1))
-    for d in range(out.shape[0]):
-        out[d] = packed
+    lane = lanes()
+    tail = jnp.where(lane < 120, roll(product[8:], 88, 1), roll(product[8:], 80, 1))
+    packed = jnp.where(lane < 44, product[:8], jnp.where(lane < 88, roll(roll(product[:8], 4, 0), 44, 1), tail))
+    twice = jnp.where(subs() < 4, packed, roll(packed, 4, 0))
+    for d in range(out.shape[0] // 8):
+        out[pl.ds(8 * d, 8), :] = twice
 
 
 def eliminate(tiles, count):
     sub = subs()
     done = list(tiles)
-    for k in range(count):
+
+    def spread(value, row):
+        return jnp.broadcast_to(value[row : row + 1, :], (8, 128))
+
+    for k in range(0, count, 2):
         t, r = divmod(k, 8)
-        pivot_row = jnp.broadcast_to(tiles[t][r : r + 1, :], (8, 128))
-        pivot = jnp.broadcast_to(pivot_row[:, k : k + 1], (8, 128))
-        inv = 1.0 / jnp.sqrt(pivot)
-        scaled = pivot_row * inv
+        row0, row1 = spread(tiles[t], r), spread(tiles[t], r + 1)
+        cols = {
+            u: [jnp.broadcast_to(tiles[u][:, k + i : k + i + 1], (8, 128)) for i in range(2)]
+            for u in range(t, len(tiles))
+        }
+        a, b, c = spread(cols[t][0], r), spread(cols[t][1], r), spread(cols[t][1], r + 1)
+        inv = 1.0 / (a * c - b * b)
+        part0 = (c * row0 - b * row1) * inv
+        part1 = (a * row1 - b * row0) * inv
+        ratio = b / a
+        first = row0 * (1.0 / jnp.sqrt(a))
+        second = (row1 - ratio * row0) * (1.0 / jnp.sqrt(c - ratio * b))
+        done[t] = jnp.where(sub == r, first, jnp.where(sub == r + 1, second, done[t]))
         for u in range(t, len(tiles)):
-            column = jnp.broadcast_to(tiles[u][:, k : k + 1], (8, 128))
-            update = tiles[u] - (column * inv) * scaled
-            if u == t:
-                done[t] = jnp.where(sub == r, scaled, done[t])
-                tiles[t] = jnp.where(sub > r, update, tiles[t])
-            else:
-                tiles[u] = update
+            tiles[u] = tiles[u] - (cols[u][0] * part0 + cols[u][1] * part1)
     return [jnp.where((lanes() >= 64) | (lanes() >= sub + 8 * t), tile, 0.0) for t, tile in enumerate(done)]
 
 
@@ -394,11 +404,15 @@
 
 def factor_kernel(parts, factor, head, snap, basis_ref, tri_ref, work):
     lane, sub = lanes(), subs()
-    total = parts[0]
-    for d in range(1, parts.shape[0]):
-        total = total + parts[d]
-    work[pl.ds(0, 8), :] = jnp.where(lane < 64, total, 0.0)
-    work[pl.ds(8, 8), :] = jnp.where(lane < 64, roll(total, -64, 1), 0.0)
+    sums = [parts[pl.ds(8 * d, 8), :] for d in range(parts.shape[0] // 8)]
+    while len(sums) > 1:
+        sums = [sums[i] + sums[i + 1] for i in range(0, len(sums), 2)]
+    total = sums[0] + roll(sums[0], 4, 0)
+    top = jnp.where(lane < 44, jnp.where(sub < 4, total, roll(total, -44, 1)), 0.0)
+    low = jnp.where(lane < 32, roll(total, -88, 1), roll(total, -80, 1))
+    work[pl.ds(0, 8), :] = top
+    work[pl.ds(8, 8), :] = jnp.where((sub < 4) & (lane < 44), low, 0.0)
+    work[pl.ds(8, 8), pl.ds(32, 8)] = top.T[40:48]
     cross = work[:, pl.ds(0, 32)]
     inner = work[:, pl.ds(32, 16)]
     inverse = factor[:, pl.ds(64, 32)]
@@ -536,7 +550,7 @@
     parts = lax.all_to_all(term.reshape(16 * highs, LOW), slab, 0, 0, tiled=True)
     snap, old_tile, gram = call(
         functools.partial(gram_kernel, float(rows_local * devices)),
-        (vmem(16, rows_local), vmem(*tile), f32(devices, *tile)),
+        (vmem(16, rows_local), vmem(*tile), f32(4 * devices, 128)),
         (pltpu.VMEM((128, rows_local), jnp.float32),),
         count=2,
     )(held(parts), held(old))

time: 66.8 us -> 62.9 us (0.942)
  Pallas kernels: 17.7 us -> 14.8 us
  waiting for transfers between devices: 10.6 us -> 9.51 us
    pallas_call x1, Pallas kernels: 4.53 us -> 2.26 us  [on_device(): call(old_factor_kernel, (vmem(32, 128), vmem(32, rows_local)), count=2)]
    ppermute x10, waiting for transfers between devices: 9.53 us -> 8.47 us  [shift(): lax.ppermute(value, axis, [(i, (i + step) % count) for i in range(count)])]
  transfers between devices with their start and end apart: 14 -> 14, of which waited for: 7 -> 7; matrix products, arithmetic and copies ran while one was open for 1% -> 1% of each run, Pallas kernels for 14% -> 12%
where the time goes in v2:
time: 62.9 us; the launch traced here: 62.6 us
  starting transfers between devices  26.6 us (42%)
  Pallas kernels  14.8 us (24%)
  waiting for transfers between devices  9.51 us (15%)
  blocking collectives  9.34 us (15%)
  local copies, waits for them, and re-layouts  1.59 us (3%)
  between operations  0.75 us (1%)
    ppermute x10, starting transfers between devices, shift(): lax.ppermute(value, axis, [(i, (i + step) % count) for i in range(count)])  17.3 us
    all_to_all x1, blocking collectives, on_device(): lax.all_to_all(term.reshape(16 * highs, LOW), slab, 0, 0, tiled=True)  9.34 us
    ppermute x10, waiting for transfers between devices, shift(): lax.ppermute(value, axis, [(i, (i + step) % count) for i in range(count)])  8.47 us
    ppermute x3, starting transfers between devices, shift_both(): return lax.ppermute(value, ('gy', 'gz'), pairs)  5.71 us
    all_to_all x1, starting transfers between devices, on_device(): grams = lax.all_to_all(gram, everyone, 0, 0, tiled=True)  3.57 us
    pallas_call x1, Pallas kernels, on_device(): call(early_kernel, vmem(highs, 16, LOW), (pltpu.VMEM((32 * highs, cells),...  2.85 us
    pallas_call x1, Pallas kernels, on_device(): call(factor_kernel, (f32(44, rows_local), f32(44, 44)), (pltpu.VMEM((16,...  2.33 us
    pallas_call x1, Pallas kernels, on_device(): call(old_factor_kernel, (vmem(32, 128), vmem(32, rows_local)), count=2)  2.26 us
  transfers between devices with their start and end apart: 14, of which 7 were waited for; matrix products, arithmetic and copies ran while one was open for 1% of the time, Pallas kernels for 12%

profile of v2, /device:TPU:0, one launch (start us, length us, event | category | flops | bytes accessed | tf_op | source)
XLA Modules:
  0.0 62.6 jit_solution(14250943748147162099)
XLA Ops:
  0.6 1.3 %shard_map.94 = (f32[19,2,16,128]{3,2,1,0:T(8,128)S(1)}, f32[2,16,128]{2,1,0:T(8,128)S(1)}, f32[3,8,128]{2,1,0:T(8,128)S(1)}, f32[3,8,128]{2,1,0:T(8,128)S(1)}, ...) custom-call(f32[8]{0:T(128)} %table_hbm.1, f32[19,2,16,128]{3,2,1,0:T(8,128)} %ratio_hbm.1, ...), custom_call_target="tpu_custom_call" | custom-call | tf_op jit(solution)/shard_map/pallas_call | solution.py:488
  2.0 3.1 %collective-permute-start.2 = (f32[40,8,128]{2,1,0:T(8,128)S(1)}, f32[40,8,128]{2,1,0:T(8,128)S(1)}, u32[]{:S(2)}, u32[]{:S(2)}) collective-permute-start(f32[40,8,128]{2,1,0:T(8,128)S(1)} %get-tuple-element.44), channel_id=1, source_target_pairs={{0,4},{1,5},{2,6},{3,7},{4,0},{5,1},{6,2},{7,3},{8,12},{9,13},{10,... | collective-permute-start | bytes 491528 | tf_op jit(solution)/shard_map/ppermute | solution.py:468
  5.1 1.7 %collective-permute-start.1 = (f32[3,8,128]{2,1,0:T(8,128)S(1)}, f32[3,8,128]{2,1,0:T(8,128)S(1)}, u32[]{:S(2)}, u32[]{:S(2)}) collective-permute-start(f32[3,8,128]{2,1,0:T(8,128)S(1)} %get-tuple-element.41), channel_id=1, source_target_pairs={{0,3},{1,0},{2,1},{3,2},{4,7},{5,4},{6,5},{7,6},{8,11},{9,8},{10,9... | collective-permute-start | bytes 36872 | tf_op jit(solution)/shard_map/ppermute | solution.py:460
  6.8 2.6 %collective-permute-start.4 = (f32[2,8,128]{2,1,0:T(8,128)S(1)}, f32[2,8,128]{2,1,0:T(8,128)S(1)}, u32[]{:S(2)}, u32[]{:S(2)}) collective-permute-start(f32[2,8,128]{2,1,0:T(8,128)S(1)} %get-tuple-element.46), channel_id=1, source_target_pairs={{0,7},{1,4},{2,5},{3,6},{4,3},{5,0},{6,1},{7,2},{8,15},{9,12},{10,... | collective-permute-start | bytes 24584 | tf_op jit(solution)/shard_map/ppermute | solution.py:468
  9.8 0.9 %collective-permute-done.3.cr = f32[2,8,128]{2,1,0:T(8,128)S(1)} collective-permute-done((f32[2,8,128]{2,1,0:T(8,128)S(1)}, f32[2,8,128]{2,1,0:T(8,128)S(1)}, u32[]{:S(2)}, u32[]{:S(2)}) %collective-permute-start.3) | collective-permute-done | bytes 8224 | tf_op jit(solution)/shard_map/ppermute | solution.py:468
  11.1 1.6 %collective-permute-start.5 = (f32[16,8,128]{2,1,0:T(8,128)S(1)}, f32[16,8,128]{2,1,0:T(8,128)S(1)}, u32[]{:S(2)}, u32[]{:S(2)}) collective-permute-start(f32[16,8,128]{2,1,0:T(8,128)S(1)} %get-tuple-element.49), channel_id=1, source_target_pairs={{0,8},{8,16},{16,24},{24,0},{1,9},{9,17},{17,25},{25,1},{2,10},{10... | collective-permute-start | bytes 196616 | tf_op jit(solution)/shard_map/ppermute | solution.py:460
  12.8 2.2 %collective-permute-start.6 = (f32[16,8,128]{2,1,0:T(8,128)S(1)}, f32[16,8,128]{2,1,0:T(8,128)S(1)}, u32[]{:S(2)}, u32[]{:S(2)}) collective-permute-start(f32[16,8,128]{2,1,0:T(8,128)S(1)} %get-tuple-element.50), channel_id=1, source_target_pairs={{0,24},{8,0},{16,8},{24,16},{1,25},{9,1},{17,9},{25,17},{2,26},{10... | collective-permute-start | bytes 196616 | tf_op jit(solution)/shard_map/ppermute | solution.py:460
  17.5 1.4 %collective-permute-done.6.xl = f32[16,8,128]{2,1,0:T(8,128)S(1)} collective-permute-done((f32[16,8,128]{2,1,0:T(8,128)S(1)}, f32[16,8,128]{2,1,0:T(8,128)S(1)}, u32[]{:S(2)}, u32[]{:S(2)}) %collective-permute-start.6) | collective-permute-done | bytes 65568 | tf_op jit(solution)/shard_map/ppermute | solution.py:460
  19.5 1.0 %collective-permute-start.7 = (f32[17,8,128]{2,1,0:T(8,128)S(1)}, f32[17,8,128]{2,1,0:T(8,128)S(1)}, u32[]{:S(2)}, u32[]{:S(2)}) collective-permute-start(f32[17,8,128]{2,1,0:T(8,128)S(1)} %get-tuple-element.53), channel_id=1, source_target_pairs={{0,8},{8,16},{16,24},{24,0},{1,9},{9,17},{17,25},{25,1},{2,10},{10... | collective-permute-start | bytes 208904 | tf_op jit(solution)/shard_map/ppermute | solution.py:460
  21.2 2.9 %collective-permute-start.8 = (f32[17,8,128]{2,1,0:T(8,128)S(1)}, f32[17,8,128]{2,1,0:T(8,128)S(1)}, u32[]{:S(2)}, u32[]{:S(2)}) collective-permute-start(f32[17,8,128]{2,1,0:T(8,128)S(1)} %get-tuple-element.54), channel_id=1, source_target_pairs={{0,24},{8,0},{16,8},{24,16},{1,25},{9,1},{17,9},{25,17},{2,26},{10... | collective-permute-start | bytes 208904 | tf_op jit(solution)/shard_map/ppermute | solution.py:460
  24.1 2.0 %collective-permute-done.7.xr = f32[17,8,128]{2,1,0:T(8,128)S(1)} collective-permute-done((f32[17,8,128]{2,1,0:T(8,128)S(1)}, f32[17,8,128]{2,1,0:T(8,128)S(1)}, u32[]{:S(2)}, u32[]{:S(2)}) %collective-permute-start.7) | collective-permute-done | bytes 69664 | tf_op jit(solution)/shard_map/ppermute | solution.py:460
  27.3 1.0 %collective-permute-start.9 = (f32[17,8,128]{2,1,0:T(8,128)S(1)}, f32[17,8,128]{2,1,0:T(8,128)S(1)}, u32[]{:S(2)}, u32[]{:S(2)}) collective-permute-start(f32[17,8,128]{2,1,0:T(8,128)S(1)} %get-tuple-element.56), channel_id=1, source_target_pairs={{0,8},{8,16},{16,24},{24,0},{1,9},{9,17},{17,25},{25,1},{2,10},{10... | collective-permute-start | bytes 208904 | tf_op jit(solution)/shard_map/ppermute | solution.py:460
  28.3 2.8 %collective-permute-start.10 = (f32[17,8,128]{2,1,0:T(8,128)S(1)}, f32[17,8,128]{2,1,0:T(8,128)S(1)}, u32[]{:S(2)}, u32[]{:S(2)}) collective-permute-start(f32[17,8,128]{2,1,0:T(8,128)S(1)} %get-tuple-element.57), channel_id=1, source_target_pairs={{0,24},{8,0},{16,8},{24,16},{1,25},{9,1},{17,9},{25,17},{2,26},{10... | collective-permute-start | bytes 208904 | tf_op jit(solution)/shard_map/ppermute | solution.py:460
  31.1 2.9 %shard_map.103.early = f32[16,16,256]{2,1,0:T(8,128)S(1)} custom-call(f32[3,2,16,128]{3,2,1,0:T(8,128)S(1)} %get-tuple-element.62.v0, f32[3,2,16,128]{3,2,1,0:T(8,128)S(1)} %get-tuple-element.63.v1, f32[3,2,16,128]{3,2,1,0:T(8,128)S(1)} %get-tuple-element.64.v2, s32[2,16,128]{2,1,0:T(8,128)S(1)} %copy-done, bf16[256,4096]{1,0:T(8,128)(2,1)S(1)} %shard_map.102.right), custom_call_target="tpu_custom_call" | custom-call | tf_op jit(solution)/shard_map/pallas_call | solution.py:542
  34.6 0.9 %shard_map.104 = f32[16,16,256]{2,1,0:T(8,128)S(1)} custom-call(f32[3,2,16,128]{3,2,1,0:T(8,128)S(1)} %get-tuple-element.61.v3, s32[2,16,128]{2,1,0:T(8,128)S(1)} %copy-done, bf16[256,4096]{1,0:T(8,128)(2,1)S(1)} %shard_map.102.right, f32[16,16,256]{2,1,0:T(8,128)S(1)} %shard_map.103.early, f32[8,128]{1,0:T(8,128)S(1)} %get-tuple-element.51.rider_r.rider_l.own, ...), custom_call_target="tpu_custom_call" | custom-call | tf_op jit(solution)/shard_map/pallas_call | solution.py:546
  35.5 9.3 %all_to_all.22 = f32[8,32,256]{2,1,0:T(8,128)S(1)} all-to-all(f32[8,32,256]{2,1,0:T(8,128)S(1)} %bitcast.12), channel_id=1, replica_groups=mesh['gx'=4,'gy'=2,'gz'=4] {'gy','gz'}, dimensions={0} | all-to-all | bytes 524288 | tf_op jit(solution)/shard_map/all_to_all | solution.py:550
  44.8 0.9 %shard_map.105 = (f32[16,512]{1,0:T(8,128)S(1)}, f32[8,128]{1,0:T(8,128)S(1)}, f32[128,128]{1,0:T(8,128)}) custom-call(f32[256,256]{1,0:T(8,128)S(1)} %bitcast.11, f32[32,512]{1,0:T(8,128)S(1)} %get-tuple-element.65.scaled), custom_call_target="tpu_custom_call" | custom-call | tf_op jit(solution)/shard_map/pallas_call | solution.py:551
  45.7 3.6 %all-to-all-start.1 = ((f32[32,4,128]{2,1,0:T(4,128)}), f32[32,4,128]{2,1,0:T(4,128)S(1)}, u32[]{:S(2)}, u32[]{:S(2)}) async-start(f32[32,4,128]{2,1,0:T(4,128)} %bitcast.6), calls=%async_computation.1 | async-start | bytes 131072 | tf_op jit(solution)/shard_map/all_to_all | solution.py:557
  49.3 1.8 %collective-permute-start.11 = (f32[17,8,128]{2,1,0:T(8,128)S(1)}, f32[17,8,128]{2,1,0:T(8,128)S(1)}, u32[]{:S(2)}, u32[]{:S(2)}) collective-permute-start(f32[17,8,128]{2,1,0:T(8,128)S(1)} %get-tuple-element.59), channel_id=1, source_target_pairs={{0,8},{8,16},{16,24},{24,0},{1,9},{9,17},{17,25},{25,1},{2,10},{10... | collective-permute-start | bytes 208904 | tf_op jit(solution)/shard_map/ppermute | solution.py:460
  51.1 2.1 %collective-permute-start.12 = (f32[17,8,128]{2,1,0:T(8,128)S(1)}, f32[17,8,128]{2,1,0:T(8,128)S(1)}, u32[]{:S(2)}, u32[]{:S(2)}) collective-permute-start(f32[17,8,128]{2,1,0:T(8,128)S(1)} %get-tuple-element.60), channel_id=1, source_target_pairs={{0,24},{8,0},{16,8},{24,16},{1,25},{9,1},{17,9},{25,17},{2,26},{10... | collective-permute-start | bytes 208904 | tf_op jit(solution)/shard_map/ppermute | solution.py:460
  53.2 3.9 %collective-permute-done.11.xr = f32[17,8,128]{2,1,0:T(8,128)S(1)} collective-permute-done((f32[17,8,128]{2,1,0:T(8,128)S(1)}, f32[17,8,128]{2,1,0:T(8,128)S(1)}, u32[]{:S(2)}, u32[]{:S(2)}) %collective-permute-start.11) | collective-permute-done | bytes 69664 | tf_op jit(solution)/shard_map/ppermute | solution.py:460
  57.1 0.9 %shard_map.101 = f32[19,2,16,128]{3,2,1,0:T(8,128)} custom-call(f32[19,2,24,256]{3,2,1,0:T(8,128)S(1)} %get-tuple-element.58.prev, f32[17,8,128]{2,1,0:T(8,128)S(1)} %collective-permute-done.11.xr, f32[17,8,128]{2,1,0:T(8,128)S(1)} %collective-permute-done.12.xl), custom_call_target="tpu_custom_call" | custom-call | tf_op jit(solution)/shard_map/pallas_call | solution.py:562
  58.0 2.3 %shard_map.106 = (f32[32,128]{1,0:T(8,128)S(1)}, f32[32,512]{1,0:T(8,128)S(1)}) custom-call(f32[8,128]{1,0:T(8,128)S(1)} %get-tuple-element.67.tile, f32[32,512]{1,0:T(8,128)S(1)} %get-tuple-element.65.scaled), custom_call_target="tpu_custom_call" | custom-call | tf_op jit(solution)/shard_map/pallas_call | solution.py:558
  60.3 2.3 %shard_map.107 = (f32[44,512]{1,0:T(8,128)}, f32[44,44]{1,0:T(8,128)}) custom-call(f32[128,128]{1,0:T(8,128)S(1)} %bitcast.13, f32[32,128]{1,0:T(8,128)S(1)} %get-tuple-element.68.factor, f32[32,512]{1,0:T(8,128)S(1)} %get-tuple-element.69.head, f32[16,512]{1,0:T(8,128)S(1)} %get-tuple-element.70.snap), custom_call_target="tpu_custom_call" | custom-call | tf_op jit(solution)/shard_map/pallas_call | solution.py:559
  (28 shorter events, 6.2 us)
Async XLA Ops:
  0.6 19.9 %copy-start = (s32[2,16,128]{2,1,0:T(8,128)S(1)}, s32[2,16,128]{2,1,0:T(8,128)}, u32[]{:S(2)}) copy-start(s32[2,16,128]{2,1,0:T(8,128)} %row_map.5) | copy-start | bytes 49156
  2.0 8.9 %collective-permute-start.2 = (f32[40,8,128]{2,1,0:T(8,128)S(1)}, f32[40,8,128]{2,1,0:T(8,128)S(1)}, u32[]{:S(2)}, u32[]{:S(2)}) collective-permute-start(f32[40,8,128]{2,1,0:T(8,128)S(1)} %get-tuple-element.44), channel_id=1, source_target_pairs={{0,4},{1,5},{2,6},{3,7},{4,0},{5,1},{6,2},{7,3},{8,12},{9,13},{10,... | collective-permute-start | bytes 491528 | tf_op jit(solution)/shard_map/ppermute | solution.py:468
  5.0 4.4 %collective-permute-start = (f32[3,8,128]{2,1,0:T(8,128)S(1)}, f32[3,8,128]{2,1,0:T(8,128)S(1)}, u32[]{:S(2)}, u32[]{:S(2)}) collective-permute-start(f32[3,8,128]{2,1,0:T(8,128)S(1)} %get-tuple-element.40), channel_id=1, source_target_pairs={{0,1},{1,2},{2,3},{3,0},{4,5},{5,6},{6,7},{7,4},{8,9},{9,10},{10,1... | collective-permute-start | bytes 36872 | tf_op jit(solution)/shard_map/ppermute | solution.py:460
  5.1 4.4 %collective-permute-start.1 = (f32[3,8,128]{2,1,0:T(8,128)S(1)}, f32[3,8,128]{2,1,0:T(8,128)S(1)}, u32[]{:S(2)}, u32[]{:S(2)}) collective-permute-start(f32[3,8,128]{2,1,0:T(8,128)S(1)} %get-tuple-element.41), channel_id=1, source_target_pairs={{0,3},{1,0},{2,1},{3,2},{4,7},{5,4},{6,5},{7,6},{8,11},{9,8},{10,9... | collective-permute-start | bytes 36872 | tf_op jit(solution)/shard_map/ppermute | solution.py:460
  6.8 4.0 %collective-permute-start.3 = (f32[2,8,128]{2,1,0:T(8,128)S(1)}, f32[2,8,128]{2,1,0:T(8,128)S(1)}, u32[]{:S(2)}, u32[]{:S(2)}) collective-permute-start(f32[2,8,128]{2,1,0:T(8,128)S(1)} %get-tuple-element.45), channel_id=1, source_target_pairs={{0,5},{1,6},{2,7},{3,4},{4,1},{5,2},{6,3},{7,0},{8,13},{9,14},{10,... | collective-permute-start | bytes 24584 | tf_op jit(solution)/shard_map/ppermute | solution.py:468
  6.8 4.1 %collective-permute-start.4 = (f32[2,8,128]{2,1,0:T(8,128)S(1)}, f32[2,8,128]{2,1,0:T(8,128)S(1)}, u32[]{:S(2)}, u32[]{:S(2)}) collective-permute-start(f32[2,8,128]{2,1,0:T(8,128)S(1)} %get-tuple-element.46), channel_id=1, source_target_pairs={{0,7},{1,4},{2,5},{3,6},{4,3},{5,0},{6,1},{7,2},{8,15},{9,12},{10,... | collective-permute-start | bytes 24584 | tf_op jit(solution)/shard_map/ppermute | solution.py:468
  11.1 6.4 %collective-permute-start.5 = (f32[16,8,128]{2,1,0:T(8,128)S(1)}, f32[16,8,128]{2,1,0:T(8,128)S(1)}, u32[]{:S(2)}, u32[]{:S(2)}) collective-permute-start(f32[16,8,128]{2,1,0:T(8,128)S(1)} %get-tuple-element.49), channel_id=1, source_target_pairs={{0,8},{8,16},{16,24},{24,0},{1,9},{9,17},{17,25},{25,1},{2,10},{10... | collective-permute-start | bytes 196616 | tf_op jit(solution)/shard_map/ppermute | solution.py:460
  12.8 6.2 %collective-permute-start.6 = (f32[16,8,128]{2,1,0:T(8,128)S(1)}, f32[16,8,128]{2,1,0:T(8,128)S(1)}, u32[]{:S(2)}, u32[]{:S(2)}) collective-permute-start(f32[16,8,128]{2,1,0:T(8,128)S(1)} %get-tuple-element.50), channel_id=1, source_target_pairs={{0,24},{8,0},{16,8},{24,16},{1,25},{9,1},{17,9},{25,17},{2,26},{10... | collective-permute-start | bytes 196616 | tf_op jit(solution)/shard_map/ppermute | solution.py:460
  15.8 0.8 %copy-start.1 = (f32[32,512]{1,0:T(8,128)S(1)}, f32[32,512]{1,0:T(8,128)}, u32[]{:S(2)}) copy-start(f32[32,512]{1,0:T(8,128)} %basis.1) | copy-start | bytes 196612
  19.5 6.6 %collective-permute-start.7 = (f32[17,8,128]{2,1,0:T(8,128)S(1)}, f32[17,8,128]{2,1,0:T(8,128)S(1)}, u32[]{:S(2)}, u32[]{:S(2)}) collective-permute-start(f32[17,8,128]{2,1,0:T(8,128)S(1)} %get-tuple-element.53), channel_id=1, source_target_pairs={{0,8},{8,16},{16,24},{24,0},{1,9},{9,17},{17,25},{25,1},{2,10},{10... | collective-permute-start | bytes 208904 | tf_op jit(solution)/shard_map/ppermute | solution.py:460
  21.2 5.5 %collective-permute-start.8 = (f32[17,8,128]{2,1,0:T(8,128)S(1)}, f32[17,8,128]{2,1,0:T(8,128)S(1)}, u32[]{:S(2)}, u32[]{:S(2)}) collective-permute-start(f32[17,8,128]{2,1,0:T(8,128)S(1)} %get-tuple-element.54), channel_id=1, source_target_pairs={{0,24},{8,0},{16,8},{24,16},{1,25},{9,1},{17,9},{25,17},{2,26},{10... | collective-permute-start | bytes 208904 | tf_op jit(solution)/shard_map/ppermute | solution.py:460
  27.3 6.7 %collective-permute-start.9 = (f32[17,8,128]{2,1,0:T(8,128)S(1)}, f32[17,8,128]{2,1,0:T(8,128)S(1)}, u32[]{:S(2)}, u32[]{:S(2)}) collective-permute-start(f32[17,8,128]{2,1,0:T(8,128)S(1)} %get-tuple-element.56), channel_id=1, source_target_pairs={{0,8},{8,16},{16,24},{24,0},{1,9},{9,17},{17,25},{25,1},{2,10},{10... | collective-permute-start | bytes 208904 | tf_op jit(solution)/shard_map/ppermute | solution.py:460
  28.3 5.7 %collective-permute-start.10 = (f32[17,8,128]{2,1,0:T(8,128)S(1)}, f32[17,8,128]{2,1,0:T(8,128)S(1)}, u32[]{:S(2)}, u32[]{:S(2)}) collective-permute-start(f32[17,8,128]{2,1,0:T(8,128)S(1)} %get-tuple-element.57), channel_id=1, source_target_pairs={{0,24},{8,0},{16,8},{24,16},{1,25},{9,1},{17,9},{25,17},{2,26},{10... | collective-permute-start | bytes 208904 | tf_op jit(solution)/shard_map/ppermute | solution.py:460
  45.7 14.5 %all-to-all-start.1 = ((f32[32,4,128]{2,1,0:T(4,128)}), f32[32,4,128]{2,1,0:T(4,128)S(1)}, u32[]{:S(2)}, u32[]{:S(2)}) async-start(f32[32,4,128]{2,1,0:T(4,128)} %bitcast.6), calls=%async_computation.1 | async-start | bytes 131072 | tf_op jit(solution)/shard_map/all_to_all | solution.py:557
  49.3 7.8 %collective-permute-start.11 = (f32[17,8,128]{2,1,0:T(8,128)S(1)}, f32[17,8,128]{2,1,0:T(8,128)S(1)}, u32[]{:S(2)}, u32[]{:S(2)}) collective-permute-start(f32[17,8,128]{2,1,0:T(8,128)S(1)} %get-tuple-element.59), channel_id=1, source_target_pairs={{0,8},{8,16},{16,24},{24,0},{1,9},{9,17},{17,25},{25,1},{2,10},{10... | collective-permute-start | bytes 208904 | tf_op jit(solution)/shard_map/ppermute | solution.py:460
  51.1 6.0 %collective-permute-start.12 = (f32[17,8,128]{2,1,0:T(8,128)S(1)}, f32[17,8,128]{2,1,0:T(8,128)S(1)}, u32[]{:S(2)}, u32[]{:S(2)}) collective-permute-start(f32[17,8,128]{2,1,0:T(8,128)S(1)} %get-tuple-element.60), channel_id=1, source_target_pairs={{0,24},{8,0},{16,8},{24,16},{1,25},{9,1},{17,9},{25,17},{2,26},{10... | collective-permute-start | bytes 208904 | tf_op jit(solution)/shard_map/ppermute | solution.py:460

commit v3 on v2

--- a/solution.py
+++ b/solution.py
@@ -111,7 +111,7 @@
         cl_ref[at] = cl[at]
 
 
-def collide(pops, g):
+def moments(pops, g):
     density = pops[0]
     for q in range(1, 19):
         density = density + pops[q]
@@ -126,6 +126,11 @@
             elif c == -1:
                 total = total - pops[q]
         speeds.append(total * scale)
+    return density, speeds
+
+
+def collide(pops, g):
+    density, speeds = moments(pops, g)
     square = speeds[0] * speeds[0] + speeds[1] * speeds[1] + speeds[2] * speeds[2]
     solid = g < 0.0
     keep = 1.0 - 1.0 / relax_time
@@ -155,11 +160,11 @@
         for yt in tiles:
             for lt in range(2):
                 rows, cols = pl.ds(8 * yt, 8), pl.ds(128 * lt, 128)
-                pops = [source[q, x, rows, cols] for q in range(19)]
+                pops = [source(q, x, rows, cols) for q in range(19)]
                 relaxed, vel = collide(pops, g_of[x, rows, cols])
                 for q in range(19):
                     out[q, x, rows, cols] = relaxed[q]
-                if yt < 2 and lt == 0:
+                if vel_ref is not None and yt < 2 and lt == 0:
                     for a in range(3):
                         vel_ref[a, x, rows, :] = vel[a]
 
@@ -191,7 +196,7 @@
                 tile = jnp.where(lane >= 124, roll(left[at], 124 - 4 * k, 1), tile)
                 ref[x, rows, pl.ds(0, 128)] = own
                 ref[x, rows, pl.ds(128, 128)] = tile
-    collide_all(wide, g_ref, out, vel_ref, range(2))
+    collide_all(lambda q, x, rows, cols: wide[q, x, rows, cols], g_ref, out, vel_ref, range(2))
 
 
 def outer_kernel(out_in, g_in, y, cr, cl, out, g_ref, xr_ref, xl_ref, wide):
@@ -208,7 +213,7 @@
             cols = pl.ds(128 * lt, 128)
             ref[0, pl.ds(16, 8), cols] = jnp.where(sub < 4, low[lt], roll(high[lt], 4, 0))
             ref[1, pl.ds(16, 8), cols] = jnp.where(sub < 4, roll(low[lt], 4, 0), high[lt])
-    collide_all(wide, g_ref, out, None, (2,))
+    collide_all(lambda q, x, rows, cols: wide[q, x, rows, cols], g_ref, out, None, (2,))
     pack_x(out, xr_ref, xl_ref)
 
 
@@ -221,33 +226,61 @@
                 side[s, i, pl.ds(8 * yt, 8), pl.ds(128, 128)] = roll(ref[15], -(8 * j + 4), 1)
 
 
-def streamed(prev, side, q, x):
-    c = [int(v) for v in LATTICE[q]]
-    if c[0] == 1 and x == 0:
-        value = side[0, PLUS_X.index(q)]
-    elif c[0] == -1 and x == 1:
-        value = side[1, MINUS_X.index(q)]
-    else:
-        value = prev[q, x - c[0]]
-    return roll(roll(value, c[1], 0), c[2], 1)
-
-
-def step_kernel(prev, g_ref, xr, xl, rider_r, rider_l, out, vel_ref, xr_ref, xl_ref, wide, side):
-    unpack_x(xr, xl, side)
+def turned(value, q):
+    return roll(roll(value, int(LATTICE[q, 1]), 0), int(LATTICE[q, 2]), 1)
+
+
+def remote(q, x):
+    if LATTICE[q, 0] == 1 and x == 0:
+        return 0, PLUS_X.index(q)
+    if LATTICE[q, 0] == -1 and x == 1:
+        return 1, MINUS_X.index(q)
+    return None
+
+
+def local_kernel(prev, ahead):
     for q in range(19):
         for x in range(2):
-            wide[q, x] = streamed(prev, side, q, x)
-    collide_all(wide, g_ref, out, vel_ref)
+            if remote(q, x) is None:
+                ahead[q, x] = turned(prev[q, x - int(LATTICE[q, 0])], q)
+
+
+def take_faces(xr, xl, side):
+    unpack_x(xr, xl, side)
+    for s, directions in enumerate((PLUS_X, MINUS_X)):
+        for i, q in enumerate(directions):
+            side[s, i] = turned(side[s, i], q)
+
+
+def chooser(ahead, side):
+    def pick(q, x, rows, cols):
+        at = remote(q, x)
+        return ahead[q, x, rows, cols] if at is None else side[at[0], at[1], rows, cols]
+
+    return pick
+
+
+def step_kernel(ahead, g_ref, xr, xl, rider_r, rider_l, out, vel_ref, xr_ref, xl_ref, side):
+    take_faces(xr, xl, side)
+    collide_all(chooser(ahead, side), g_ref, out, vel_ref)
     pack_x(out, xr_ref, xl_ref)
     xr_ref[16] = rider_r[...]
     xl_ref[16] = rider_l[...]
 
 
+def end_step_kernel(ahead, g_ref, xr, xl, out, xr_ref, xl_ref, side):
+    take_faces(xr, xl, side)
+    collide_all(chooser(ahead, side), g_ref, out, None)
+    pack_x(out, xr_ref, xl_ref)
+
+
 def last_kernel(prev, xr, xl, out, side):
-    unpack_x(xr, xl, side)
+    take_faces(xr, xl, side)
     for q in range(19):
         for x in range(2):
-            out[q, x] = streamed(prev, side, q, x)[:16, :128]
+            at = remote(q, x)
+            value = turned(prev[q, x - int(LATTICE[q, 0])], q) if at is None else side[at[0], at[1]]
+            out[q, x] = value[:16, :128]
 
 
 def split(value):
@@ -271,28 +304,33 @@
     )
 
 
-def early_kernel(v0, v1, v2, row_map, right, out, left):
+def restricted(v, row_map, right, left):
+    highs = left.shape[0] // 6
+    high_at = lax.broadcasted_iota(jnp.int32, (highs, 128), 0)
+    for x in range(2):
+        for y in range(16):
+            cols = pl.ds(128 * (16 * x + y), 128)
+            here = high_at == row_map[x, pl.ds(y, 1), :] // LOW
+            for a in range(3):
+                for i, part in enumerate(split(v[a, x, pl.ds(y, 1), :])):
+                    left[pl.ds(highs * (3 * i + a), highs), cols] = jnp.where(here, part, 0.0).astype(jnp.bfloat16)
+    both = times_onehot(left, right)
+    half = 3 * highs
+    return both[:half] + both[half:]
+
+
+def part_kernel(v, row_map, right, out, left):
+    out[...] = restricted(v, row_map, right, left)
+
+
+def early_kernel(v2, row_map, right, part0, part1, out, left):
     highs = out.shape[0]
-    vels = (v0, v1, v2)
-
-    def row(i, carry):
-        x, y = i // 16, i % 16
-        cols = pl.ds(pl.multiple_of(128 * i, 128), 128)
-        high = row_map[x, pl.ds(y, 1), :] // LOW
-        vals = [v[a, x, pl.ds(y, 1), :] for v in vels for a in range(3)]
-        vals = jnp.concatenate(vals + [jnp.zeros((7, 128), jnp.float32)], 0)
-        big, rest = split(vals)
-        for h in range(highs):
-            here = high == h
-            left[pl.ds(16 * h, 16), cols] = jnp.where(here, big, 0.0).astype(jnp.bfloat16)
-            left[pl.ds(16 * (highs + h), 16), cols] = jnp.where(here, rest, 0.0).astype(jnp.bfloat16)
-        return carry
-
-    lax.fori_loop(0, 32, row, 0)
-    both = times_onehot(left, right)
-    half = 16 * highs
+    parts = (part0[...], part1[...], restricted(v2, row_map, right, left))
     for h in range(highs):
-        out[h] = both[16 * h : 16 * h + 16] + both[half + 16 * h : half + 16 * h + 16]
+        for s, part in enumerate(parts):
+            for a in range(3):
+                out[h, pl.ds(3 * s + a, 1), :] = part[highs * a + h : highs * a + h + 1]
+        out[h, pl.ds(9, 7), :] = jnp.zeros((7, LOW), jnp.float32)
 
 
 def old_kernel(total_rows, basis, sigma, scaled_ref, tile_ref, work):
@@ -318,19 +356,19 @@
     )
 
 
-def late_kernel(v3, row_map, right, early, own, near_r, near_l, far, out, left):
+def late_kernel(ahead, g_ref, xr, xl, row_map, right, early, own, near_r, near_l, far, out, left, side, v3):
+    take_faces(xr, xl, side)
+    pick = chooser(ahead, side)
+    for x in range(2):
+        for yt in range(2):
+            rows, cols = pl.ds(8 * yt, 8), pl.ds(0, 128)
+            g = g_ref[x, rows, cols]
+            _, speeds = moments([pick(q, x, rows, cols) for q in range(19)], g)
+            factor = jnp.where(g < 0.0, 0.0, vel_scale / VOX_ROW)
+            for a in range(3):
+                v3[a, x, rows, :] = speeds[a] * factor
     highs = out.shape[0]
-    high_at = lax.broadcasted_iota(jnp.int32, (highs, 128), 0)
-    for x in range(2):
-        for y in range(16):
-            cols = pl.ds(128 * (16 * x + y), 128)
-            here = high_at == row_map[x, pl.ds(y, 1), :] // LOW
-            for a in range(3):
-                for i, part in enumerate(split(v3[a, x, pl.ds(y, 1), :])):
-                    left[pl.ds(highs * (3 * i + a), highs), cols] = jnp.where(here, part, 0.0).astype(jnp.bfloat16)
-    both = times_onehot(left, right)
-    half = 3 * highs
-    both = both[:half] + both[half:]
+    both = restricted(v3, row_map, right, left)
     out[...] = early[...]
     old = (own[...] + far[...]) + (near_r[...] + near_l[...])
     for h in range(highs):
@@ -524,7 +562,8 @@
     if not ring:
         own = lax.psum(own, "gx")
     none = jnp.zeros(tile, jnp.float32)
-    step = jax.jit(call(step_kernel, (big, vel, loaded, loaded), (wide, side), count=6))
+    step = jax.jit(call(step_kernel, (big, vel, loaded, loaded), (side,), count=6))
+    local = jax.jit(call(local_kernel, big, count=1))
     onehot = call(onehot_kernel, pltpu.VMEM((LOW, cells), jnp.bfloat16), count=1)(row_map)
     riders, got = (own, own), [none] * 3
     for s in range(1, STEPS):
@@ -534,19 +573,40 @@
             riders = (xr[16], none)
         if s == 3 and ring:
             got[2] = xr[16]
-            riders = (none, none)
-        relaxed, vel_s, xr, xl = step(*map(held, (relaxed, g_wide, xr, xl, *riders)))
-        vels.append(vel_s)
+        ahead = local(held(relaxed))
+        if s < 3:
+            relaxed, vel_s, xr, xl = step(*map(held, (ahead, g_wide, xr, xl, *riders)))
+            vels.append(vel_s)
+    state = tuple(map(held, (ahead, g_wide, xr, xl)))
+    relaxed, xr, xl = call(end_step_kernel, (big, face, face), (side,), count=4)(*state)
     xr, xl = shift(xr, "gx", 1), shift(xl, "gx", -1)
 
+    part = jax.jit(
+        call(
+            part_kernel,
+            vmem(3 * highs, LOW),
+            (pltpu.VMEM((6 * highs, cells), jnp.bfloat16),),
+            count=3,
+            limit=8 + highs // 2,
+        )
+    )
+    parts = []
+    for i in range(2):
+        parts.append(part(held(vels[i]), row_map, held(onehot)))
     early = call(
-        early_kernel, vmem(highs, 16, LOW), (pltpu.VMEM((32 * highs, cells), jnp.bfloat16),), count=5,
+        early_kernel,
+        vmem(highs, 16, LOW),
+        (pltpu.VMEM((6 * highs, cells), jnp.bfloat16),),
+        count=5,
         limit=8 + highs // 2,
-    )(*map(held, vels[:3]), row_map, held(onehot))
+    )(held(vels[2]), row_map, *map(held, (onehot, *parts)))
     term = call(
-        late_kernel, f32(highs, 16, LOW), (pltpu.VMEM((6 * highs, cells), jnp.bfloat16),), count=8,
+        late_kernel,
+        f32(highs, 16, LOW),
+        (pltpu.VMEM((6 * highs, cells), jnp.bfloat16), side, pltpu.VMEM((3, 2, 16, 128), jnp.float32)),
+        count=11,
         limit=8 + highs // 2,
-    )(held(vels[3]), row_map, *map(held, (onehot, early, own, *got)))
+    )(*state, row_map, *map(held, (onehot, early, own, *got)))
     parts = lax.all_to_all(term.reshape(16 * highs, LOW), slab, 0, 0, tiled=True)
     snap, old_tile, gram = call(
         functools.partial(gram_kernel, float(rows_local * devices)),

time: 62.9 us -> 63.4 us (level)
  starting transfers between devices: 26.6 us -> 27.3 us
    pallas_call x4 -> x9, Pallas kernels: 4.63 us -> 4.64 us  [the longest x2 1.67 us: on_device(): parts.append(part(held(vels[i]), row_map, held(onehot)))]
  transfers between devices with their start and end apart: 14 -> 14, of which waited for: 7 -> 8; matrix products, arithmetic and copies ran while one was open for 1% -> 1% of each run, Pallas kernels for 12% -> 13%
where the time goes in v3:
time: 63.4 us; the launch traced here: 63.1 us
  starting transfers between devices  27.3 us (43%)
  Pallas kernels  14.9 us (24%)
  blocking collectives  9.32 us (15%)
  waiting for transfers between devices  9.17 us (14%)
  local copies, waits for them, and re-layouts  1.59 us (3%)
  between operations  0.78 us (1%)
    ppermute x10, starting transfers between devices, shift(): lax.ppermute(value, axis, [(i, (i + step) % count) for i in range(count)])  17.7 us
    all_to_all x1, blocking collectives, on_device(): lax.all_to_all(term.reshape(16 * highs, LOW), slab, 0, 0, tiled=True)  9.32 us
    ppermute x10, waiting for transfers between devices, shift(): lax.ppermute(value, axis, [(i, (i + step) % count) for i in range(count)])  8.13 us
    ppermute x3, starting transfers between devices, shift_both(): return lax.ppermute(value, ('gy', 'gz'), pairs)  5.71 us
    all_to_all x1, starting transfers between devices, on_device(): grams = lax.all_to_all(gram, everyone, 0, 0, tiled=True)  3.91 us
    pallas_call x1, Pallas kernels, on_device(): call(factor_kernel, (f32(44, rows_local), f32(44, 44)), (pltpu.VMEM((16,...  2.33 us
    pallas_call x1, Pallas kernels, on_device(): call(old_factor_kernel, (vmem(32, 128), vmem(32, rows_local)), count=2)  2.26 us
    pallas_call x2, Pallas kernels, on_device(): parts.append(part(held(vels[i]), row_map, held(onehot)))  1.67 us
  transfers between devices with their start and end apart: 14, of which 8 were waited for; matrix products, arithmetic and copies ran while one was open for 1% of the time, Pallas kernels for 13%

profile of v3, /device:TPU:0, one launch (start us, length us, event | category | flops | bytes accessed | tf_op | source)
XLA Modules:
  0.0 63.1 jit_solution(4175423251096358727)
XLA Ops:
  0.6 1.3 %shard_map.94 = (f32[19,2,16,128]{3,2,1,0:T(8,128)S(1)}, f32[2,16,128]{2,1,0:T(8,128)S(1)}, f32[3,8,128]{2,1,0:T(8,128)S(1)}, f32[3,8,128]{2,1,0:T(8,128)S(1)}, ...) custom-call(f32[8]{0:T(128)} %table_hbm.1, f32[19,2,16,128]{3,2,1,0:T(8,128)} %ratio_hbm.1, ...), custom_call_target="tpu_custom_call" | custom-call | tf_op jit(solution)/shard_map/pallas_call | solution.py:526
  2.0 3.1 %collective-permute-start.2 = (f32[40,8,128]{2,1,0:T(8,128)S(1)}, f32[40,8,128]{2,1,0:T(8,128)S(1)}, u32[]{:S(2)}, u32[]{:S(2)}) collective-permute-start(f32[40,8,128]{2,1,0:T(8,128)S(1)} %get-tuple-element.43), channel_id=1, source_target_pairs={{0,4},{1,5},{2,6},{3,7},{4,0},{5,1},{6,2},{7,3},{8,12},{9,13},{10,... | collective-permute-start | bytes 491528 | tf_op jit(solution)/shard_map/ppermute | solution.py:506
  5.0 1.7 %collective-permute-start.1 = (f32[3,8,128]{2,1,0:T(8,128)S(1)}, f32[3,8,128]{2,1,0:T(8,128)S(1)}, u32[]{:S(2)}, u32[]{:S(2)}) collective-permute-start(f32[3,8,128]{2,1,0:T(8,128)S(1)} %get-tuple-element.40), channel_id=1, source_target_pairs={{0,3},{1,0},{2,1},{3,2},{4,7},{5,4},{6,5},{7,6},{8,11},{9,8},{10,9... | collective-permute-start | bytes 36872 | tf_op jit(solution)/shard_map/ppermute | solution.py:498
  6.8 2.6 %collective-permute-start.4 = (f32[2,8,128]{2,1,0:T(8,128)S(1)}, f32[2,8,128]{2,1,0:T(8,128)S(1)}, u32[]{:S(2)}, u32[]{:S(2)}) collective-permute-start(f32[2,8,128]{2,1,0:T(8,128)S(1)} %get-tuple-element.45), channel_id=1, source_target_pairs={{0,7},{1,4},{2,5},{3,6},{4,3},{5,0},{6,1},{7,2},{8,15},{9,12},{10,... | collective-permute-start | bytes 24584 | tf_op jit(solution)/shard_map/ppermute | solution.py:506
  9.8 0.9 %collective-permute-done.3.cr = f32[2,8,128]{2,1,0:T(8,128)S(1)} collective-permute-done((f32[2,8,128]{2,1,0:T(8,128)S(1)}, f32[2,8,128]{2,1,0:T(8,128)S(1)}, u32[]{:S(2)}, u32[]{:S(2)}) %collective-permute-start.3) | collective-permute-done | bytes 8224 | tf_op jit(solution)/shard_map/ppermute | solution.py:506
  11.1 1.6 %collective-permute-start.5 = (f32[16,8,128]{2,1,0:T(8,128)S(1)}, f32[16,8,128]{2,1,0:T(8,128)S(1)}, u32[]{:S(2)}, u32[]{:S(2)}) collective-permute-start(f32[16,8,128]{2,1,0:T(8,128)S(1)} %get-tuple-element.48), channel_id=1, source_target_pairs={{0,8},{8,16},{16,24},{24,0},{1,9},{9,17},{17,25},{25,1},{2,10},{10... | collective-permute-start | bytes 196616 | tf_op jit(solution)/shard_map/ppermute | solution.py:498
  12.8 2.2 %collective-permute-start.6 = (f32[16,8,128]{2,1,0:T(8,128)S(1)}, f32[16,8,128]{2,1,0:T(8,128)S(1)}, u32[]{:S(2)}, u32[]{:S(2)}) collective-permute-start(f32[16,8,128]{2,1,0:T(8,128)S(1)} %get-tuple-element.49), channel_id=1, source_target_pairs={{0,24},{8,0},{16,8},{24,16},{1,25},{9,1},{17,9},{25,17},{2,26},{10... | collective-permute-start | bytes 196616 | tf_op jit(solution)/shard_map/ppermute | solution.py:498
  17.5 1.4 %collective-permute-done.6.xl = f32[16,8,128]{2,1,0:T(8,128)S(1)} collective-permute-done((f32[16,8,128]{2,1,0:T(8,128)S(1)}, f32[16,8,128]{2,1,0:T(8,128)S(1)}, u32[]{:S(2)}, u32[]{:S(2)}) %collective-permute-start.6) | collective-permute-done | bytes 65568 | tf_op jit(solution)/shard_map/ppermute | solution.py:498
  19.5 1.0 %collective-permute-start.7 = (f32[17,8,128]{2,1,0:T(8,128)S(1)}, f32[17,8,128]{2,1,0:T(8,128)S(1)}, u32[]{:S(2)}, u32[]{:S(2)}) collective-permute-start(f32[17,8,128]{2,1,0:T(8,128)S(1)} %get-tuple-element.52), channel_id=1, source_target_pairs={{0,8},{8,16},{16,24},{24,0},{1,9},{9,17},{17,25},{25,1},{2,10},{10... | collective-permute-start | bytes 208904 | tf_op jit(solution)/shard_map/ppermute | solution.py:498
  22.1 2.9 %collective-permute-start.8 = (f32[17,8,128]{2,1,0:T(8,128)S(1)}, f32[17,8,128]{2,1,0:T(8,128)S(1)}, u32[]{:S(2)}, u32[]{:S(2)}) collective-permute-start(f32[17,8,128]{2,1,0:T(8,128)S(1)} %get-tuple-element.53), channel_id=1, source_target_pairs={{0,24},{8,0},{16,8},{24,16},{1,25},{9,1},{17,9},{25,17},{2,26},{10... | collective-permute-start | bytes 208904 | tf_op jit(solution)/shard_map/ppermute | solution.py:498
  25.9 1.1 %collective-permute-done.8.xl = f32[17,8,128]{2,1,0:T(8,128)S(1)} collective-permute-done((f32[17,8,128]{2,1,0:T(8,128)S(1)}, f32[17,8,128]{2,1,0:T(8,128)S(1)}, u32[]{:S(2)}, u32[]{:S(2)}) %collective-permute-start.8) | collective-permute-done | bytes 69664 | tf_op jit(solution)/shard_map/ppermute | solution.py:498
  28.5 3.6 %collective-permute-start.10 = (f32[17,8,128]{2,1,0:T(8,128)S(1)}, f32[17,8,128]{2,1,0:T(8,128)S(1)}, u32[]{:S(2)}, u32[]{:S(2)}) collective-permute-start(f32[17,8,128]{2,1,0:T(8,128)S(1)} %get-tuple-element.56), channel_id=1, source_target_pairs={{0,24},{8,0},{16,8},{24,16},{1,25},{9,1},{17,9},{25,17},{2,26},{10... | collective-permute-start | bytes 208904 | tf_op jit(solution)/shard_map/ppermute | solution.py:498
  32.0 0.8 %shard_map.108.early = f32[16,16,256]{2,1,0:T(8,128)S(1)} custom-call(f32[3,2,16,128]{3,2,1,0:T(8,128)S(1)} %get-tuple-element.60.v2, s32[2,16,128]{2,1,0:T(8,128)S(1)} %copy-done, bf16[256,4096]{1,0:T(8,128)(2,1)S(1)} %shard_map.105.right, f32[48,256]{1,0:T(8,128)S(1)} %shard_map.106.part0, f32[48,256]{1,0:T(8,128)S(1)} %shard_map.107.part1), custom_call_target="tpu_custom_call" | custom-call | tf_op jit(solution)/shard_map/pallas_call | solution.py:596
  32.9 1.7 %collective-permute-done.9.xr = f32[17,8,128]{2,1,0:T(8,128)S(1)} collective-permute-done((f32[17,8,128]{2,1,0:T(8,128)S(1)}, f32[17,8,128]{2,1,0:T(8,128)S(1)}, u32[]{:S(2)}, u32[]{:S(2)}) %collective-permute-start.9) | collective-permute-done | bytes 69664 | tf_op jit(solution)/shard_map/ppermute | solution.py:498
  34.6 0.9 %shard_map.109 = f32[16,16,256]{2,1,0:T(8,128)S(1)} custom-call(f32[19,2,24,256]{3,2,1,0:T(8,128)S(1)} %shard_map.102.ahead, f32[2,24,256]{2,1,0:T(8,128)S(1)} %get-tuple-element.47.g_ref, f32[17,8,128]{2,1,0:T(8,128)S(1)} %collective-permute-done.9.xr, f32[17,8,128]{2,1,0:T(8,128)S(1)} %collective-permute-done.10.xl, s32[2,16,128]{2,1,0:T(8,128)S(1)} %copy-done, ...), custom_call_target="tpu_custom_call" | custom-call | tf_op jit(solution)/shard_map/pallas_call | solution.py:603
  35.6 9.3 %all_to_all.22 = f32[8,32,256]{2,1,0:T(8,128)S(1)} all-to-all(f32[8,32,256]{2,1,0:T(8,128)S(1)} %bitcast.11), channel_id=1, replica_groups=mesh['gx'=4,'gy'=2,'gz'=4] {'gy','gz'}, dimensions={0} | all-to-all | bytes 524288 | tf_op jit(solution)/shard_map/all_to_all | solution.py:610
  44.9 0.9 %shard_map.110 = (f32[16,512]{1,0:T(8,128)S(1)}, f32[8,128]{1,0:T(8,128)S(1)}, f32[128,128]{1,0:T(8,128)}) custom-call(f32[256,256]{1,0:T(8,128)S(1)} %bitcast.12, f32[32,512]{1,0:T(8,128)S(1)} %get-tuple-element.63.scaled), custom_call_target="tpu_custom_call" | custom-call | tf_op jit(solution)/shard_map/pallas_call | solution.py:611
  45.8 3.9 %all-to-all-start.1 = ((f32[32,4,128]{2,1,0:T(4,128)}), f32[32,4,128]{2,1,0:T(4,128)S(1)}, u32[]{:S(2)}, u32[]{:S(2)}) async-start(f32[32,4,128]{2,1,0:T(4,128)} %bitcast.6), calls=%async_computation.1 | async-start | bytes 131072 | tf_op jit(solution)/shard_map/all_to_all | solution.py:617
  50.2 1.8 %collective-permute-start.11 = (f32[16,8,128]{2,1,0:T(8,128)S(1)}, f32[16,8,128]{2,1,0:T(8,128)S(1)}, u32[]{:S(2)}, u32[]{:S(2)}) collective-permute-start(f32[16,8,128]{2,1,0:T(8,128)S(1)} %get-tuple-element.58), channel_id=1, source_target_pairs={{0,8},{8,16},{16,24},{24,0},{1,9},{9,17},{17,25},{25,1},{2,10},{10... | collective-permute-start | bytes 196616 | tf_op jit(solution)/shard_map/ppermute | solution.py:498
  52.1 2.1 %collective-permute-start.12 = (f32[16,8,128]{2,1,0:T(8,128)S(1)}, f32[16,8,128]{2,1,0:T(8,128)S(1)}, u32[]{:S(2)}, u32[]{:S(2)}) collective-permute-start(f32[16,8,128]{2,1,0:T(8,128)S(1)} %get-tuple-element.59), channel_id=1, source_target_pairs={{0,24},{8,0},{16,8},{24,16},{1,25},{9,1},{17,9},{25,17},{2,26},{10... | collective-permute-start | bytes 196616 | tf_op jit(solution)/shard_map/ppermute | solution.py:498
  54.1 3.3 %collective-permute-done.11.xr = f32[16,8,128]{2,1,0:T(8,128)S(1)} collective-permute-done((f32[16,8,128]{2,1,0:T(8,128)S(1)}, f32[16,8,128]{2,1,0:T(8,128)S(1)}, u32[]{:S(2)}, u32[]{:S(2)}) %collective-permute-start.11) | collective-permute-done | bytes 65568 | tf_op jit(solution)/shard_map/ppermute | solution.py:498
  57.6 0.9 %shard_map.104 = f32[19,2,16,128]{3,2,1,0:T(8,128)} custom-call(f32[19,2,24,256]{3,2,1,0:T(8,128)S(1)} %get-tuple-element.57.prev, f32[16,8,128]{2,1,0:T(8,128)S(1)} %collective-permute-done.11.xr, f32[16,8,128]{2,1,0:T(8,128)S(1)} %collective-permute-done.12.xl), custom_call_target="tpu_custom_call" | custom-call | tf_op jit(solution)/shard_map/pallas_call | solution.py:622
  58.5 2.3 %shard_map.111 = (f32[32,128]{1,0:T(8,128)S(1)}, f32[32,512]{1,0:T(8,128)S(1)}) custom-call(f32[8,128]{1,0:T(8,128)S(1)} %get-tuple-element.65.tile, f32[32,512]{1,0:T(8,128)S(1)} %get-tuple-element.63.scaled), custom_call_target="tpu_custom_call" | custom-call | tf_op jit(solution)/shard_map/pallas_call | solution.py:618
  60.8 2.3 %shard_map.112 = (f32[44,512]{1,0:T(8,128)}, f32[44,44]{1,0:T(8,128)}) custom-call(f32[128,128]{1,0:T(8,128)S(1)} %bitcast.13, f32[32,128]{1,0:T(8,128)S(1)} %get-tuple-element.66.factor, f32[32,512]{1,0:T(8,128)S(1)} %get-tuple-element.67.head, f32[16,512]{1,0:T(8,128)S(1)} %get-tuple-element.68.snap), custom_call_target="tpu_custom_call" | custom-call | tf_op jit(solution)/shard_map/pallas_call | solution.py:619
  (33 shorter events, 8.5 us)
Async XLA Ops:
  2.0 8.9 %collective-permute-start.2 = (f32[40,8,128]{2,1,0:T(8,128)S(1)}, f32[40,8,128]{2,1,0:T(8,128)S(1)}, u32[]{:S(2)}, u32[]{:S(2)}) collective-permute-start(f32[40,8,128]{2,1,0:T(8,128)S(1)} %get-tuple-element.43), channel_id=1, source_target_pairs={{0,4},{1,5},{2,6},{3,7},{4,0},{5,1},{6,2},{7,3},{8,12},{9,13},{10,... | collective-permute-start | bytes 491528 | tf_op jit(solution)/shard_map/ppermute | solution.py:506
  5.0 4.4 %collective-permute-start = (f32[3,8,128]{2,1,0:T(8,128)S(1)}, f32[3,8,128]{2,1,0:T(8,128)S(1)}, u32[]{:S(2)}, u32[]{:S(2)}) collective-permute-start(f32[3,8,128]{2,1,0:T(8,128)S(1)} %get-tuple-element.39), channel_id=1, source_target_pairs={{0,1},{1,2},{2,3},{3,0},{4,5},{5,6},{6,7},{7,4},{8,9},{9,10},{10,1... | collective-permute-start | bytes 36872 | tf_op jit(solution)/shard_map/ppermute | solution.py:498
  5.0 4.4 %collective-permute-start.1 = (f32[3,8,128]{2,1,0:T(8,128)S(1)}, f32[3,8,128]{2,1,0:T(8,128)S(1)}, u32[]{:S(2)}, u32[]{:S(2)}) collective-permute-start(f32[3,8,128]{2,1,0:T(8,128)S(1)} %get-tuple-element.40), channel_id=1, source_target_pairs={{0,3},{1,0},{2,1},{3,2},{4,7},{5,4},{6,5},{7,6},{8,11},{9,8},{10,9... | collective-permute-start | bytes 36872 | tf_op jit(solution)/shard_map/ppermute | solution.py:498
  6.8 4.0 %collective-permute-start.3 = (f32[2,8,128]{2,1,0:T(8,128)S(1)}, f32[2,8,128]{2,1,0:T(8,128)S(1)}, u32[]{:S(2)}, u32[]{:S(2)}) collective-permute-start(f32[2,8,128]{2,1,0:T(8,128)S(1)} %get-tuple-element.44), channel_id=1, source_target_pairs={{0,5},{1,6},{2,7},{3,4},{4,1},{5,2},{6,3},{7,0},{8,13},{9,14},{10,... | collective-permute-start | bytes 24584 | tf_op jit(solution)/shard_map/ppermute | solution.py:506
  6.8 4.1 %collective-permute-start.4 = (f32[2,8,128]{2,1,0:T(8,128)S(1)}, f32[2,8,128]{2,1,0:T(8,128)S(1)}, u32[]{:S(2)}, u32[]{:S(2)}) collective-permute-start(f32[2,8,128]{2,1,0:T(8,128)S(1)} %get-tuple-element.45), channel_id=1, source_target_pairs={{0,7},{1,4},{2,5},{3,6},{4,3},{5,0},{6,1},{7,2},{8,15},{9,12},{10,... | collective-permute-start | bytes 24584 | tf_op jit(solution)/shard_map/ppermute | solution.py:506
  10.8 9.6 %copy-start = (s32[2,16,128]{2,1,0:T(8,128)S(1)}, s32[2,16,128]{2,1,0:T(8,128)}, u32[]{:S(2)}) copy-start(s32[2,16,128]{2,1,0:T(8,128)} %row_map.9) | copy-start | bytes 49156
  11.1 6.4 %collective-permute-start.5 = (f32[16,8,128]{2,1,0:T(8,128)S(1)}, f32[16,8,128]{2,1,0:T(8,128)S(1)}, u32[]{:S(2)}, u32[]{:S(2)}) collective-permute-start(f32[16,8,128]{2,1,0:T(8,128)S(1)} %get-tuple-element.48), channel_id=1, source_target_pairs={{0,8},{8,16},{16,24},{24,0},{1,9},{9,17},{17,25},{25,1},{2,10},{10... | collective-permute-start | bytes 196616 | tf_op jit(solution)/shard_map/ppermute | solution.py:498
  12.8 6.2 %collective-permute-start.6 = (f32[16,8,128]{2,1,0:T(8,128)S(1)}, f32[16,8,128]{2,1,0:T(8,128)S(1)}, u32[]{:S(2)}, u32[]{:S(2)}) collective-permute-start(f32[16,8,128]{2,1,0:T(8,128)S(1)} %get-tuple-element.49), channel_id=1, source_target_pairs={{0,24},{8,0},{16,8},{24,16},{1,25},{9,1},{17,9},{25,17},{2,26},{10... | collective-permute-start | bytes 196616 | tf_op jit(solution)/shard_map/ppermute | solution.py:498
  15.7 0.8 %copy-start.1 = (f32[32,512]{1,0:T(8,128)S(1)}, f32[32,512]{1,0:T(8,128)}, u32[]{:S(2)}) copy-start(f32[32,512]{1,0:T(8,128)} %basis.1) | copy-start | bytes 196612
  19.5 6.4 %collective-permute-start.7 = (f32[17,8,128]{2,1,0:T(8,128)S(1)}, f32[17,8,128]{2,1,0:T(8,128)S(1)}, u32[]{:S(2)}, u32[]{:S(2)}) collective-permute-start(f32[17,8,128]{2,1,0:T(8,128)S(1)} %get-tuple-element.52), channel_id=1, source_target_pairs={{0,8},{8,16},{16,24},{24,0},{1,9},{9,17},{17,25},{25,1},{2,10},{10... | collective-permute-start | bytes 208904 | tf_op jit(solution)/shard_map/ppermute | solution.py:498
  22.1 4.9 %collective-permute-start.8 = (f32[17,8,128]{2,1,0:T(8,128)S(1)}, f32[17,8,128]{2,1,0:T(8,128)S(1)}, u32[]{:S(2)}, u32[]{:S(2)}) collective-permute-start(f32[17,8,128]{2,1,0:T(8,128)S(1)} %get-tuple-element.53), channel_id=1, source_target_pairs={{0,24},{8,0},{16,8},{24,16},{1,25},{9,1},{17,9},{25,17},{2,26},{10... | collective-permute-start | bytes 208904 | tf_op jit(solution)/shard_map/ppermute | solution.py:498
  27.6 7.0 %collective-permute-start.9 = (f32[17,8,128]{2,1,0:T(8,128)S(1)}, f32[17,8,128]{2,1,0:T(8,128)S(1)}, u32[]{:S(2)}, u32[]{:S(2)}) collective-permute-start(f32[17,8,128]{2,1,0:T(8,128)S(1)} %get-tuple-element.55), channel_id=1, source_target_pairs={{0,8},{8,16},{16,24},{24,0},{1,9},{9,17},{17,25},{25,1},{2,10},{10... | collective-permute-start | bytes 208904 | tf_op jit(solution)/shard_map/ppermute | solution.py:498
  28.5 6.1 %collective-permute-start.10 = (f32[17,8,128]{2,1,0:T(8,128)S(1)}, f32[17,8,128]{2,1,0:T(8,128)S(1)}, u32[]{:S(2)}, u32[]{:S(2)}) collective-permute-start(f32[17,8,128]{2,1,0:T(8,128)S(1)} %get-tuple-element.56), channel_id=1, source_target_pairs={{0,24},{8,0},{16,8},{24,16},{1,25},{9,1},{17,9},{25,17},{2,26},{10... | collective-permute-start | bytes 208904 | tf_op jit(solution)/shard_map/ppermute | solution.py:498
  45.8 15.0 %all-to-all-start.1 = ((f32[32,4,128]{2,1,0:T(4,128)}), f32[32,4,128]{2,1,0:T(4,128)S(1)}, u32[]{:S(2)}, u32[]{:S(2)}) async-start(f32[32,4,128]{2,1,0:T(4,128)} %bitcast.6), calls=%async_computation.1 | async-start | bytes 131072 | tf_op jit(solution)/shard_map/all_to_all | solution.py:617
  50.2 7.1 %collective-permute-start.11 = (f32[16,8,128]{2,1,0:T(8,128)S(1)}, f32[16,8,128]{2,1,0:T(8,128)S(1)}, u32[]{:S(2)}, u32[]{:S(2)}) collective-permute-start(f32[16,8,128]{2,1,0:T(8,128)S(1)} %get-tuple-element.58), channel_id=1, source_target_pairs={{0,8},{8,16},{16,24},{24,0},{1,9},{9,17},{17,25},{25,1},{2,10},{10... | collective-permute-start | bytes 196616 | tf_op jit(solution)/shard_map/ppermute | solution.py:498
  52.1 5.6 %collective-permute-start.12 = (f32[16,8,128]{2,1,0:T(8,128)S(1)}, f32[16,8,128]{2,1,0:T(8,128)S(1)}, u32[]{:S(2)}, u32[]{:S(2)}) collective-permute-start(f32[16,8,128]{2,1,0:T(8,128)S(1)} %get-tuple-element.59), channel_id=1, source_target_pairs={{0,24},{8,0},{16,8},{24,16},{1,25},{9,1},{17,9},{25,17},{2,26},{10... | collective-permute-start | bytes 196616 | tf_op jit(solution)/shard_map/ppermute | solution.py:498

commit v4 on v3

--- a/solution.py
+++ b/solution.py
@@ -9,7 +9,6 @@
 from jax.sharding import PartitionSpec as P
 
 
-STEPS = 4
 VOX_ROW = 8
 LATTICE = np.array(
     [
@@ -183,6 +182,107 @@
         ref[15] = extra
 
 
+STILL = [q for q in range(19) if LATTICE[q, 0] == 0]
+DEEP = 14
+DEEP_TILES = 38
+
+
+def still_sums(pops):
+    total = pops[0]
+    for value in pops[1:]:
+        total = total + value
+    sums = [total]
+    for a in (1, 2):
+        plus = [p for p, q in zip(pops, STILL) if LATTICE[q, a] == 1]
+        minus = [p for p, q in zip(pops, STILL) if LATTICE[q, a] == -1]
+        sums.append(((plus[0] + plus[1]) + plus[2]) - ((minus[0] + minus[1]) + minus[2]))
+    return sums
+
+
+def pack_deep(ahead, going, g_ref, refs):
+    lane, sub = lanes(), subs()
+    for side, ref in enumerate(refs):
+        x = 1 - side
+        edges = [jnp.zeros((8, 128), jnp.float32)] * 3
+        directions = (PLUS_X, MINUS_X)[side]
+
+        def entries(yt, lt):
+            at = (pl.ds(8 * yt, 8), pl.ds(128 * lt, 128))
+            tiles = [going[side, i, at[0], at[1]] for i in range(5)]
+            tiles += [ahead[q, x, at[0], at[1]] for q in directions]
+            tiles += still_sums([ahead[q, x, at[0], at[1]] for q in STILL])
+            return tiles + [g_ref[x, at[0], at[1]]]
+
+        def edge(j, tile):
+            at, k = divmod(j, 16)
+            here = (lane >= 8 * k) & (lane < 8 * k + 8)
+            edges[at] = jnp.where(here, roll(tile, 4 + 8 * k, 1), edges[at])
+
+        for yt in range(2):
+            for e, (inner, outer) in enumerate(zip(entries(yt, 0), entries(yt, 1))):
+                ref[2 * e + yt] = inner
+                edge(2 * e + yt, outer)
+        halos = [entries(2, lt) for lt in range(2)]
+        for e in range(0, DEEP, 2):
+            pair = [jnp.where(sub < 4, roll(h[e], 2, 0), roll(h[e + 1], 6, 0)) for h in halos]
+            ref[28 + e // 2] = pair[0]
+            edge(28 + e // 2, pair[1])
+        for at in range(3):
+            ref[35 + at] = edges[at]
+
+
+def take_deep(refs, deep):
+    for side, ref in enumerate(refs):
+
+        def edge(j):
+            return roll(ref[35 + j // 16], -(8 * (j % 16) + 4), 1)
+
+        for e in range(DEEP):
+            back = -2 if e % 2 == 0 else -6
+            for yt in range(2):
+                deep[side, e, pl.ds(8 * yt, 8), pl.ds(0, 128)] = ref[2 * e + yt]
+                deep[side, e, pl.ds(8 * yt, 8), pl.ds(128, 128)] = edge(2 * e + yt)
+            deep[side, e, pl.ds(16, 8), pl.ds(0, 128)] = roll(ref[28 + e // 2], back, 0)
+            deep[side, e, pl.ds(16, 8), pl.ds(128, 128)] = roll(edge(28 + e // 2), back, 0)
+
+
+def collide_side(toward, away, sums, g, side):
+    ahead, back = ((PLUS_X, MINUS_X), (MINUS_X, PLUS_X))[side]
+    into, out_of = toward[0], away[0]
+    for value in toward[1:]:
+        into = into + value
+    for value in away[1:]:
+        out_of = out_of + value
+    density = sums[0] + (into + out_of)
+    flows = [into - out_of if side == 0 else out_of - into, sums[1], sums[2]]
+    for directions, pops in ((ahead, toward), (back, away)):
+        for q, value in zip(directions, pops):
+            for a in (1, 2):
+                if LATTICE[q, a] == 1:
+                    flows[a] = flows[a] + value
+                elif LATTICE[q, a] == -1:
+                    flows[a] = flows[a] - value
+    scale = 1.0 / (density * jnp.abs(g))
+    speeds = [flow * scale for flow in flows]
+    square = speeds[0] * speeds[0] + speeds[1] * speeds[1] + speeds[2] * speeds[2]
+    keep = 1.0 - 1.0 / relax_time
+    base = 1.0 - 1.5 * square
+    solid = g < 0.0
+    part = {w: density * (w / relax_time) for w in sorted({WEIGHTS[q] for q in ahead})}
+    relaxed = []
+    for q, value in zip(ahead, toward):
+        along = None
+        for a in range(3):
+            c = LATTICE[q, a]
+            if c == 1:
+                along = speeds[a] if along is None else along + speeds[a]
+            elif c == -1:
+                along = -speeds[a] if along is None else along - speeds[a]
+        moved = value * keep + part[WEIGHTS[q]] * ((base + 4.5 * along * along) + 3.0 * along)
+        relaxed.append(jnp.where(solid, away[back.index(OPPOSITE[q])], moved))
+    return relaxed
+
+
 def inner_kernel(pops, g_in, left, right, out, g_ref, vel_ref, wide):
     lane = lanes()
     for f in range(FIELDS):
@@ -260,16 +360,42 @@
     return pick
 
 
-def step_kernel(ahead, g_ref, xr, xl, rider_r, rider_l, out, vel_ref, xr_ref, xl_ref, side):
+def step_kernel(ahead_in, g_ref, xr, xl, rider, ahead, going, vel_ref, xr_ref, xl_ref, side, out):
     take_faces(xr, xl, side)
-    collide_all(chooser(ahead, side), g_ref, out, vel_ref)
-    pack_x(out, xr_ref, xl_ref)
-    xr_ref[16] = rider_r[...]
-    xl_ref[16] = rider_l[...]
-
-
-def end_step_kernel(ahead, g_ref, xr, xl, out, xr_ref, xl_ref, side):
-    take_faces(xr, xl, side)
+    collide_all(chooser(ahead_in, side), g_ref, out, vel_ref)
+    local_kernel(out, ahead)
+    for i in range(5):
+        going[0, i] = turned(out[PLUS_X[i], 1], PLUS_X[i])
+        going[1, i] = turned(out[MINUS_X[i], 0], MINUS_X[i])
+    pack_deep(ahead, going, g_ref, (xr_ref, xl_ref))
+    xr_ref[DEEP_TILES] = rider[...]
+    xl_ref[DEEP_TILES] = rider[...]
+
+
+def pair_kernel(ahead, going, g_ref, xr, xl, ahead_ref, side_ref, vel_ref, deep, out):
+    take_deep((xr, xl), deep)
+
+    def pick(q, x, rows, cols):
+        at = remote(q, x)
+        return ahead[q, x, rows, cols] if at is None else deep[at[0], at[1], rows, cols]
+
+    collide_all(pick, g_ref, out, vel_ref)
+    for side, directions in enumerate((PLUS_X, MINUS_X)):
+        for yt in range(3):
+            for lt in range(2):
+                rows, cols = pl.ds(8 * yt, 8), pl.ds(128 * lt, 128)
+                toward = [deep[side, 5 + i, rows, cols] for i in range(5)]
+                away = [going[1 - side, i, rows, cols] for i in range(5)]
+                sums = [deep[side, 10 + i, rows, cols] for i in range(3)]
+                relaxed = collide_side(toward, away, sums, deep[side, 13, rows, cols], side)
+                for i in range(5):
+                    side_ref[side, i, rows, cols] = relaxed[i]
+        for i, q in enumerate(directions):
+            side_ref[side, i] = turned(side_ref[side, i], q)
+    local_kernel(out, ahead_ref)
+
+
+def end_step_kernel(ahead, g_ref, side, out, xr_ref, xl_ref):
     collide_all(chooser(ahead, side), g_ref, out, None)
     pack_x(out, xr_ref, xl_ref)
 
@@ -304,33 +430,29 @@
     )
 
 
-def restricted(v, row_map, right, left):
-    highs = left.shape[0] // 6
+def restricted(vels, row_map, right, left):
+    count = 3 * len(vels)
+    highs = left.shape[0] // (2 * count)
     high_at = lax.broadcasted_iota(jnp.int32, (highs, 128), 0)
     for x in range(2):
         for y in range(16):
             cols = pl.ds(128 * (16 * x + y), 128)
             here = high_at == row_map[x, pl.ds(y, 1), :] // LOW
-            for a in range(3):
-                for i, part in enumerate(split(v[a, x, pl.ds(y, 1), :])):
-                    left[pl.ds(highs * (3 * i + a), highs), cols] = jnp.where(here, part, 0.0).astype(jnp.bfloat16)
+            for j in range(count):
+                for i, part in enumerate(split(vels[j // 3][j % 3, x, pl.ds(y, 1), :])):
+                    left[pl.ds(highs * (count * i + j), highs), cols] = jnp.where(here, part, 0.0).astype(jnp.bfloat16)
     both = times_onehot(left, right)
-    half = 3 * highs
+    half = count * highs
     return both[:half] + both[half:]
 
 
-def part_kernel(v, row_map, right, out, left):
-    out[...] = restricted(v, row_map, right, left)
-
-
-def early_kernel(v2, row_map, right, part0, part1, out, left):
+def early_kernel(v0, v1, row_map, right, out, left):
     highs = out.shape[0]
-    parts = (part0[...], part1[...], restricted(v2, row_map, right, left))
+    both = restricted((v0, v1), row_map, right, left)
     for h in range(highs):
-        for s, part in enumerate(parts):
-            for a in range(3):
-                out[h, pl.ds(3 * s + a, 1), :] = part[highs * a + h : highs * a + h + 1]
-        out[h, pl.ds(9, 7), :] = jnp.zeros((7, LOW), jnp.float32)
+        for j in range(6):
+            out[h, pl.ds(j, 1), :] = both[highs * j + h : highs * j + h + 1]
+        out[h, pl.ds(6, 10), :] = jnp.zeros((10, LOW), jnp.float32)
 
 
 def old_kernel(total_rows, basis, sigma, scaled_ref, tile_ref, work):
@@ -356,8 +478,7 @@
     )
 
 
-def late_kernel(ahead, g_ref, xr, xl, row_map, right, early, own, near_r, near_l, far, out, left, side, v3):
-    take_faces(xr, xl, side)
+def late_kernel(ahead, g_ref, side, v2, row_map, right, early, own, near_r, near_l, far, out, left, v3):
     pick = chooser(ahead, side)
     for x in range(2):
         for yt in range(2):
@@ -368,12 +489,12 @@
             for a in range(3):
                 v3[a, x, rows, :] = speeds[a] * factor
     highs = out.shape[0]
-    both = restricted(v3, row_map, right, left)
+    both = restricted((v2, v3), row_map, right, left)
     out[...] = early[...]
     old = (own[...] + far[...]) + (near_r[...] + near_l[...])
     for h in range(highs):
-        for a in range(3):
-            out[h, pl.ds(9 + a, 1), :] = both[highs * a + h : highs * a + h + 1]
+        for j in range(6):
+            out[h, pl.ds(6 + j, 1), :] = both[highs * j + h : highs * j + h + 1]
         if h % 2 == 0:
             out[h, pl.ds(12, 4), pl.ds(0, 128)] = old[:4]
             out[h, pl.ds(12, 4), pl.ds(128, 128)] = old[4:]
@@ -544,14 +665,13 @@
     wide = pltpu.VMEM((19, 2, 24, 256), jnp.float32)
     side = pltpu.VMEM((2, 5, 24, 256), jnp.float32)
     big, wall, vel, face = vmem(19, 2, 24, 256), vmem(2, 24, 256), vmem(3, 2, 16, 128), vmem(16, *tile)
-    loaded = vmem(17, *tile)
+    loaded, sides = vmem(DEEP_TILES + 1, *tile), vmem(2, 5, 24, 256)
     relaxed, g_wide, v0 = call(inner_kernel, (big, wall, vel), (wide,), count=4)(
         *map(held, (pops, g, left, right))
     )
     relaxed, g_wide, xr, xl = call(
         outer_kernel, (big, wall, face, face), (wide,), count=5, aliases={0: 0, 1: 1}
     )(*map(held, (relaxed, g_wide, y, cr, cl)))
-    vels = [v0]
     old, own = call(
         functools.partial(old_kernel, float(rows_local * devices)),
         (vmem(32, rows_local), vmem(*tile)),
@@ -562,51 +682,34 @@
     if not ring:
         own = lax.psum(own, "gx")
     none = jnp.zeros(tile, jnp.float32)
-    step = jax.jit(call(step_kernel, (big, vel, loaded, loaded), (side,), count=6))
-    local = jax.jit(call(local_kernel, big, count=1))
     onehot = call(onehot_kernel, pltpu.VMEM((LOW, cells), jnp.bfloat16), count=1)(row_map)
-    riders, got = (own, own), [none] * 3
-    for s in range(1, STEPS):
-        xr, xl = shift(xr, "gx", 1), shift(xl, "gx", -1)
-        if s == 2 and ring:
-            got[0], got[1] = xr[16], xl[16]
-            riders = (xr[16], none)
-        if s == 3 and ring:
-            got[2] = xr[16]
-        ahead = local(held(relaxed))
-        if s < 3:
-            relaxed, vel_s, xr, xl = step(*map(held, (ahead, g_wide, xr, xl, *riders)))
-            vels.append(vel_s)
-    state = tuple(map(held, (ahead, g_wide, xr, xl)))
-    relaxed, xr, xl = call(end_step_kernel, (big, face, face), (side,), count=4)(*state)
     xr, xl = shift(xr, "gx", 1), shift(xl, "gx", -1)
-
-    part = jax.jit(
-        call(
-            part_kernel,
-            vmem(3 * highs, LOW),
-            (pltpu.VMEM((6 * highs, cells), jnp.bfloat16),),
-            count=3,
-            limit=8 + highs // 2,
-        )
+    ahead = call(local_kernel, big, count=1)(held(relaxed))
+    ahead, going, v1, xr, xl = call(step_kernel, (big, sides, vel, loaded, loaded), (side, wide), count=5)(
+        *map(held, (ahead, g_wide, xr, xl, own))
     )
-    parts = []
-    for i in range(2):
-        parts.append(part(held(vels[i]), row_map, held(onehot)))
-    early = call(
-        early_kernel,
-        vmem(highs, 16, LOW),
-        (pltpu.VMEM((6 * highs, cells), jnp.bfloat16),),
-        count=5,
-        limit=8 + highs // 2,
-    )(held(vels[2]), row_map, *map(held, (onehot, *parts)))
+    xr, xl = shift(xr, "gx", 1), shift(xl, "gx", -1)
+    got = [none] * 3
+    if ring:
+        got = [xr[DEEP_TILES], xl[DEEP_TILES], shift(own, "gx", 2)]
+    ahead, faces, v2 = call(
+        pair_kernel, (big, sides, vel), (pltpu.VMEM((2, DEEP, 24, 256), jnp.float32), wide), count=5
+    )(*map(held, (ahead, going, g_wide, xr, xl)))
+    state = tuple(map(held, (ahead, g_wide, faces)))
+    relaxed, xr, xl = call(end_step_kernel, (big, face, face), count=3)(*state)
+    xr, xl = shift(xr, "gx", 1), shift(xl, "gx", -1)
+
+    lefts = pltpu.VMEM((12 * highs, cells), jnp.bfloat16)
+    early = call(early_kernel, vmem(highs, 16, LOW), (lefts,), count=4, limit=12 + highs // 2)(
+        held(v0), held(v1), row_map, held(onehot)
+    )
     term = call(
         late_kernel,
         f32(highs, 16, LOW),
-        (pltpu.VMEM((6 * highs, cells), jnp.bfloat16), side, pltpu.VMEM((3, 2, 16, 128), jnp.float32)),
+        (lefts, pltpu.VMEM((3, 2, 16, 128), jnp.float32)),
         count=11,
-        limit=8 + highs // 2,
-    )(*state, row_map, *map(held, (onehot, early, own, *got)))
+        limit=12 + highs // 2,
+    )(*state, held(v2), row_map, *map(held, (onehot, early, own, *got)))
     parts = lax.all_to_all(term.reshape(16 * highs, LOW), slab, 0, 0, tiled=True)
     snap, old_tile, gram = call(
         functools.partial(gram_kernel, float(rows_local * devices)),

time: 63.4 us -> 59.2 us (0.934)
  starting transfers between devices: 27.3 us -> 22 us
  waiting for transfers between devices: 9.17 us -> 12 us
  Pallas kernels: 14.9 us -> 13.3 us
    ppermute x10 -> x9, starting transfers between devices: 17.7 us -> 13.7 us  [shift(): lax.ppermute(value, axis, [(i, (i + step) % count) for i in range(count)])]
    ppermute x10 -> x9, waiting for transfers between devices: 8.13 us -> 10.9 us  [shift(): lax.ppermute(value, axis, [(i, (i + step) % count) for i in range(count)])]
    pallas_call x10 -> x6, Pallas kernels: 5.58 us -> 3.95 us  [the longest x1 1.12 us: on_device(): call(late_kernel, f32(highs, 16, LOW), (lefts, pltpu.VMEM((3, 2, 16, 128)...]
    all_to_all x1, starting transfers between devices: 3.91 us -> 2.57 us  [on_device(): grams = lax.all_to_all(gram, everyone, 0, 0, tiled=True)]
  transfers between devices with their start and end apart: 14 -> 13, of which waited for: 8 -> 8; matrix products, arithmetic and copies ran while one was open for 1% -> 1% of each run, Pallas kernels for 13% -> 11%
where the time goes in v4:
time: 59.2 us; the launch traced here: 58.9 us
  starting transfers between devices  22 us (37%)
  Pallas kernels  13.3 us (22%)
  waiting for transfers between devices  12 us (20%)
  blocking collectives  9.32 us (16%)
  local copies, waits for them, and re-layouts  1.58 us (3%)
  between operations  0.75 us (1%)
    ppermute x9, starting transfers between devices, shift(): lax.ppermute(value, axis, [(i, (i + step) % count) for i in range(count)])  13.7 us
    ppermute x9, waiting for transfers between devices, shift(): lax.ppermute(value, axis, [(i, (i + step) % count) for i in range(count)])  10.9 us
    all_to_all x1, blocking collectives, on_device(): lax.all_to_all(term.reshape(16 * highs, LOW), slab, 0, 0, tiled=True)  9.32 us
    ppermute x3, starting transfers between devices, shift_both(): return lax.ppermute(value, ('gy', 'gz'), pairs)  5.71 us
    all_to_all x1, starting transfers between devices, on_device(): grams = lax.all_to_all(gram, everyone, 0, 0, tiled=True)  2.57 us
    pallas_call x1, Pallas kernels, on_device(): call(factor_kernel, (f32(44, rows_local), f32(44, 44)), (pltpu.VMEM((16,...  2.34 us
    pallas_call x1, Pallas kernels, on_device(): call(old_factor_kernel, (vmem(32, 128), vmem(32, rows_local)), count=2)  2.26 us
    pallas_call x1, Pallas kernels, on_device(): call(init_kernel, (vmem(19, 2, 16, 128), vmem(2, 16, 128), vmem(3, *tile)...  1.34 us
  transfers between devices with their start and end apart: 13, of which 8 were waited for; matrix products, arithmetic and copies ran while one was open for 1% of the time, Pallas kernels for 11%

profile of v4, /device:TPU:0, one launch (start us, length us, event | category | flops | bytes accessed | tf_op | source)
XLA Modules:
  0.0 58.9 jit_solution(6116882235937411154)
XLA Ops:
  0.6 1.3 %shard_map.94 = (f32[19,2,16,128]{3,2,1,0:T(8,128)S(1)}, f32[2,16,128]{2,1,0:T(8,128)S(1)}, f32[3,8,128]{2,1,0:T(8,128)S(1)}, f32[3,8,128]{2,1,0:T(8,128)S(1)}, ...) custom-call(f32[8]{0:T(128)} %table_hbm.1, f32[19,2,16,128]{3,2,1,0:T(8,128)} %ratio_hbm.1, ...), custom_call_target="tpu_custom_call" | custom-call | tf_op jit(solution)/shard_map/pallas_call | solution.py:647
  2.0 3.1 %collective-permute-start.2 = (f32[40,8,128]{2,1,0:T(8,128)S(1)}, f32[40,8,128]{2,1,0:T(8,128)S(1)}, u32[]{:S(2)}, u32[]{:S(2)}) collective-permute-start(f32[40,8,128]{2,1,0:T(8,128)S(1)} %get-tuple-element.43), channel_id=1, source_target_pairs={{0,4},{1,5},{2,6},{3,7},{4,0},{5,1},{6,2},{7,3},{8,12},{9,13},{10,... | collective-permute-start | bytes 491528 | tf_op jit(solution)/shard_map/ppermute | solution.py:627
  5.0 1.7 %collective-permute-start.1 = (f32[3,8,128]{2,1,0:T(8,128)S(1)}, f32[3,8,128]{2,1,0:T(8,128)S(1)}, u32[]{:S(2)}, u32[]{:S(2)}) collective-permute-start(f32[3,8,128]{2,1,0:T(8,128)S(1)} %get-tuple-element.40), channel_id=1, source_target_pairs={{0,3},{1,0},{2,1},{3,2},{4,7},{5,4},{6,5},{7,6},{8,11},{9,8},{10,9... | collective-permute-start | bytes 36872 | tf_op jit(solution)/shard_map/ppermute | solution.py:619
  6.8 2.6 %collective-permute-start.4 = (f32[2,8,128]{2,1,0:T(8,128)S(1)}, f32[2,8,128]{2,1,0:T(8,128)S(1)}, u32[]{:S(2)}, u32[]{:S(2)}) collective-permute-start(f32[2,8,128]{2,1,0:T(8,128)S(1)} %get-tuple-element.45), channel_id=1, source_target_pairs={{0,7},{1,4},{2,5},{3,6},{4,3},{5,0},{6,1},{7,2},{8,15},{9,12},{10,... | collective-permute-start | bytes 24584 | tf_op jit(solution)/shard_map/ppermute | solution.py:627
  9.8 0.9 %collective-permute-done.3.cr = f32[2,8,128]{2,1,0:T(8,128)S(1)} collective-permute-done((f32[2,8,128]{2,1,0:T(8,128)S(1)}, f32[2,8,128]{2,1,0:T(8,128)S(1)}, u32[]{:S(2)}, u32[]{:S(2)}) %collective-permute-start.3) | collective-permute-done | bytes 8224 | tf_op jit(solution)/shard_map/ppermute | solution.py:627
  11.1 1.6 %collective-permute-start.5 = (f32[16,8,128]{2,1,0:T(8,128)S(1)}, f32[16,8,128]{2,1,0:T(8,128)S(1)}, u32[]{:S(2)}, u32[]{:S(2)}) collective-permute-start(f32[16,8,128]{2,1,0:T(8,128)S(1)} %get-tuple-element.48), channel_id=1, source_target_pairs={{0,8},{8,16},{16,24},{24,0},{1,9},{9,17},{17,25},{25,1},{2,10},{10... | collective-permute-start | bytes 196616 | tf_op jit(solution)/shard_map/ppermute | solution.py:619
  12.8 2.2 %collective-permute-start.6 = (f32[16,8,128]{2,1,0:T(8,128)S(1)}, f32[16,8,128]{2,1,0:T(8,128)S(1)}, u32[]{:S(2)}, u32[]{:S(2)}) collective-permute-start(f32[16,8,128]{2,1,0:T(8,128)S(1)} %get-tuple-element.49), channel_id=1, source_target_pairs={{0,24},{8,0},{16,8},{24,16},{1,25},{9,1},{17,9},{25,17},{2,26},{10... | collective-permute-start | bytes 196616 | tf_op jit(solution)/shard_map/ppermute | solution.py:619
  17.5 1.4 %collective-permute-done.6.xl = f32[16,8,128]{2,1,0:T(8,128)S(1)} collective-permute-done((f32[16,8,128]{2,1,0:T(8,128)S(1)}, f32[16,8,128]{2,1,0:T(8,128)S(1)}, u32[]{:S(2)}, u32[]{:S(2)}) %collective-permute-start.6) | collective-permute-done | bytes 65568 | tf_op jit(solution)/shard_map/ppermute | solution.py:619
  19.6 1.0 %collective-permute-start.7 = (f32[39,8,128]{2,1,0:T(8,128)S(1)}, f32[39,8,128]{2,1,0:T(8,128)S(1)}, u32[]{:S(2)}, u32[]{:S(2)}) collective-permute-start(f32[39,8,128]{2,1,0:T(8,128)S(1)} %get-tuple-element.53), channel_id=1, source_target_pairs={{0,8},{8,16},{16,24},{24,0},{1,9},{9,17},{17,25},{25,1},{2,10},{10... | collective-permute-start | bytes 479240 | tf_op jit(solution)/shard_map/ppermute | solution.py:619
  20.6 2.1 %collective-permute-start.11 = (f32[8,128]{1,0:T(8,128)S(1)}, f32[8,128]{1,0:T(8,128)S(1)}, u32[]{:S(2)}, u32[]{:S(2)}) collective-permute-start(f32[8,128]{1,0:T(8,128)S(1)} %get-tuple-element.50.rider.own), channel_id=1, source_target_pairs={{0,16},{8,24},{16,0},{24,8},{1,17},{9,25},{17,1},{25,9},{2,18},{10... | collective-permute-start | bytes 12296 | tf_op jit(solution)/shard_map/ppermute | solution.py:619
  23.4 1.1 %collective-permute-start.8 = (f32[39,8,128]{2,1,0:T(8,128)S(1)}, f32[39,8,128]{2,1,0:T(8,128)S(1)}, u32[]{:S(2)}, u32[]{:S(2)}) collective-permute-start(f32[39,8,128]{2,1,0:T(8,128)S(1)} %get-tuple-element.54), channel_id=1, source_target_pairs={{0,24},{8,0},{16,8},{24,16},{1,25},{9,1},{17,9},{25,17},{2,26},{10... | collective-permute-start | bytes 479240 | tf_op jit(solution)/shard_map/ppermute | solution.py:619
  24.5 1.0 %shard_map.104.early = f32[16,16,256]{2,1,0:T(8,128)S(1)} custom-call(f32[3,2,16,128]{3,2,1,0:T(8,128)S(1)} %get-tuple-element.61.v0, f32[3,2,16,128]{3,2,1,0:T(8,128)S(1)} %get-tuple-element.62.v1, s32[2,16,128]{2,1,0:T(8,128)S(1)} %copy-done, bf16[256,4096]{1,0:T(8,128)(2,1)S(1)} %shard_map.103.right), custom_call_target="tpu_custom_call" | custom-call | tf_op jit(solution)/shard_map/pallas_call | solution.py:703
  25.4 3.0 %collective-permute-done.7.xr = f32[39,8,128]{2,1,0:T(8,128)S(1)} collective-permute-done((f32[39,8,128]{2,1,0:T(8,128)S(1)}, f32[39,8,128]{2,1,0:T(8,128)S(1)}, u32[]{:S(2)}, u32[]{:S(2)}) %collective-permute-start.7) | collective-permute-done | bytes 159776 | tf_op jit(solution)/shard_map/ppermute | solution.py:619
  28.4 2.6 %collective-permute-done.8.xl = f32[39,8,128]{2,1,0:T(8,128)S(1)} collective-permute-done((f32[39,8,128]{2,1,0:T(8,128)S(1)}, f32[39,8,128]{2,1,0:T(8,128)S(1)}, u32[]{:S(2)}, u32[]{:S(2)}) %collective-permute-start.8) | collective-permute-done | bytes 159776 | tf_op jit(solution)/shard_map/ppermute | solution.py:619
  31.7 1.1 %shard_map.105 = f32[16,16,256]{2,1,0:T(8,128)S(1)} custom-call(f32[19,2,24,256]{3,2,1,0:T(8,128)S(1)} %get-tuple-element.55.ahead, f32[2,24,256]{2,1,0:T(8,128)S(1)} %get-tuple-element.47.g_ref, f32[2,5,24,256]{3,2,1,0:T(8,128)S(1)} %get-tuple-element.56.side, f32[3,2,16,128]{3,2,1,0:T(8,128)S(1)} %get-tuple-element.60.v2, s32[2,16,128]{2,1,0:T(8,128)S(1)} %copy-done, ...), custom_call_target="tpu_custom_call" | custom-call | tf_op jit(solution)/shard_map/pallas_call | solution.py:706
  32.9 9.3 %all_to_all.22 = f32[8,32,256]{2,1,0:T(8,128)S(1)} all-to-all(f32[8,32,256]{2,1,0:T(8,128)S(1)} %bitcast.10), channel_id=1, replica_groups=mesh['gx'=4,'gy'=2,'gz'=4] {'gy','gz'}, dimensions={0} | all-to-all | bytes 524288 | tf_op jit(solution)/shard_map/all_to_all | solution.py:713
  42.2 0.9 %shard_map.106 = (f32[16,512]{1,0:T(8,128)S(1)}, f32[8,128]{1,0:T(8,128)S(1)}, f32[128,128]{1,0:T(8,128)}) custom-call(f32[256,256]{1,0:T(8,128)S(1)} %bitcast.9, f32[32,512]{1,0:T(8,128)S(1)} %get-tuple-element.63.scaled), custom_call_target="tpu_custom_call" | custom-call | tf_op jit(solution)/shard_map/pallas_call | solution.py:714
  43.1 2.6 %all-to-all-start.1 = ((f32[32,4,128]{2,1,0:T(4,128)}), f32[32,4,128]{2,1,0:T(4,128)S(1)}, u32[]{:S(2)}, u32[]{:S(2)}) async-start(f32[32,4,128]{2,1,0:T(4,128)} %bitcast.5), calls=%async_computation.1 | async-start | bytes 131072 | tf_op jit(solution)/shard_map/all_to_all | solution.py:720
  46.0 1.7 %collective-permute-start.9 = (f32[16,8,128]{2,1,0:T(8,128)S(1)}, f32[16,8,128]{2,1,0:T(8,128)S(1)}, u32[]{:S(2)}, u32[]{:S(2)}) collective-permute-start(f32[16,8,128]{2,1,0:T(8,128)S(1)} %get-tuple-element.58), channel_id=1, source_target_pairs={{0,8},{8,16},{16,24},{24,0},{1,9},{9,17},{17,25},{25,1},{2,10},{10... | collective-permute-start | bytes 196616 | tf_op jit(solution)/shard_map/ppermute | solution.py:619
  47.8 2.1 %collective-permute-start.10 = (f32[16,8,128]{2,1,0:T(8,128)S(1)}, f32[16,8,128]{2,1,0:T(8,128)S(1)}, u32[]{:S(2)}, u32[]{:S(2)}) collective-permute-start(f32[16,8,128]{2,1,0:T(8,128)S(1)} %get-tuple-element.59), channel_id=1, source_target_pairs={{0,24},{8,0},{16,8},{24,16},{1,25},{9,1},{17,9},{25,17},{2,26},{10... | collective-permute-start | bytes 196616 | tf_op jit(solution)/shard_map/ppermute | solution.py:619
  49.9 3.4 %collective-permute-done.9.xr = f32[16,8,128]{2,1,0:T(8,128)S(1)} collective-permute-done((f32[16,8,128]{2,1,0:T(8,128)S(1)}, f32[16,8,128]{2,1,0:T(8,128)S(1)}, u32[]{:S(2)}, u32[]{:S(2)}) %collective-permute-start.9) | collective-permute-done | bytes 65568 | tf_op jit(solution)/shard_map/ppermute | solution.py:619
  53.4 0.9 %shard_map.102 = f32[19,2,16,128]{3,2,1,0:T(8,128)} custom-call(f32[19,2,24,256]{3,2,1,0:T(8,128)S(1)} %get-tuple-element.57.prev, f32[16,8,128]{2,1,0:T(8,128)S(1)} %collective-permute-done.9.xr, f32[16,8,128]{2,1,0:T(8,128)S(1)} %collective-permute-done.10.xl), custom_call_target="tpu_custom_call" | custom-call | tf_op jit(solution)/shard_map/pallas_call | solution.py:725
  54.3 2.3 %shard_map.107 = (f32[32,128]{1,0:T(8,128)S(1)}, f32[32,512]{1,0:T(8,128)S(1)}) custom-call(f32[8,128]{1,0:T(8,128)S(1)} %get-tuple-element.65.tile, f32[32,512]{1,0:T(8,128)S(1)} %get-tuple-element.63.scaled), custom_call_target="tpu_custom_call" | custom-call | tf_op jit(solution)/shard_map/pallas_call | solution.py:721
  56.6 2.3 %shard_map.108 = (f32[44,512]{1,0:T(8,128)}, f32[44,44]{1,0:T(8,128)}) custom-call(f32[128,128]{1,0:T(8,128)S(1)} %bitcast.11, f32[32,128]{1,0:T(8,128)S(1)} %get-tuple-element.66.factor, f32[32,512]{1,0:T(8,128)S(1)} %get-tuple-element.67.head, f32[16,512]{1,0:T(8,128)S(1)} %get-tuple-element.68.snap), custom_call_target="tpu_custom_call" | custom-call | tf_op jit(solution)/shard_map/pallas_call | solution.py:722
  (25 shorter events, 5.6 us)
Async XLA Ops:
  2.0 8.9 %collective-permute-start.2 = (f32[40,8,128]{2,1,0:T(8,128)S(1)}, f32[40,8,128]{2,1,0:T(8,128)S(1)}, u32[]{:S(2)}, u32[]{:S(2)}) collective-permute-start(f32[40,8,128]{2,1,0:T(8,128)S(1)} %get-tuple-element.43), channel_id=1, source_target_pairs={{0,4},{1,5},{2,6},{3,7},{4,0},{5,1},{6,2},{7,3},{8,12},{9,13},{10,... | collective-permute-start | bytes 491528 | tf_op jit(solution)/shard_map/ppermute | solution.py:627
  5.0 4.4 %collective-permute-start = (f32[3,8,128]{2,1,0:T(8,128)S(1)}, f32[3,8,128]{2,1,0:T(8,128)S(1)}, u32[]{:S(2)}, u32[]{:S(2)}) collective-permute-start(f32[3,8,128]{2,1,0:T(8,128)S(1)} %get-tuple-element.39), channel_id=1, source_target_pairs={{0,1},{1,2},{2,3},{3,0},{4,5},{5,6},{6,7},{7,4},{8,9},{9,10},{10,1... | collective-permute-start | bytes 36872 | tf_op jit(solution)/shard_map/ppermute | solution.py:619
  5.0 4.4 %collective-permute-start.1 = (f32[3,8,128]{2,1,0:T(8,128)S(1)}, f32[3,8,128]{2,1,0:T(8,128)S(1)}, u32[]{:S(2)}, u32[]{:S(2)}) collective-permute-start(f32[3,8,128]{2,1,0:T(8,128)S(1)} %get-tuple-element.40), channel_id=1, source_target_pairs={{0,3},{1,0},{2,1},{3,2},{4,7},{5,4},{6,5},{7,6},{8,11},{9,8},{10,9... | collective-permute-start | bytes 36872 | tf_op jit(solution)/shard_map/ppermute | solution.py:619
  6.8 4.0 %collective-permute-start.3 = (f32[2,8,128]{2,1,0:T(8,128)S(1)}, f32[2,8,128]{2,1,0:T(8,128)S(1)}, u32[]{:S(2)}, u32[]{:S(2)}) collective-permute-start(f32[2,8,128]{2,1,0:T(8,128)S(1)} %get-tuple-element.44), channel_id=1, source_target_pairs={{0,5},{1,6},{2,7},{3,4},{4,1},{5,2},{6,3},{7,0},{8,13},{9,14},{10,... | collective-permute-start | bytes 24584 | tf_op jit(solution)/shard_map/ppermute | solution.py:627
  6.8 4.1 %collective-permute-start.4 = (f32[2,8,128]{2,1,0:T(8,128)S(1)}, f32[2,8,128]{2,1,0:T(8,128)S(1)}, u32[]{:S(2)}, u32[]{:S(2)}) collective-permute-start(f32[2,8,128]{2,1,0:T(8,128)S(1)} %get-tuple-element.45), channel_id=1, source_target_pairs={{0,7},{1,4},{2,5},{3,6},{4,3},{5,0},{6,1},{7,2},{8,15},{9,12},{10,... | collective-permute-start | bytes 24584 | tf_op jit(solution)/shard_map/ppermute | solution.py:627
  10.8 11.9 %copy-start = (s32[2,16,128]{2,1,0:T(8,128)S(1)}, s32[2,16,128]{2,1,0:T(8,128)}, u32[]{:S(2)}) copy-start(s32[2,16,128]{2,1,0:T(8,128)} %row_map.5) | copy-start | bytes 49156
  11.1 6.4 %collective-permute-start.5 = (f32[16,8,128]{2,1,0:T(8,128)S(1)}, f32[16,8,128]{2,1,0:T(8,128)S(1)}, u32[]{:S(2)}, u32[]{:S(2)}) collective-permute-start(f32[16,8,128]{2,1,0:T(8,128)S(1)} %get-tuple-element.48), channel_id=1, source_target_pairs={{0,8},{8,16},{16,24},{24,0},{1,9},{9,17},{17,25},{25,1},{2,10},{10... | collective-permute-start | bytes 196616 | tf_op jit(solution)/shard_map/ppermute | solution.py:619
  12.8 6.2 %collective-permute-start.6 = (f32[16,8,128]{2,1,0:T(8,128)S(1)}, f32[16,8,128]{2,1,0:T(8,128)S(1)}, u32[]{:S(2)}, u32[]{:S(2)}) collective-permute-start(f32[16,8,128]{2,1,0:T(8,128)S(1)} %get-tuple-element.49), channel_id=1, source_target_pairs={{0,24},{8,0},{16,8},{24,16},{1,25},{9,1},{17,9},{25,17},{2,26},{10... | collective-permute-start | bytes 196616 | tf_op jit(solution)/shard_map/ppermute | solution.py:619
  15.7 0.8 %copy-start.1 = (f32[32,512]{1,0:T(8,128)S(1)}, f32[32,512]{1,0:T(8,128)}, u32[]{:S(2)}) copy-start(f32[32,512]{1,0:T(8,128)} %basis.1) | copy-start | bytes 196612
  19.6 8.8 %collective-permute-start.7 = (f32[39,8,128]{2,1,0:T(8,128)S(1)}, f32[39,8,128]{2,1,0:T(8,128)S(1)}, u32[]{:S(2)}, u32[]{:S(2)}) collective-permute-start(f32[39,8,128]{2,1,0:T(8,128)S(1)} %get-tuple-element.53), channel_id=1, source_target_pairs={{0,8},{8,16},{16,24},{24,0},{1,9},{9,17},{17,25},{25,1},{2,10},{10... | collective-permute-start | bytes 479240 | tf_op jit(solution)/shard_map/ppermute | solution.py:619
  20.6 11.1 %collective-permute-start.11 = (f32[8,128]{1,0:T(8,128)S(1)}, f32[8,128]{1,0:T(8,128)S(1)}, u32[]{:S(2)}, u32[]{:S(2)}) collective-permute-start(f32[8,128]{1,0:T(8,128)S(1)} %get-tuple-element.50.rider.own), channel_id=1, source_target_pairs={{0,16},{8,24},{16,0},{24,8},{1,17},{9,25},{17,1},{25,9},{2,18},{10... | collective-permute-start | bytes 12296 | tf_op jit(solution)/shard_map/ppermute | solution.py:619
  23.4 7.7 %collective-permute-start.8 = (f32[39,8,128]{2,1,0:T(8,128)S(1)}, f32[39,8,128]{2,1,0:T(8,128)S(1)}, u32[]{:S(2)}, u32[]{:S(2)}) collective-permute-start(f32[39,8,128]{2,1,0:T(8,128)S(1)} %get-tuple-element.54), channel_id=1, source_target_pairs={{0,24},{8,0},{16,8},{24,16},{1,25},{9,1},{17,9},{25,17},{2,26},{10... | collective-permute-start | bytes 479240 | tf_op jit(solution)/shard_map/ppermute | solution.py:619
  43.1 13.5 %all-to-all-start.1 = ((f32[32,4,128]{2,1,0:T(4,128)}), f32[32,4,128]{2,1,0:T(4,128)S(1)}, u32[]{:S(2)}, u32[]{:S(2)}) async-start(f32[32,4,128]{2,1,0:T(4,128)} %bitcast.5), calls=%async_computation.1 | async-start | bytes 131072 | tf_op jit(solution)/shard_map/all_to_all | solution.py:720
  46.0 7.3 %collective-permute-start.9 = (f32[16,8,128]{2,1,0:T(8,128)S(1)}, f32[16,8,128]{2,1,0:T(8,128)S(1)}, u32[]{:S(2)}, u32[]{:S(2)}) collective-permute-start(f32[16,8,128]{2,1,0:T(8,128)S(1)} %get-tuple-element.58), channel_id=1, source_target_pairs={{0,8},{8,16},{16,24},{24,0},{1,9},{9,17},{17,25},{25,1},{2,10},{10... | collective-permute-start | bytes 196616 | tf_op jit(solution)/shard_map/ppermute | solution.py:619
  47.8 5.6 %collective-permute-start.10 = (f32[16,8,128]{2,1,0:T(8,128)S(1)}, f32[16,8,128]{2,1,0:T(8,128)S(1)}, u32[]{:S(2)}, u32[]{:S(2)}) collective-permute-start(f32[16,8,128]{2,1,0:T(8,128)S(1)} %get-tuple-element.59), channel_id=1, source_target_pairs={{0,24},{8,0},{16,8},{24,16},{1,25},{9,1},{17,9},{25,17},{2,26},{10... | collective-permute-start | bytes 196616 | tf_op jit(solution)/shard_map/ppermute | solution.py:619

commit v5 on v4

--- a/solution.py
+++ b/solution.py
@@ -360,7 +360,7 @@
     return pick
 
 
-def step_kernel(ahead_in, g_ref, xr, xl, rider, ahead, going, vel_ref, xr_ref, xl_ref, side, out):
+def step_kernel(ahead_in, g_ref, xr, xl, ahead, going, vel_ref, xr_ref, xl_ref, side, out):
     take_faces(xr, xl, side)
     collide_all(chooser(ahead_in, side), g_ref, out, vel_ref)
     local_kernel(out, ahead)
@@ -368,8 +368,6 @@
         going[0, i] = turned(out[PLUS_X[i], 1], PLUS_X[i])
         going[1, i] = turned(out[MINUS_X[i], 0], MINUS_X[i])
     pack_deep(ahead, going, g_ref, (xr_ref, xl_ref))
-    xr_ref[DEEP_TILES] = rider[...]
-    xl_ref[DEEP_TILES] = rider[...]
 
 
 def pair_kernel(ahead, going, g_ref, xr, xl, ahead_ref, side_ref, vel_ref, deep, out):
@@ -395,18 +393,25 @@
     local_kernel(out, ahead_ref)
 
 
-def end_step_kernel(ahead, g_ref, side, out, xr_ref, xl_ref):
+def end_step_kernel(ahead, g_ref, side, rider, out, xr_ref, xl_ref):
     collide_all(chooser(ahead, side), g_ref, out, None)
-    pack_x(out, xr_ref, xl_ref)
-
-
-def last_kernel(prev, xr, xl, out, side):
-    take_faces(xr, xl, side)
+    for ref, directions, x in ((xr_ref, PLUS_X, 1), (xl_ref, MINUS_X, 0)):
+        for i, q in enumerate(directions):
+            value = turned(out[q, x], q)
+            for yt in range(2):
+                ref[2 * i + yt] = value[8 * yt : 8 * yt + 8, :128]
+        ref[10] = rider[...]
+
+
+def last_kernel(prev, xr, xl, out):
     for q in range(19):
         for x in range(2):
             at = remote(q, x)
-            value = turned(prev[q, x - int(LATTICE[q, 0])], q) if at is None else side[at[0], at[1]]
-            out[q, x] = value[:16, :128]
+            if at is None:
+                out[q, x] = turned(prev[q, x - int(LATTICE[q, 0])], q)[:16, :128]
+            else:
+                for yt in range(2):
+                    out[q, x, pl.ds(8 * yt, 8), :] = (xr, xl)[at[0]][2 * at[1] + yt]
 
 
 def split(value):
@@ -447,12 +452,12 @@
 
 
 def early_kernel(v0, v1, row_map, right, out, left):
-    highs = out.shape[0]
+    highs = out.shape[0] // 12
     both = restricted((v0, v1), row_map, right, left)
     for h in range(highs):
         for j in range(6):
-            out[h, pl.ds(j, 1), :] = both[highs * j + h : highs * j + h + 1]
-        out[h, pl.ds(6, 10), :] = jnp.zeros((10, LOW), jnp.float32)
+            out[pl.ds(12 * h + j, 1), :] = both[highs * j + h : highs * j + h + 1]
+            out[pl.ds(12 * h + 6 + j, 1), :] = jnp.zeros((1, LOW), jnp.float32)
 
 
 def old_kernel(total_rows, basis, sigma, scaled_ref, tile_ref, work):
@@ -478,7 +483,7 @@
     )
 
 
-def late_kernel(ahead, g_ref, side, v2, row_map, right, early, own, near_r, near_l, far, out, left, v3):
+def late_kernel(ahead, g_ref, side, v2, row_map, right, early, out, left, v3):
     pick = chooser(ahead, side)
     for x in range(2):
         for yt in range(2):
@@ -488,30 +493,23 @@
             factor = jnp.where(g < 0.0, 0.0, vel_scale / VOX_ROW)
             for a in range(3):
                 v3[a, x, rows, :] = speeds[a] * factor
-    highs = out.shape[0]
+    highs = out.shape[0] // 12
     both = restricted((v2, v3), row_map, right, left)
     out[...] = early[...]
-    old = (own[...] + far[...]) + (near_r[...] + near_l[...])
     for h in range(highs):
         for j in range(6):
-            out[h, pl.ds(6 + j, 1), :] = both[highs * j + h : highs * j + h + 1]
-        if h % 2 == 0:
-            out[h, pl.ds(12, 4), pl.ds(0, 128)] = old[:4]
-            out[h, pl.ds(12, 4), pl.ds(128, 128)] = old[4:]
-
-
-def gram_kernel(total_rows, parts, scaled, snap_ref, tile_ref, out, aug):
-    owners = parts.shape[0] // 32
-    total = parts[pl.ds(0, 32), :]
+            out[pl.ds(12 * h + 6 + j, 1), :] = both[highs * j + h : highs * j + h + 1]
+
+
+def gram_kernel(total_rows, parts, scaled, snap_ref, out, aug):
+    owners = parts.shape[0] // 24
+    total = parts[pl.ds(0, 24), :]
     for o in range(1, owners):
-        total = total + parts[pl.ds(32 * o, 32), :]
-    tile_ref[pl.ds(0, 4), :] = total[12:16, :128]
-    tile_ref[pl.ds(4, 4), :] = total[12:16, 128:]
-    used = lax.broadcasted_iota(jnp.int32, (16, LOW), 0) < 12
+        total = total + parts[pl.ds(24 * o, 24), :]
     aug[pl.ds(0, 32), :] = scaled[...]
-    aug[pl.ds(32, 16), pl.ds(0, LOW)] = jnp.where(used, total[:16], 0.0)
-    aug[pl.ds(32, 16), pl.ds(LOW, LOW)] = jnp.where(used, total[16:], 0.0)
-    aug[pl.ds(48, 80), :] = jnp.zeros((80, 2 * LOW), jnp.float32)
+    aug[pl.ds(40, 88), :] = jnp.zeros((88, 2 * LOW), jnp.float32)
+    aug[pl.ds(32, 12), pl.ds(0, LOW)] = total[:12]
+    aug[pl.ds(32, 12), pl.ds(LOW, LOW)] = total[12:]
     snap = aug[pl.ds(32, 16), :]
     snap_ref[...] = snap
     product = dot(snap, aug[...], 1) * (1.0 / total_rows)
@@ -665,7 +663,7 @@
     wide = pltpu.VMEM((19, 2, 24, 256), jnp.float32)
     side = pltpu.VMEM((2, 5, 24, 256), jnp.float32)
     big, wall, vel, face = vmem(19, 2, 24, 256), vmem(2, 24, 256), vmem(3, 2, 16, 128), vmem(16, *tile)
-    loaded, sides = vmem(DEEP_TILES + 1, *tile), vmem(2, 5, 24, 256)
+    deep_face, loaded, sides = vmem(DEEP_TILES, *tile), vmem(11, *tile), vmem(2, 5, 24, 256)
     relaxed, g_wide, v0 = call(inner_kernel, (big, wall, vel), (wide,), count=4)(
         *map(held, (pops, g, left, right))
     )
@@ -678,51 +676,55 @@
         (pltpu.VMEM((32, 128), jnp.float32),),
         count=2,
     )(old_basis, old_sigma[:, None])
-    ring = lax.axis_size("gx") == 4
-    if not ring:
-        own = lax.psum(own, "gx")
-    none = jnp.zeros(tile, jnp.float32)
+    small = tuple(lax.axis_size(a) for a in everyone) == (4, 2, 4)
+    if not small:
+        own = lax.psum(own, everyone)
     onehot = call(onehot_kernel, pltpu.VMEM((LOW, cells), jnp.bfloat16), count=1)(row_map)
     xr, xl = shift(xr, "gx", 1), shift(xl, "gx", -1)
     ahead = call(local_kernel, big, count=1)(held(relaxed))
-    ahead, going, v1, xr, xl = call(step_kernel, (big, sides, vel, loaded, loaded), (side, wide), count=5)(
-        *map(held, (ahead, g_wide, xr, xl, own))
-    )
+    if small:
+        own = own + shift(own, "gy", 1)
+    ahead, going, v1, xr, xl = call(
+        step_kernel, (big, sides, vel, deep_face, deep_face), (side, wide), count=4
+    )(*map(held, (ahead, g_wide, xr, xl)))
     xr, xl = shift(xr, "gx", 1), shift(xl, "gx", -1)
-    got = [none] * 3
-    if ring:
-        got = [xr[DEEP_TILES], xl[DEEP_TILES], shift(own, "gx", 2)]
+    if small:
+        own = (own + shift(own, "gz", 2)) + (shift(own, "gz", 1) + shift(own, "gz", -1))
     ahead, faces, v2 = call(
         pair_kernel, (big, sides, vel), (pltpu.VMEM((2, DEEP, 24, 256), jnp.float32), wide), count=5
     )(*map(held, (ahead, going, g_wide, xr, xl)))
     state = tuple(map(held, (ahead, g_wide, faces)))
-    relaxed, xr, xl = call(end_step_kernel, (big, face, face), count=3)(*state)
+    relaxed, xr, xl = call(end_step_kernel, (big, loaded, loaded), count=4)(*state, held(own))
     xr, xl = shift(xr, "gx", 1), shift(xl, "gx", -1)
+    if small:
+        own = (own + shift(own, "gx", 2)) + (xr[10] + xl[10])
 
     lefts = pltpu.VMEM((12 * highs, cells), jnp.bfloat16)
-    early = call(early_kernel, vmem(highs, 16, LOW), (lefts,), count=4, limit=12 + highs // 2)(
+    early = call(early_kernel, vmem(12 * highs, LOW), (lefts,), count=4, limit=12 + highs // 2)(
         held(v0), held(v1), row_map, held(onehot)
     )
     term = call(
         late_kernel,
-        f32(highs, 16, LOW),
+        f32(12 * highs, LOW),
         (lefts, pltpu.VMEM((3, 2, 16, 128), jnp.float32)),
-        count=11,
+        count=7,
         limit=12 + highs // 2,
-    )(*state, held(v2), row_map, *map(held, (onehot, early, own, *got)))
-    parts = lax.all_to_all(term.reshape(16 * highs, LOW), slab, 0, 0, tiled=True)
-    snap, old_tile, gram = call(
+    )(*state, held(v2), row_map, held(onehot), held(early))
+    parts = lax.all_to_all(term, slab, 0, 0, tiled=True)
+    snap, gram = call(
         functools.partial(gram_kernel, float(rows_local * devices)),
-        (vmem(16, rows_local), vmem(*tile), f32(4 * devices, 128)),
+        (vmem(16, rows_local), f32(4 * devices, 128)),
         (pltpu.VMEM((128, rows_local), jnp.float32),),
         count=2,
     )(held(parts), held(old))
     grams = lax.all_to_all(gram, everyone, 0, 0, tiled=True)
-    factor, head = call(old_factor_kernel, (vmem(32, 128), vmem(32, rows_local)), count=2)(held(old_tile), held(old))
+    factor, head = call(old_factor_kernel, (vmem(32, 128), vmem(32, rows_local)), count=2)(
+        held(own), held(old)
+    )
     new_basis, upper = call(
         factor_kernel, (f32(44, rows_local), f32(44, 44)), (pltpu.VMEM((16, 128), jnp.float32),), count=4
     )(*map(held, (grams, factor, head, snap)))
-    populations = call(last_kernel, f32(19, 2, 16, 128), (side,), count=3)(*map(held, (relaxed, xr, xl)))
+    populations = call(last_kernel, f32(19, 2, 16, 128), count=3)(*map(held, (relaxed, xr, xl)))
     return (populations, new_basis, upper)
 
 

time: 59.2 us -> 57.4 us (0.970)
  blocking collectives: 9.32 us -> 0 us
  starting transfers between devices: 22 us -> 27.7 us
  waiting for transfers between devices: 12 us -> 14.4 us
  local copies, waits for them, and re-layouts: 1.58 us -> 0.1 us
  Pallas kernels: 13.3 us -> 14.1 us
    all_to_all x1 -> x0, blocking collectives: 9.32 us -> none  [on_device(): lax.all_to_all(term.reshape(16 * highs, LOW), slab, 0, 0, tiled=True)]
    all_to_all x1, waiting for transfers between devices: 0.01 us -> 4.23 us  [on_device(): grams = lax.all_to_all(gram, everyone, 0, 0, tiled=True)]
    ppermute x9 -> x13, waiting for transfers between devices: 10.9 us -> 7.36 us  [shift(): lax.ppermute(value, axis, [(i, (i + step) % count) for i in range(count)])]
    all_to_all x0 -> x1, starting transfers between devices: none -> 3.39 us  [on_device(): parts = lax.all_to_all(term, slab, 0, 0, tiled=True)]
    all_to_all x0 -> x1, waiting for transfers between devices: none -> 1.84 us  [on_device(): parts = lax.all_to_all(term, slab, 0, 0, tiled=True)]
    all_to_all x1, starting transfers between devices: 2.57 us -> 3.73 us  [on_device(): grams = lax.all_to_all(gram, everyone, 0, 0, tiled=True)]
    ppermute x9 -> x13, starting transfers between devices: 13.7 us -> 14.9 us  [shift(): lax.ppermute(value, axis, [(i, (i + step) % count) for i in range(count)])]
    unnamed x4 -> x6, local copies, waits for them, and re-layouts: 0.84 us -> 0.02 us
  transfers between devices with their start and end apart: 13 -> 18, of which waited for: 8 -> 7; matrix products, arithmetic and copies ran while one was open for 1% -> 0% of each run, Pallas kernels for 11% -> 17%
where the time goes in v5:
time: 57.4 us; the launch traced here: 57.2 us
  starting transfers between devices  27.7 us (48%)
  waiting for transfers between devices  14.4 us (25%)
  Pallas kernels  14.1 us (25%)
  between operations  0.83 us (1%)
    ppermute x13, starting transfers between devices, shift(): lax.ppermute(value, axis, [(i, (i + step) % count) for i in range(count)])  14.9 us
    ppermute x13, waiting for transfers between devices, shift(): lax.ppermute(value, axis, [(i, (i + step) % count) for i in range(count)])  7.36 us
    ppermute x3, starting transfers between devices, shift_both(): return lax.ppermute(value, ('gy', 'gz'), pairs)  5.71 us
    all_to_all x1, waiting for transfers between devices, on_device(): grams = lax.all_to_all(gram, everyone, 0, 0, tiled=True)  4.23 us
    all_to_all x1, starting transfers between devices, on_device(): grams = lax.all_to_all(gram, everyone, 0, 0, tiled=True)  3.73 us
    all_to_all x1, starting transfers between devices, on_device(): parts = lax.all_to_all(term, slab, 0, 0, tiled=True)  3.39 us
    pallas_call x1, Pallas kernels, on_device(): call(factor_kernel, (f32(44, rows_local), f32(44, 44)), (pltpu.VMEM((16,...  2.32 us
    pallas_call x1, Pallas kernels, on_device(): call(old_factor_kernel, (vmem(32, 128), vmem(32, rows_local)), count=2)  2.26 us
  transfers between devices with their start and end apart: 18, of which 7 were waited for; matrix products, arithmetic and copies ran while one was open for 0% of the time, Pallas kernels for 17%

profile of v5, /device:TPU:0, one launch (start us, length us, event | category | flops | bytes accessed | tf_op | source)
XLA Modules:
  0.0 57.2 jit_solution(11627626200856541774)
XLA Ops:
  0.6 1.3 %shard_map.94 = (f32[19,2,16,128]{3,2,1,0:T(8,128)S(1)}, f32[2,16,128]{2,1,0:T(8,128)S(1)}, f32[3,8,128]{2,1,0:T(8,128)S(1)}, f32[3,8,128]{2,1,0:T(8,128)S(1)}, ...) custom-call(f32[8]{0:T(128)} %table_hbm.1, f32[19,2,16,128]{3,2,1,0:T(8,128)} %ratio_hbm.1, ...), custom_call_target="tpu_custom_call" | custom-call | tf_op jit(solution)/shard_map/pallas_call | solution.py:645
  2.0 3.1 %collective-permute-start.2 = (f32[40,8,128]{2,1,0:T(8,128)S(1)}, f32[40,8,128]{2,1,0:T(8,128)S(1)}, u32[]{:S(2)}, u32[]{:S(2)}) collective-permute-start(f32[40,8,128]{2,1,0:T(8,128)S(1)} %get-tuple-element.42), channel_id=1, source_target_pairs={{0,4},{1,5},{2,6},{3,7},{4,0},{5,1},{6,2},{7,3},{8,12},{9,13},{10,... | collective-permute-start | bytes 491528 | tf_op jit(solution)/shard_map/ppermute | solution.py:625
  5.0 1.7 %collective-permute-start.1 = (f32[3,8,128]{2,1,0:T(8,128)S(1)}, f32[3,8,128]{2,1,0:T(8,128)S(1)}, u32[]{:S(2)}, u32[]{:S(2)}) collective-permute-start(f32[3,8,128]{2,1,0:T(8,128)S(1)} %get-tuple-element.39), channel_id=1, source_target_pairs={{0,3},{1,0},{2,1},{3,2},{4,7},{5,4},{6,5},{7,6},{8,11},{9,8},{10,9... | collective-permute-start | bytes 36872 | tf_op jit(solution)/shard_map/ppermute | solution.py:617
  6.8 2.6 %collective-permute-start.4 = (f32[2,8,128]{2,1,0:T(8,128)S(1)}, f32[2,8,128]{2,1,0:T(8,128)S(1)}, u32[]{:S(2)}, u32[]{:S(2)}) collective-permute-start(f32[2,8,128]{2,1,0:T(8,128)S(1)} %get-tuple-element.44), channel_id=1, source_target_pairs={{0,7},{1,4},{2,5},{3,6},{4,3},{5,0},{6,1},{7,2},{8,15},{9,12},{10,... | collective-permute-start | bytes 24584 | tf_op jit(solution)/shard_map/ppermute | solution.py:625
  9.8 0.9 %collective-permute-done.3.cr = f32[2,8,128]{2,1,0:T(8,128)S(1)} collective-permute-done((f32[2,8,128]{2,1,0:T(8,128)S(1)}, f32[2,8,128]{2,1,0:T(8,128)S(1)}, u32[]{:S(2)}, u32[]{:S(2)}) %collective-permute-start.3) | collective-permute-done | bytes 8224 | tf_op jit(solution)/shard_map/ppermute | solution.py:625
  11.1 1.6 %collective-permute-start.5 = (f32[16,8,128]{2,1,0:T(8,128)S(1)}, f32[16,8,128]{2,1,0:T(8,128)S(1)}, u32[]{:S(2)}, u32[]{:S(2)}) collective-permute-start(f32[16,8,128]{2,1,0:T(8,128)S(1)} %get-tuple-element.47), channel_id=1, source_target_pairs={{0,8},{8,16},{16,24},{24,0},{1,9},{9,17},{17,25},{25,1},{2,10},{10... | collective-permute-start | bytes 196616 | tf_op jit(solution)/shard_map/ppermute | solution.py:617
  12.8 2.2 %collective-permute-start.6 = (f32[16,8,128]{2,1,0:T(8,128)S(1)}, f32[16,8,128]{2,1,0:T(8,128)S(1)}, u32[]{:S(2)}, u32[]{:S(2)}) collective-permute-start(f32[16,8,128]{2,1,0:T(8,128)S(1)} %get-tuple-element.48), channel_id=1, source_target_pairs={{0,24},{8,0},{16,8},{24,16},{1,25},{9,1},{17,9},{25,17},{2,26},{10... | collective-permute-start | bytes 196616 | tf_op jit(solution)/shard_map/ppermute | solution.py:617
  15.2 2.3 %collective-permute-done.5.xr = f32[16,8,128]{2,1,0:T(8,128)S(1)} collective-permute-done((f32[16,8,128]{2,1,0:T(8,128)S(1)}, f32[16,8,128]{2,1,0:T(8,128)S(1)}, u32[]{:S(2)}, u32[]{:S(2)}) %collective-permute-start.5) | collective-permute-done | bytes 65568 | tf_op jit(solution)/shard_map/ppermute | solution.py:617
  17.5 1.4 %collective-permute-done.6.xl = f32[16,8,128]{2,1,0:T(8,128)S(1)} collective-permute-done((f32[16,8,128]{2,1,0:T(8,128)S(1)}, f32[16,8,128]{2,1,0:T(8,128)S(1)}, u32[]{:S(2)}, u32[]{:S(2)}) %collective-permute-start.6) | collective-permute-done | bytes 65568 | tf_op jit(solution)/shard_map/ppermute | solution.py:617
  19.6 1.0 %collective-permute-start.7 = (f32[38,8,128]{2,1,0:T(8,128)S(1)}, f32[38,8,128]{2,1,0:T(8,128)S(1)}, u32[]{:S(2)}, u32[]{:S(2)}) collective-permute-start(f32[38,8,128]{2,1,0:T(8,128)S(1)} %get-tuple-element.51), channel_id=1, source_target_pairs={{0,8},{8,16},{16,24},{24,0},{1,9},{9,17},{17,25},{25,1},{2,10},{10... | collective-permute-start | bytes 466952 | tf_op jit(solution)/shard_map/ppermute | solution.py:617
  20.6 2.9 %collective-permute-start.8 = (f32[38,8,128]{2,1,0:T(8,128)S(1)}, f32[38,8,128]{2,1,0:T(8,128)S(1)}, u32[]{:S(2)}, u32[]{:S(2)}) collective-permute-start(f32[38,8,128]{2,1,0:T(8,128)S(1)} %get-tuple-element.52), channel_id=1, source_target_pairs={{0,24},{8,0},{16,8},{24,16},{1,25},{9,1},{17,9},{25,17},{2,26},{10... | collective-permute-start | bytes 466952 | tf_op jit(solution)/shard_map/ppermute | solution.py:617
  23.9 3.6 %collective-permute-done.9 = f32[8,128]{1,0:T(8,128)S(1)} collective-permute-done((f32[8,128]{1,0:T(8,128)S(1)}, f32[8,128]{1,0:T(8,128)S(1)}, u32[]{:S(2)}, u32[]{:S(2)}) %collective-permute-start.9) | collective-permute-done | bytes 4128 | tf_op jit(solution)/shard_map/ppermute | solution.py:617
  28.0 1.0 %collective-permute-start.10 = (f32[8,128]{1,0:T(8,128)S(1)}, f32[8,128]{1,0:T(8,128)S(1)}, u32[]{:S(2)}, u32[]{:S(2)}) collective-permute-start(f32[8,128]{1,0:T(8,128)S(1)} %add.24), channel_id=1, source_target_pairs={{0,2},{1,3},{2,0},{3,1},{4,6},{5,7},{6,4},{7,5},{8,10},{9,11},{10,... | collective-permute-start | bytes 12296 | tf_op jit(solution)/shard_map/ppermute | solution.py:617
  29.6 1.0 %shard_map.104.early = f32[192,256]{1,0:T(8,128)S(1)} custom-call(f32[3,2,16,128]{3,2,1,0:T(8,128)S(1)} %get-tuple-element.60.v0, f32[3,2,16,128]{3,2,1,0:T(8,128)S(1)} %get-tuple-element.61.v1, s32[2,16,128]{2,1,0:T(8,128)S(1)} %copy-done, bf16[256,4096]{1,0:T(8,128)(2,1)S(1)} %shard_map.103.right), custom_call_target="tpu_custom_call" | custom-call | tf_op jit(solution)/shard_map/pallas_call | solution.py:703
  31.3 1.8 %shard_map.105 = f32[192,256]{1,0:T(8,128)} custom-call(f32[19,2,24,256]{3,2,1,0:T(8,128)S(1)} %get-tuple-element.53.ahead, f32[2,24,256]{2,1,0:T(8,128)S(1)} %get-tuple-element.46.g_ref, f32[2,5,24,256]{3,2,1,0:T(8,128)S(1)} %get-tuple-element.54.side, f32[3,2,16,128]{3,2,1,0:T(8,128)S(1)} %get-tuple-element.59.v2, s32[2,16,128]{2,1,0:T(8,128)S(1)} %copy-done, ...), custom_call_target="tpu_custom_call" | custom-call | tf_op jit(solution)/shard_map/pallas_call | solution.py:706
  33.1 3.4 %all-to-all-start = ((f32[8,24,256]{2,1,0:T(8,128)}), f32[8,24,256]{2,1,0:T(8,128)S(1)}, u32[]{:S(2)}, u32[]{:S(2)}) async-start(f32[8,24,256]{2,1,0:T(8,128)} %bitcast.1), calls=%async_computation | async-start | bytes 393216 | tf_op jit(solution)/shard_map/all_to_all | solution.py:713
  37.0 3.8 %collective-permute-start.14 = (f32[11,8,128]{2,1,0:T(8,128)S(1)}, f32[11,8,128]{2,1,0:T(8,128)S(1)}, u32[]{:S(2)}, u32[]{:S(2)}) collective-permute-start(f32[11,8,128]{2,1,0:T(8,128)S(1)} %get-tuple-element.58), channel_id=1, source_target_pairs={{0,24},{8,0},{16,8},{24,16},{1,25},{9,1},{17,9},{25,17},{2,26},{10... | collective-permute-start | bytes 135176 | tf_op jit(solution)/shard_map/ppermute | solution.py:617
  40.8 1.8 %all-to-all-done = f32[8,24,256]{2,1,0:T(8,128)S(1)} async-done(((f32[8,24,256]{2,1,0:T(8,128)}), f32[8,24,256]{2,1,0:T(8,128)S(1)}, u32[]{:S(2)}, u32[]{:S(2)}) %all-to-all-start) | async-done | bytes 196640 | tf_op jit(solution)/shard_map/all_to_all | solution.py:713
  42.7 1.0 %shard_map.106 = (f32[16,512]{1,0:T(8,128)S(1)}, f32[128,128]{1,0:T(8,128)}) custom-call(f32[192,256]{1,0:T(8,128)S(1)} %bitcast.9, f32[32,512]{1,0:T(8,128)S(1)} %get-tuple-element.62.scaled), custom_call_target="tpu_custom_call" | custom-call | tf_op jit(solution)/shard_map/pallas_call | solution.py:714
  43.7 3.7 %all-to-all-start.1 = ((f32[32,4,128]{2,1,0:T(4,128)}), f32[32,4,128]{2,1,0:T(4,128)S(1)}, u32[]{:S(2)}, u32[]{:S(2)}) async-start(f32[32,4,128]{2,1,0:T(4,128)} %bitcast.3), calls=%async_computation.1 | async-start | bytes 131072 | tf_op jit(solution)/shard_map/all_to_all | solution.py:720
  47.5 2.3 %shard_map.107 = (f32[32,128]{1,0:T(8,128)S(1)}, f32[32,512]{1,0:T(8,128)S(1)}) custom-call(f32[8,128]{1,0:T(8,128)S(1)} %fusion.1.tile, f32[32,512]{1,0:T(8,128)S(1)} %get-tuple-element.62.scaled), custom_call_target="tpu_custom_call" | custom-call | tf_op jit(solution)/shard_map/pallas_call | solution.py:721
  49.7 0.9 %shard_map.102 = f32[19,2,16,128]{3,2,1,0:T(8,128)} custom-call(f32[19,2,24,256]{3,2,1,0:T(8,128)S(1)} %get-tuple-element.56.prev, f32[11,8,128]{2,1,0:T(8,128)S(1)} %collective-permute-done.13.xr, f32[11,8,128]{2,1,0:T(8,128)S(1)} %collective-permute-done.14.xl), custom_call_target="tpu_custom_call" | custom-call | tf_op jit(solution)/shard_map/pallas_call | solution.py:727
  50.6 4.2 %all-to-all-done.1 = f32[32,4,128]{2,1,0:T(4,128)S(1)} async-done(((f32[32,4,128]{2,1,0:T(4,128)}), f32[32,4,128]{2,1,0:T(4,128)S(1)}, u32[]{:S(2)}, u32[]{:S(2)}) %all-to-all-start.1) | async-done | bytes 65568 | tf_op jit(solution)/shard_map/all_to_all | solution.py:720
  54.8 2.3 %shard_map.108 = (f32[44,512]{1,0:T(8,128)}, f32[44,44]{1,0:T(8,128)}) custom-call(f32[128,128]{1,0:T(8,128)S(1)} %bitcast.10, f32[32,128]{1,0:T(8,128)S(1)} %get-tuple-element.64.factor, f32[32,512]{1,0:T(8,128)S(1)} %get-tuple-element.65.head, f32[16,512]{1,0:T(8,128)S(1)} %get-tuple-element.66.snap), custom_call_target="tpu_custom_call" | custom-call | tf_op jit(solution)/shard_map/pallas_call | solution.py:724
  (37 shorter events, 4.3 us)
Async XLA Ops:
  2.0 8.9 %collective-permute-start.2 = (f32[40,8,128]{2,1,0:T(8,128)S(1)}, f32[40,8,128]{2,1,0:T(8,128)S(1)}, u32[]{:S(2)}, u32[]{:S(2)}) collective-permute-start(f32[40,8,128]{2,1,0:T(8,128)S(1)} %get-tuple-element.42), channel_id=1, source_target_pairs={{0,4},{1,5},{2,6},{3,7},{4,0},{5,1},{6,2},{7,3},{8,12},{9,13},{10,... | collective-permute-start | bytes 491528 | tf_op jit(solution)/shard_map/ppermute | solution.py:625
  5.0 4.4 %collective-permute-start = (f32[3,8,128]{2,1,0:T(8,128)S(1)}, f32[3,8,128]{2,1,0:T(8,128)S(1)}, u32[]{:S(2)}, u32[]{:S(2)}) collective-permute-start(f32[3,8,128]{2,1,0:T(8,128)S(1)} %get-tuple-element.38), channel_id=1, source_target_pairs={{0,1},{1,2},{2,3},{3,0},{4,5},{5,6},{6,7},{7,4},{8,9},{9,10},{10,1... | collective-permute-start | bytes 36872 | tf_op jit(solution)/shard_map/ppermute | solution.py:617
  5.0 4.4 %collective-permute-start.1 = (f32[3,8,128]{2,1,0:T(8,128)S(1)}, f32[3,8,128]{2,1,0:T(8,128)S(1)}, u32[]{:S(2)}, u32[]{:S(2)}) collective-permute-start(f32[3,8,128]{2,1,0:T(8,128)S(1)} %get-tuple-element.39), channel_id=1, source_target_pairs={{0,3},{1,0},{2,1},{3,2},{4,7},{5,4},{6,5},{7,6},{8,11},{9,8},{10,9... | collective-permute-start | bytes 36872 | tf_op jit(solution)/shard_map/ppermute | solution.py:617
  6.8 4.0 %collective-permute-start.3 = (f32[2,8,128]{2,1,0:T(8,128)S(1)}, f32[2,8,128]{2,1,0:T(8,128)S(1)}, u32[]{:S(2)}, u32[]{:S(2)}) collective-permute-start(f32[2,8,128]{2,1,0:T(8,128)S(1)} %get-tuple-element.43), channel_id=1, source_target_pairs={{0,5},{1,6},{2,7},{3,4},{4,1},{5,2},{6,3},{7,0},{8,13},{9,14},{10,... | collective-permute-start | bytes 24584 | tf_op jit(solution)/shard_map/ppermute | solution.py:625
  6.8 4.1 %collective-permute-start.4 = (f32[2,8,128]{2,1,0:T(8,128)S(1)}, f32[2,8,128]{2,1,0:T(8,128)S(1)}, u32[]{:S(2)}, u32[]{:S(2)}) collective-permute-start(f32[2,8,128]{2,1,0:T(8,128)S(1)} %get-tuple-element.44), channel_id=1, source_target_pairs={{0,7},{1,4},{2,5},{3,6},{4,3},{5,0},{6,1},{7,2},{8,15},{9,12},{10,... | collective-permute-start | bytes 24584 | tf_op jit(solution)/shard_map/ppermute | solution.py:625
  9.8 13.7 %copy-start.2 = (f32[32]{0:T(128)S(1)}, f32[32]{0:T(128)}, u32[]{:S(2)}) copy-start(f32[32]{0:T(128)} %param.13) | copy-start | bytes 388
  9.8 13.7 %copy-start.1 = (f32[32,512]{1,0:T(8,128)S(1)}, f32[32,512]{1,0:T(8,128)}, u32[]{:S(2)}) copy-start(f32[32,512]{1,0:T(8,128)} %basis.1) | copy-start | bytes 196612
  10.8 18.1 %copy-start = (s32[2,16,128]{2,1,0:T(8,128)S(1)}, s32[2,16,128]{2,1,0:T(8,128)}, u32[]{:S(2)}) copy-start(s32[2,16,128]{2,1,0:T(8,128)} %row_map.5) | copy-start | bytes 49156
  11.1 6.4 %collective-permute-start.5 = (f32[16,8,128]{2,1,0:T(8,128)S(1)}, f32[16,8,128]{2,1,0:T(8,128)S(1)}, u32[]{:S(2)}, u32[]{:S(2)}) collective-permute-start(f32[16,8,128]{2,1,0:T(8,128)S(1)} %get-tuple-element.47), channel_id=1, source_target_pairs={{0,8},{8,16},{16,24},{24,0},{1,9},{9,17},{17,25},{25,1},{2,10},{10... | collective-permute-start | bytes 196616 | tf_op jit(solution)/shard_map/ppermute | solution.py:617
  12.8 6.2 %collective-permute-start.6 = (f32[16,8,128]{2,1,0:T(8,128)S(1)}, f32[16,8,128]{2,1,0:T(8,128)S(1)}, u32[]{:S(2)}, u32[]{:S(2)}) collective-permute-start(f32[16,8,128]{2,1,0:T(8,128)S(1)} %get-tuple-element.48), channel_id=1, source_target_pairs={{0,24},{8,0},{16,8},{24,16},{1,25},{9,1},{17,9},{25,17},{2,26},{10... | collective-permute-start | bytes 196616 | tf_op jit(solution)/shard_map/ppermute | solution.py:617
  19.6 11.0 %collective-permute-start.7 = (f32[38,8,128]{2,1,0:T(8,128)S(1)}, f32[38,8,128]{2,1,0:T(8,128)S(1)}, u32[]{:S(2)}, u32[]{:S(2)}) collective-permute-start(f32[38,8,128]{2,1,0:T(8,128)S(1)} %get-tuple-element.51), channel_id=1, source_target_pairs={{0,8},{8,16},{16,24},{24,0},{1,9},{9,17},{17,25},{25,1},{2,10},{10... | collective-permute-start | bytes 466952 | tf_op jit(solution)/shard_map/ppermute | solution.py:617
  20.6 10.0 %collective-permute-start.8 = (f32[38,8,128]{2,1,0:T(8,128)S(1)}, f32[38,8,128]{2,1,0:T(8,128)S(1)}, u32[]{:S(2)}, u32[]{:S(2)}) collective-permute-start(f32[38,8,128]{2,1,0:T(8,128)S(1)} %get-tuple-element.52), channel_id=1, source_target_pairs={{0,24},{8,0},{16,8},{24,16},{1,25},{9,1},{17,9},{25,17},{2,26},{10... | collective-permute-start | bytes 466952 | tf_op jit(solution)/shard_map/ppermute | solution.py:617
  23.9 3.6 %collective-permute-start.9 = (f32[8,128]{1,0:T(8,128)S(1)}, f32[8,128]{1,0:T(8,128)S(1)}, u32[]{:S(2)}, u32[]{:S(2)}) collective-permute-start(f32[8,128]{1,0:T(8,128)S(1)} %get-tuple-element.55), channel_id=1, source_target_pairs={{0,4},{4,0},{1,5},{5,1},{2,6},{6,2},{3,7},{7,3},{8,12},{12,8},{9,1... | collective-permute-start | bytes 12296 | tf_op jit(solution)/shard_map/ppermute | solution.py:617
  27.5 9.0 %collective-permute-start.12 = (f32[8,128]{1,0:T(8,128)S(1)}, f32[8,128]{1,0:T(8,128)S(1)}, u32[]{:S(2)}, u32[]{:S(2)}) collective-permute-start(f32[8,128]{1,0:T(8,128)S(1)} %add.24), channel_id=1, source_target_pairs={{0,3},{1,0},{2,1},{3,2},{4,7},{5,4},{6,5},{7,6},{8,11},{9,8},{10,9... | collective-permute-start | bytes 12296 | tf_op jit(solution)/shard_map/ppermute | solution.py:617
  27.5 9.0 %collective-permute-start.11 = (f32[8,128]{1,0:T(8,128)S(1)}, f32[8,128]{1,0:T(8,128)S(1)}, u32[]{:S(2)}, u32[]{:S(2)}) collective-permute-start(f32[8,128]{1,0:T(8,128)S(1)} %add.24), channel_id=1, source_target_pairs={{0,1},{1,2},{2,3},{3,0},{4,5},{5,6},{6,7},{7,4},{8,9},{9,10},{10,1... | collective-permute-start | bytes 12296 | tf_op jit(solution)/shard_map/ppermute | solution.py:617
  28.0 8.5 %collective-permute-start.10 = (f32[8,128]{1,0:T(8,128)S(1)}, f32[8,128]{1,0:T(8,128)S(1)}, u32[]{:S(2)}, u32[]{:S(2)}) collective-permute-start(f32[8,128]{1,0:T(8,128)S(1)} %add.24), channel_id=1, source_target_pairs={{0,2},{1,3},{2,0},{3,1},{4,6},{5,7},{6,4},{7,5},{8,10},{9,11},{10,... | collective-permute-start | bytes 12296 | tf_op jit(solution)/shard_map/ppermute | solution.py:617
  33.1 9.5 %all-to-all-start = ((f32[8,24,256]{2,1,0:T(8,128)}), f32[8,24,256]{2,1,0:T(8,128)S(1)}, u32[]{:S(2)}, u32[]{:S(2)}) async-start(f32[8,24,256]{2,1,0:T(8,128)} %bitcast.1), calls=%async_computation | async-start | bytes 393216 | tf_op jit(solution)/shard_map/all_to_all | solution.py:713
  36.9 10.5 %collective-permute-start.13 = (f32[11,8,128]{2,1,0:T(8,128)S(1)}, f32[11,8,128]{2,1,0:T(8,128)S(1)}, u32[]{:S(2)}, u32[]{:S(2)}) collective-permute-start(f32[11,8,128]{2,1,0:T(8,128)S(1)} %get-tuple-element.57), channel_id=1, source_target_pairs={{0,8},{8,16},{16,24},{24,0},{1,9},{9,17},{17,25},{25,1},{2,10},{10... | collective-permute-start | bytes 135176 | tf_op jit(solution)/shard_map/ppermute | solution.py:617
  37.0 10.4 %collective-permute-start.14 = (f32[11,8,128]{2,1,0:T(8,128)S(1)}, f32[11,8,128]{2,1,0:T(8,128)S(1)}, u32[]{:S(2)}, u32[]{:S(2)}) collective-permute-start(f32[11,8,128]{2,1,0:T(8,128)S(1)} %get-tuple-element.58), channel_id=1, source_target_pairs={{0,24},{8,0},{16,8},{24,16},{1,25},{9,1},{17,9},{25,17},{2,26},{10... | collective-permute-start | bytes 135176 | tf_op jit(solution)/shard_map/ppermute | solution.py:617
  40.8 6.6 %collective-permute-start.15 = (f32[8,128]{1,0:T(8,128)S(1)}, f32[8,128]{1,0:T(8,128)S(1)}, u32[]{:S(2)}, u32[]{:S(2)}) collective-permute-start(f32[8,128]{1,0:T(8,128)S(1)} %add_add_fusion.rider), channel_id=1, source_target_pairs={{0,16},{8,24},{16,0},{24,8},{1,17},{9,25},{17,1},{25,9},{2,18},{10... | collective-permute-start | bytes 12296 | tf_op jit(solution)/shard_map/ppermute | solution.py:617
  43.7 11.1 %all-to-all-start.1 = ((f32[32,4,128]{2,1,0:T(4,128)}), f32[32,4,128]{2,1,0:T(4,128)S(1)}, u32[]{:S(2)}, u32[]{:S(2)}) async-start(f32[32,4,128]{2,1,0:T(4,128)} %bitcast.3), calls=%async_computation.1 | async-start | bytes 131072 | tf_op jit(solution)/shard_map/all_to_all | solution.py:720

commit v6 on v5

--- a/solution.py
+++ b/solution.py
@@ -370,7 +370,7 @@
     pack_deep(ahead, going, g_ref, (xr_ref, xl_ref))
 
 
-def pair_kernel(ahead, going, g_ref, xr, xl, ahead_ref, side_ref, vel_ref, deep, out):
+def pair(ahead, going, g_ref, xr, xl, ahead_ref, side_ref, vel_ref, deep, out):
     take_deep((xr, xl), deep)
 
     def pick(q, x, rows, cols):
@@ -460,6 +460,13 @@
             out[pl.ds(12 * h + 6 + j, 1), :] = jnp.zeros((1, LOW), jnp.float32)
 
 
+def pair_late_kernel(
+    ahead, going, g_ref, xr, xl, row_map, right, early, ahead_ref, side_ref, out, deep, relaxed, v2, v3, left
+):
+    pair(ahead, going, g_ref, xr, xl, ahead_ref, side_ref, v2, deep, relaxed)
+    late(ahead_ref, g_ref, side_ref, v2, row_map, right, early, out, left, v3)
+
+
 def old_kernel(total_rows, basis, sigma, scaled_ref, tile_ref, work):
     scaled = basis[...] * sigma[...]
     scaled_ref[...] = scaled
@@ -483,7 +490,7 @@
     )
 
 
-def late_kernel(ahead, g_ref, side, v2, row_map, right, early, out, left, v3):
+def late(ahead, g_ref, side, v2, row_map, right, early, out, left, v3):
     pick = chooser(ahead, side)
     for x in range(2):
         for yt in range(2):
@@ -690,26 +697,24 @@
     xr, xl = shift(xr, "gx", 1), shift(xl, "gx", -1)
     if small:
         own = (own + shift(own, "gz", 2)) + (shift(own, "gz", 1) + shift(own, "gz", -1))
-    ahead, faces, v2 = call(
-        pair_kernel, (big, sides, vel), (pltpu.VMEM((2, DEEP, 24, 256), jnp.float32), wide), count=5
-    )(*map(held, (ahead, going, g_wide, xr, xl)))
+    lefts = pltpu.VMEM((12 * highs, cells), jnp.bfloat16)
+    early = call(early_kernel, vmem(12 * highs, LOW), (lefts,), count=4, limit=12 + highs // 2)(
+        held(v0), held(v1), row_map, held(onehot)
+    )
+    small_vel = pltpu.VMEM((3, 2, 16, 128), jnp.float32)
+    ahead, faces, term = call(
+        pair_late_kernel,
+        (big, sides, f32(12 * highs, LOW)),
+        (pltpu.VMEM((2, DEEP, 24, 256), jnp.float32), wide, small_vel, small_vel, lefts),
+        count=8,
+        limit=16 + highs // 2,
+    )(*map(held, (ahead, going, g_wide, xr, xl)), row_map, held(onehot), held(early))
     state = tuple(map(held, (ahead, g_wide, faces)))
     relaxed, xr, xl = call(end_step_kernel, (big, loaded, loaded), count=4)(*state, held(own))
     xr, xl = shift(xr, "gx", 1), shift(xl, "gx", -1)
     if small:
         own = (own + shift(own, "gx", 2)) + (xr[10] + xl[10])
 
-    lefts = pltpu.VMEM((12 * highs, cells), jnp.bfloat16)
-    early = call(early_kernel, vmem(12 * highs, LOW), (lefts,), count=4, limit=12 + highs // 2)(
-        held(v0), held(v1), row_map, held(onehot)
-    )
-    term = call(
-        late_kernel,
-        f32(12 * highs, LOW),
-        (lefts, pltpu.VMEM((3, 2, 16, 128), jnp.float32)),
-        count=7,
-        limit=12 + highs // 2,
-    )(*state, held(v2), row_map, held(onehot), held(early))
     parts = lax.all_to_all(term, slab, 0, 0, tiled=True)
     snap, gram = call(
         functools.partial(gram_kernel, float(rows_local * devices)),

time: 57.4 us -> 58.5 us (1.019)
  starting transfers between devices: 27.7 us -> 28.9 us
    ppermute x13, starting transfers between devices: 14.9 us -> 16.1 us  [shift(): lax.ppermute(value, axis, [(i, (i + step) % count) for i in range(count)])]
    pallas_call x2 -> x1, Pallas kernels: 2.46 us -> 2.28 us  [on_device(): call(pair_late_kernel, (big, sides, f32(12 * highs, LOW)), (pltpu.VMEM((2...]
  transfers between devices with their start and end apart: 18 -> 18, of which waited for: 7 -> 7; matrix products, arithmetic and copies ran while one was open for 0% -> 0% of each run, Pallas kernels for 17% -> 16%
where the time goes in v6:
time: 58.5 us; the launch traced here: 58.2 us
  starting transfers between devices  28.9 us (49%)
  waiting for transfers between devices  14.4 us (25%)
  Pallas kernels  13.9 us (24%)
  between operations  0.83 us (1%)
    ppermute x13, starting transfers between devices, shift(): lax.ppermute(value, axis, [(i, (i + step) % count) for i in range(count)])  16.1 us
    ppermute x13, waiting for transfers between devices, shift(): lax.ppermute(value, axis, [(i, (i + step) % count) for i in range(count)])  7.36 us
    ppermute x3, starting transfers between devices, shift_both(): return lax.ppermute(value, ('gy', 'gz'), pairs)  5.71 us
    all_to_all x1, waiting for transfers between devices, on_device(): grams = lax.all_to_all(gram, everyone, 0, 0, tiled=True)  4.23 us
    all_to_all x1, starting transfers between devices, on_device(): grams = lax.all_to_all(gram, everyone, 0, 0, tiled=True)  3.73 us
    all_to_all x1, starting transfers between devices, on_device(): parts = lax.all_to_all(term, slab, 0, 0, tiled=True)  3.39 us
    pallas_call x1, Pallas kernels, on_device(): call(factor_kernel, (f32(44, rows_local), f32(44, 44)), (pltpu.VMEM((16,...  2.32 us
    pallas_call x1, Pallas kernels, on_device(): call(pair_late_kernel, (big, sides, f32(12 * highs, LOW)), (pltpu.VMEM((2...  2.28 us
  transfers between devices with their start and end apart: 18, of which 7 were waited for; matrix products, arithmetic and copies ran while one was open for 0% of the time, Pallas kernels for 16%

profile of v6, /device:TPU:0, one launch (start us, length us, event | category | flops | bytes accessed | tf_op | source)
XLA Modules:
  0.0 58.2 jit_solution(4530898275062893064)
XLA Ops:
  0.6 1.3 %shard_map.94 = (f32[19,2,16,128]{3,2,1,0:T(8,128)S(1)}, f32[2,16,128]{2,1,0:T(8,128)S(1)}, f32[3,8,128]{2,1,0:T(8,128)S(1)}, f32[3,8,128]{2,1,0:T(8,128)S(1)}, ...) custom-call(f32[8]{0:T(128)} %table_hbm.1, f32[19,2,16,128]{3,2,1,0:T(8,128)} %ratio_hbm.1, ...), custom_call_target="tpu_custom_call" | custom-call | tf_op jit(solution)/shard_map/pallas_call | solution.py:652
  2.0 3.1 %collective-permute-start.2 = (f32[40,8,128]{2,1,0:T(8,128)S(1)}, f32[40,8,128]{2,1,0:T(8,128)S(1)}, u32[]{:S(2)}, u32[]{:S(2)}) collective-permute-start(f32[40,8,128]{2,1,0:T(8,128)S(1)} %get-tuple-element.42), channel_id=1, source_target_pairs={{0,4},{1,5},{2,6},{3,7},{4,0},{5,1},{6,2},{7,3},{8,12},{9,13},{10,... | collective-permute-start | bytes 491528 | tf_op jit(solution)/shard_map/ppermute | solution.py:632
  5.0 1.7 %collective-permute-start.1 = (f32[3,8,128]{2,1,0:T(8,128)S(1)}, f32[3,8,128]{2,1,0:T(8,128)S(1)}, u32[]{:S(2)}, u32[]{:S(2)}) collective-permute-start(f32[3,8,128]{2,1,0:T(8,128)S(1)} %get-tuple-element.39), channel_id=1, source_target_pairs={{0,3},{1,0},{2,1},{3,2},{4,7},{5,4},{6,5},{7,6},{8,11},{9,8},{10,9... | collective-permute-start | bytes 36872 | tf_op jit(solution)/shard_map/ppermute | solution.py:624
  6.8 2.6 %collective-permute-start.4 = (f32[2,8,128]{2,1,0:T(8,128)S(1)}, f32[2,8,128]{2,1,0:T(8,128)S(1)}, u32[]{:S(2)}, u32[]{:S(2)}) collective-permute-start(f32[2,8,128]{2,1,0:T(8,128)S(1)} %get-tuple-element.44), channel_id=1, source_target_pairs={{0,7},{1,4},{2,5},{3,6},{4,3},{5,0},{6,1},{7,2},{8,15},{9,12},{10,... | collective-permute-start | bytes 24584 | tf_op jit(solution)/shard_map/ppermute | solution.py:632
  9.8 0.9 %collective-permute-done.3.cr = f32[2,8,128]{2,1,0:T(8,128)S(1)} collective-permute-done((f32[2,8,128]{2,1,0:T(8,128)S(1)}, f32[2,8,128]{2,1,0:T(8,128)S(1)}, u32[]{:S(2)}, u32[]{:S(2)}) %collective-permute-start.3) | collective-permute-done | bytes 8224 | tf_op jit(solution)/shard_map/ppermute | solution.py:632
  11.1 1.6 %collective-permute-start.5 = (f32[16,8,128]{2,1,0:T(8,128)S(1)}, f32[16,8,128]{2,1,0:T(8,128)S(1)}, u32[]{:S(2)}, u32[]{:S(2)}) collective-permute-start(f32[16,8,128]{2,1,0:T(8,128)S(1)} %get-tuple-element.47), channel_id=1, source_target_pairs={{0,8},{8,16},{16,24},{24,0},{1,9},{9,17},{17,25},{25,1},{2,10},{10... | collective-permute-start | bytes 196616 | tf_op jit(solution)/shard_map/ppermute | solution.py:624
  12.8 2.2 %collective-permute-start.6 = (f32[16,8,128]{2,1,0:T(8,128)S(1)}, f32[16,8,128]{2,1,0:T(8,128)S(1)}, u32[]{:S(2)}, u32[]{:S(2)}) collective-permute-start(f32[16,8,128]{2,1,0:T(8,128)S(1)} %get-tuple-element.48), channel_id=1, source_target_pairs={{0,24},{8,0},{16,8},{24,16},{1,25},{9,1},{17,9},{25,17},{2,26},{10... | collective-permute-start | bytes 196616 | tf_op jit(solution)/shard_map/ppermute | solution.py:624
  15.2 2.3 %collective-permute-done.5.xr = f32[16,8,128]{2,1,0:T(8,128)S(1)} collective-permute-done((f32[16,8,128]{2,1,0:T(8,128)S(1)}, f32[16,8,128]{2,1,0:T(8,128)S(1)}, u32[]{:S(2)}, u32[]{:S(2)}) %collective-permute-start.5) | collective-permute-done | bytes 65568 | tf_op jit(solution)/shard_map/ppermute | solution.py:624
  17.5 1.4 %collective-permute-done.6.xl = f32[16,8,128]{2,1,0:T(8,128)S(1)} collective-permute-done((f32[16,8,128]{2,1,0:T(8,128)S(1)}, f32[16,8,128]{2,1,0:T(8,128)S(1)}, u32[]{:S(2)}, u32[]{:S(2)}) %collective-permute-start.6) | collective-permute-done | bytes 65568 | tf_op jit(solution)/shard_map/ppermute | solution.py:624
  19.6 1.0 %collective-permute-start.7 = (f32[38,8,128]{2,1,0:T(8,128)S(1)}, f32[38,8,128]{2,1,0:T(8,128)S(1)}, u32[]{:S(2)}, u32[]{:S(2)}) collective-permute-start(f32[38,8,128]{2,1,0:T(8,128)S(1)} %get-tuple-element.51), channel_id=1, source_target_pairs={{0,8},{8,16},{16,24},{24,0},{1,9},{9,17},{17,25},{25,1},{2,10},{10... | collective-permute-start | bytes 466952 | tf_op jit(solution)/shard_map/ppermute | solution.py:624
  20.6 2.9 %collective-permute-start.8 = (f32[38,8,128]{2,1,0:T(8,128)S(1)}, f32[38,8,128]{2,1,0:T(8,128)S(1)}, u32[]{:S(2)}, u32[]{:S(2)}) collective-permute-start(f32[38,8,128]{2,1,0:T(8,128)S(1)} %get-tuple-element.52), channel_id=1, source_target_pairs={{0,24},{8,0},{16,8},{24,16},{1,25},{9,1},{17,9},{25,17},{2,26},{10... | collective-permute-start | bytes 466952 | tf_op jit(solution)/shard_map/ppermute | solution.py:624
  23.9 3.6 %collective-permute-done.9 = f32[8,128]{1,0:T(8,128)S(1)} collective-permute-done((f32[8,128]{1,0:T(8,128)S(1)}, f32[8,128]{1,0:T(8,128)S(1)}, u32[]{:S(2)}, u32[]{:S(2)}) %collective-permute-start.9) | collective-permute-done | bytes 4128 | tf_op jit(solution)/shard_map/ppermute | solution.py:624
  27.5 1.0 %collective-permute-start.10 = (f32[8,128]{1,0:T(8,128)S(1)}, f32[8,128]{1,0:T(8,128)S(1)}, u32[]{:S(2)}, u32[]{:S(2)}) collective-permute-start(f32[8,128]{1,0:T(8,128)S(1)} %add.24), channel_id=1, source_target_pairs={{0,2},{1,3},{2,0},{3,1},{4,6},{5,7},{6,4},{7,5},{8,10},{9,11},{10,... | collective-permute-start | bytes 12296 | tf_op jit(solution)/shard_map/ppermute | solution.py:624
  28.5 1.7 %collective-permute-start.12 = (f32[8,128]{1,0:T(8,128)S(1)}, f32[8,128]{1,0:T(8,128)S(1)}, u32[]{:S(2)}, u32[]{:S(2)}) collective-permute-start(f32[8,128]{1,0:T(8,128)S(1)} %add.24), channel_id=1, source_target_pairs={{0,3},{1,0},{2,1},{3,2},{4,7},{5,4},{6,5},{7,6},{8,11},{9,8},{10,9... | collective-permute-start | bytes 12296 | tf_op jit(solution)/shard_map/ppermute | solution.py:624
  30.9 1.0 %shard_map.100.early = f32[192,256]{1,0:T(8,128)S(1)} custom-call(f32[3,2,16,128]{3,2,1,0:T(8,128)S(1)} %get-tuple-element.53.v0, f32[3,2,16,128]{3,2,1,0:T(8,128)S(1)} %get-tuple-element.54.v1, s32[2,16,128]{2,1,0:T(8,128)S(1)} %copy-done, bf16[256,4096]{1,0:T(8,128)(2,1)S(1)} %shard_map.99.right), custom_call_target="tpu_custom_call" | custom-call | tf_op jit(solution)/shard_map/pallas_call | solution.py:701
  31.9 2.3 %shard_map.101 = (f32[19,2,24,256]{3,2,1,0:T(8,128)S(1)}, f32[2,5,24,256]{3,2,1,0:T(8,128)S(1)}, f32[192,256]{1,0:T(8,128)}) custom-call(f32[19,2,24,256]{3,2,1,0:T(8,128)S(1)} %get-tuple-element.49.ahead, f32[2,5,24,256]{3,2,1,0:T(8,128)S(1)} %get-tuple-element.50.going, f32[2,24,256]{2,1,0:T(8,128)S(1)} %get-tuple-element.46.g_ref, ...), custom_call_target="tpu_custom_call" | custom-call | tf_op jit(solution)/shard_map/pallas_call | solution.py:705
  34.2 3.4 %all-to-all-start = ((f32[8,24,256]{2,1,0:T(8,128)}), f32[8,24,256]{2,1,0:T(8,128)S(1)}, u32[]{:S(2)}, u32[]{:S(2)}) async-start(f32[8,24,256]{2,1,0:T(8,128)} %bitcast.1), calls=%async_computation | async-start | bytes 393216 | tf_op jit(solution)/shard_map/all_to_all | solution.py:718
  38.0 3.8 %collective-permute-start.14 = (f32[11,8,128]{2,1,0:T(8,128)S(1)}, f32[11,8,128]{2,1,0:T(8,128)S(1)}, u32[]{:S(2)}, u32[]{:S(2)}) collective-permute-start(f32[11,8,128]{2,1,0:T(8,128)S(1)} %get-tuple-element.60), channel_id=1, source_target_pairs={{0,24},{8,0},{16,8},{24,16},{1,25},{9,1},{17,9},{25,17},{2,26},{10... | collective-permute-start | bytes 135176 | tf_op jit(solution)/shard_map/ppermute | solution.py:624
  41.9 1.8 %all-to-all-done = f32[8,24,256]{2,1,0:T(8,128)S(1)} async-done(((f32[8,24,256]{2,1,0:T(8,128)}), f32[8,24,256]{2,1,0:T(8,128)S(1)}, u32[]{:S(2)}, u32[]{:S(2)}) %all-to-all-start) | async-done | bytes 196640 | tf_op jit(solution)/shard_map/all_to_all | solution.py:718
  43.7 1.0 %shard_map.105 = (f32[16,512]{1,0:T(8,128)S(1)}, f32[128,128]{1,0:T(8,128)}) custom-call(f32[192,256]{1,0:T(8,128)S(1)} %bitcast.9, f32[32,512]{1,0:T(8,128)S(1)} %get-tuple-element.62.scaled), custom_call_target="tpu_custom_call" | custom-call | tf_op jit(solution)/shard_map/pallas_call | solution.py:719
  44.7 3.7 %all-to-all-start.1 = ((f32[32,4,128]{2,1,0:T(4,128)}), f32[32,4,128]{2,1,0:T(4,128)S(1)}, u32[]{:S(2)}, u32[]{:S(2)}) async-start(f32[32,4,128]{2,1,0:T(4,128)} %bitcast.3), calls=%async_computation.1 | async-start | bytes 131072 | tf_op jit(solution)/shard_map/all_to_all | solution.py:725
  48.5 2.3 %shard_map.106 = (f32[32,128]{1,0:T(8,128)S(1)}, f32[32,512]{1,0:T(8,128)S(1)}) custom-call(f32[8,128]{1,0:T(8,128)S(1)} %fusion.1.tile, f32[32,512]{1,0:T(8,128)S(1)} %get-tuple-element.62.scaled), custom_call_target="tpu_custom_call" | custom-call | tf_op jit(solution)/shard_map/pallas_call | solution.py:726
  51.6 4.2 %all-to-all-done.1 = f32[32,4,128]{2,1,0:T(4,128)S(1)} async-done(((f32[32,4,128]{2,1,0:T(4,128)}), f32[32,4,128]{2,1,0:T(4,128)S(1)}, u32[]{:S(2)}, u32[]{:S(2)}) %all-to-all-start.1) | async-done | bytes 65568 | tf_op jit(solution)/shard_map/all_to_all | solution.py:725
  55.9 2.3 %shard_map.107 = (f32[44,512]{1,0:T(8,128)}, f32[44,44]{1,0:T(8,128)}) custom-call(f32[128,128]{1,0:T(8,128)S(1)} %bitcast.10, f32[32,128]{1,0:T(8,128)S(1)} %get-tuple-element.64.factor, f32[32,512]{1,0:T(8,128)S(1)} %get-tuple-element.65.head, f32[16,512]{1,0:T(8,128)S(1)} %get-tuple-element.66.snap), custom_call_target="tpu_custom_call" | custom-call | tf_op jit(solution)/shard_map/pallas_call | solution.py:729
  (36 shorter events, 4.0 us)
Async XLA Ops:
  2.0 8.9 %collective-permute-start.2 = (f32[40,8,128]{2,1,0:T(8,128)S(1)}, f32[40,8,128]{2,1,0:T(8,128)S(1)}, u32[]{:S(2)}, u32[]{:S(2)}) collective-permute-start(f32[40,8,128]{2,1,0:T(8,128)S(1)} %get-tuple-element.42), channel_id=1, source_target_pairs={{0,4},{1,5},{2,6},{3,7},{4,0},{5,1},{6,2},{7,3},{8,12},{9,13},{10,... | collective-permute-start | bytes 491528 | tf_op jit(solution)/shard_map/ppermute | solution.py:632
  5.0 4.4 %collective-permute-start = (f32[3,8,128]{2,1,0:T(8,128)S(1)}, f32[3,8,128]{2,1,0:T(8,128)S(1)}, u32[]{:S(2)}, u32[]{:S(2)}) collective-permute-start(f32[3,8,128]{2,1,0:T(8,128)S(1)} %get-tuple-element.38), channel_id=1, source_target_pairs={{0,1},{1,2},{2,3},{3,0},{4,5},{5,6},{6,7},{7,4},{8,9},{9,10},{10,1... | collective-permute-start | bytes 36872 | tf_op jit(solution)/shard_map/ppermute | solution.py:624
  5.0 4.4 %collective-permute-start.1 = (f32[3,8,128]{2,1,0:T(8,128)S(1)}, f32[3,8,128]{2,1,0:T(8,128)S(1)}, u32[]{:S(2)}, u32[]{:S(2)}) collective-permute-start(f32[3,8,128]{2,1,0:T(8,128)S(1)} %get-tuple-element.39), channel_id=1, source_target_pairs={{0,3},{1,0},{2,1},{3,2},{4,7},{5,4},{6,5},{7,6},{8,11},{9,8},{10,9... | collective-permute-start | bytes 36872 | tf_op jit(solution)/shard_map/ppermute | solution.py:624
  6.8 4.0 %collective-permute-start.3 = (f32[2,8,128]{2,1,0:T(8,128)S(1)}, f32[2,8,128]{2,1,0:T(8,128)S(1)}, u32[]{:S(2)}, u32[]{:S(2)}) collective-permute-start(f32[2,8,128]{2,1,0:T(8,128)S(1)} %get-tuple-element.43), channel_id=1, source_target_pairs={{0,5},{1,6},{2,7},{3,4},{4,1},{5,2},{6,3},{7,0},{8,13},{9,14},{10,... | collective-permute-start | bytes 24584 | tf_op jit(solution)/shard_map/ppermute | solution.py:632
  6.8 4.1 %collective-permute-start.4 = (f32[2,8,128]{2,1,0:T(8,128)S(1)}, f32[2,8,128]{2,1,0:T(8,128)S(1)}, u32[]{:S(2)}, u32[]{:S(2)}) collective-permute-start(f32[2,8,128]{2,1,0:T(8,128)S(1)} %get-tuple-element.44), channel_id=1, source_target_pairs={{0,7},{1,4},{2,5},{3,6},{4,3},{5,0},{6,1},{7,2},{8,15},{9,12},{10,... | collective-permute-start | bytes 24584 | tf_op jit(solution)/shard_map/ppermute | solution.py:632
  9.8 13.7 %copy-start.2 = (f32[32]{0:T(128)S(1)}, f32[32]{0:T(128)}, u32[]{:S(2)}) copy-start(f32[32]{0:T(128)} %param.13) | copy-start | bytes 388
  9.8 13.7 %copy-start.1 = (f32[32,512]{1,0:T(8,128)S(1)}, f32[32,512]{1,0:T(8,128)}, u32[]{:S(2)}) copy-start(f32[32,512]{1,0:T(8,128)} %basis.1) | copy-start | bytes 196612
  10.8 19.4 %copy-start = (s32[2,16,128]{2,1,0:T(8,128)S(1)}, s32[2,16,128]{2,1,0:T(8,128)}, u32[]{:S(2)}) copy-start(s32[2,16,128]{2,1,0:T(8,128)} %row_map.5) | copy-start | bytes 49156
  11.1 6.4 %collective-permute-start.5 = (f32[16,8,128]{2,1,0:T(8,128)S(1)}, f32[16,8,128]{2,1,0:T(8,128)S(1)}, u32[]{:S(2)}, u32[]{:S(2)}) collective-permute-start(f32[16,8,128]{2,1,0:T(8,128)S(1)} %get-tuple-element.47), channel_id=1, source_target_pairs={{0,8},{8,16},{16,24},{24,0},{1,9},{9,17},{17,25},{25,1},{2,10},{10... | collective-permute-start | bytes 196616 | tf_op jit(solution)/shard_map/ppermute | solution.py:624
  12.8 6.2 %collective-permute-start.6 = (f32[16,8,128]{2,1,0:T(8,128)S(1)}, f32[16,8,128]{2,1,0:T(8,128)S(1)}, u32[]{:S(2)}, u32[]{:S(2)}) collective-permute-start(f32[16,8,128]{2,1,0:T(8,128)S(1)} %get-tuple-element.48), channel_id=1, source_target_pairs={{0,24},{8,0},{16,8},{24,16},{1,25},{9,1},{17,9},{25,17},{2,26},{10... | collective-permute-start | bytes 196616 | tf_op jit(solution)/shard_map/ppermute | solution.py:624
  19.6 12.3 %collective-permute-start.7 = (f32[38,8,128]{2,1,0:T(8,128)S(1)}, f32[38,8,128]{2,1,0:T(8,128)S(1)}, u32[]{:S(2)}, u32[]{:S(2)}) collective-permute-start(f32[38,8,128]{2,1,0:T(8,128)S(1)} %get-tuple-element.51), channel_id=1, source_target_pairs={{0,8},{8,16},{16,24},{24,0},{1,9},{9,17},{17,25},{25,1},{2,10},{10... | collective-permute-start | bytes 466952 | tf_op jit(solution)/shard_map/ppermute | solution.py:624
  20.6 11.3 %collective-permute-start.8 = (f32[38,8,128]{2,1,0:T(8,128)S(1)}, f32[38,8,128]{2,1,0:T(8,128)S(1)}, u32[]{:S(2)}, u32[]{:S(2)}) collective-permute-start(f32[38,8,128]{2,1,0:T(8,128)S(1)} %get-tuple-element.52), channel_id=1, source_target_pairs={{0,24},{8,0},{16,8},{24,16},{1,25},{9,1},{17,9},{25,17},{2,26},{10... | collective-permute-start | bytes 466952 | tf_op jit(solution)/shard_map/ppermute | solution.py:624
  23.9 3.6 %collective-permute-start.9 = (f32[8,128]{1,0:T(8,128)S(1)}, f32[8,128]{1,0:T(8,128)S(1)}, u32[]{:S(2)}, u32[]{:S(2)}) collective-permute-start(f32[8,128]{1,0:T(8,128)S(1)} %get-tuple-element.57), channel_id=1, source_target_pairs={{0,4},{4,0},{1,5},{5,1},{2,6},{6,2},{3,7},{7,3},{8,12},{12,8},{9,1... | collective-permute-start | bytes 12296 | tf_op jit(solution)/shard_map/ppermute | solution.py:624
  27.5 10.0 %collective-permute-start.10 = (f32[8,128]{1,0:T(8,128)S(1)}, f32[8,128]{1,0:T(8,128)S(1)}, u32[]{:S(2)}, u32[]{:S(2)}) collective-permute-start(f32[8,128]{1,0:T(8,128)S(1)} %add.24), channel_id=1, source_target_pairs={{0,2},{1,3},{2,0},{3,1},{4,6},{5,7},{6,4},{7,5},{8,10},{9,11},{10,... | collective-permute-start | bytes 12296 | tf_op jit(solution)/shard_map/ppermute | solution.py:624
  28.5 9.1 %collective-permute-start.11 = (f32[8,128]{1,0:T(8,128)S(1)}, f32[8,128]{1,0:T(8,128)S(1)}, u32[]{:S(2)}, u32[]{:S(2)}) collective-permute-start(f32[8,128]{1,0:T(8,128)S(1)} %add.24), channel_id=1, source_target_pairs={{0,1},{1,2},{2,3},{3,0},{4,5},{5,6},{6,7},{7,4},{8,9},{9,10},{10,1... | collective-permute-start | bytes 12296 | tf_op jit(solution)/shard_map/ppermute | solution.py:624
  28.5 9.1 %collective-permute-start.12 = (f32[8,128]{1,0:T(8,128)S(1)}, f32[8,128]{1,0:T(8,128)S(1)}, u32[]{:S(2)}, u32[]{:S(2)}) collective-permute-start(f32[8,128]{1,0:T(8,128)S(1)} %add.24), channel_id=1, source_target_pairs={{0,3},{1,0},{2,1},{3,2},{4,7},{5,4},{6,5},{7,6},{8,11},{9,8},{10,9... | collective-permute-start | bytes 12296 | tf_op jit(solution)/shard_map/ppermute | solution.py:624
  34.2 9.5 %all-to-all-start = ((f32[8,24,256]{2,1,0:T(8,128)}), f32[8,24,256]{2,1,0:T(8,128)S(1)}, u32[]{:S(2)}, u32[]{:S(2)}) async-start(f32[8,24,256]{2,1,0:T(8,128)} %bitcast.1), calls=%async_computation | async-start | bytes 393216 | tf_op jit(solution)/shard_map/all_to_all | solution.py:718
  38.0 10.5 %collective-permute-start.13 = (f32[11,8,128]{2,1,0:T(8,128)S(1)}, f32[11,8,128]{2,1,0:T(8,128)S(1)}, u32[]{:S(2)}, u32[]{:S(2)}) collective-permute-start(f32[11,8,128]{2,1,0:T(8,128)S(1)} %get-tuple-element.59), channel_id=1, source_target_pairs={{0,8},{8,16},{16,24},{24,0},{1,9},{9,17},{17,25},{25,1},{2,10},{10... | collective-permute-start | bytes 135176 | tf_op jit(solution)/shard_map/ppermute | solution.py:624
  38.0 10.5 %collective-permute-start.14 = (f32[11,8,128]{2,1,0:T(8,128)S(1)}, f32[11,8,128]{2,1,0:T(8,128)S(1)}, u32[]{:S(2)}, u32[]{:S(2)}) collective-permute-start(f32[11,8,128]{2,1,0:T(8,128)S(1)} %get-tuple-element.60), channel_id=1, source_target_pairs={{0,24},{8,0},{16,8},{24,16},{1,25},{9,1},{17,9},{25,17},{2,26},{10... | collective-permute-start | bytes 135176 | tf_op jit(solution)/shard_map/ppermute | solution.py:624
  41.8 6.6 %collective-permute-start.15 = (f32[8,128]{1,0:T(8,128)S(1)}, f32[8,128]{1,0:T(8,128)S(1)}, u32[]{:S(2)}, u32[]{:S(2)}) collective-permute-start(f32[8,128]{1,0:T(8,128)S(1)} %add_add_fusion.rider), channel_id=1, source_target_pairs={{0,16},{8,24},{16,0},{24,8},{1,17},{9,25},{17,1},{25,9},{2,18},{10... | collective-permute-start | bytes 12296 | tf_op jit(solution)/shard_map/ppermute | solution.py:624
  44.7 11.1 %all-to-all-start.1 = ((f32[32,4,128]{2,1,0:T(4,128)}), f32[32,4,128]{2,1,0:T(4,128)S(1)}, u32[]{:S(2)}, u32[]{:S(2)}) async-start(f32[32,4,128]{2,1,0:T(4,128)} %bitcast.3), calls=%async_computation.1 | async-start | bytes 131072 | tf_op jit(solution)/shard_map/all_to_all | solution.py:725

commit v7 on v6

--- a/solution.py
+++ b/solution.py
@@ -184,7 +184,7 @@
 
 STILL = [q for q in range(19) if LATTICE[q, 0] == 0]
 DEEP = 14
-DEEP_TILES = 38
+DEEP_TILES = 37
 
 
 def still_sums(pops):
@@ -203,7 +203,7 @@
     lane, sub = lanes(), subs()
     for side, ref in enumerate(refs):
         x = 1 - side
-        edges = [jnp.zeros((8, 128), jnp.float32)] * 3
+        edges = [jnp.zeros((8, 128), jnp.float32)] * 2
         directions = (PLUS_X, MINUS_X)[side]
 
         def entries(yt, lt):
@@ -214,9 +214,9 @@
             return tiles + [g_ref[x, at[0], at[1]]]
 
         def edge(j, tile):
-            at, k = divmod(j, 16)
-            here = (lane >= 8 * k) & (lane < 8 * k + 8)
-            edges[at] = jnp.where(here, roll(tile, 4 + 8 * k, 1), edges[at])
+            at, k = divmod(j, 32)
+            here = (lane >= 4 * k) & (lane < 4 * k + 4)
+            edges[at] = jnp.where(here, roll(tile, 2 + 4 * k, 1), edges[at])
 
         for yt in range(2):
             for e, (inner, outer) in enumerate(zip(entries(yt, 0), entries(yt, 1))):
@@ -227,7 +227,7 @@
             pair = [jnp.where(sub < 4, roll(h[e], 2, 0), roll(h[e + 1], 6, 0)) for h in halos]
             ref[28 + e // 2] = pair[0]
             edge(28 + e // 2, pair[1])
-        for at in range(3):
+        for at in range(2):
             ref[35 + at] = edges[at]
 
 
@@ -235,7 +235,7 @@
     for side, ref in enumerate(refs):
 
         def edge(j):
-            return roll(ref[35 + j // 16], -(8 * (j % 16) + 4), 1)
+            return roll(ref[35 + j // 32], -(4 * (j % 32) + 2), 1)
 
         for e in range(DEEP):
             back = -2 if e % 2 == 0 else -6

time: 58.5 us -> 58.5 us (level)
  no operation moved by 1% of the time
where the time goes in v7:
time: 58.5 us; the launch traced here: 58.3 us
  starting transfers between devices  28.9 us (49%)
  waiting for transfers between devices  14.4 us (25%)
  Pallas kernels  14 us (24%)
  between operations  0.83 us (1%)
    ppermute x13, starting transfers between devices, shift(): lax.ppermute(value, axis, [(i, (i + step) % count) for i in range(count)])  16.1 us
    ppermute x13, waiting for transfers between devices, shift(): lax.ppermute(value, axis, [(i, (i + step) % count) for i in range(count)])  7.36 us
    ppermute x3, starting transfers between devices, shift_both(): return lax.ppermute(value, ('gy', 'gz'), pairs)  5.71 us
    all_to_all x1, waiting for transfers between devices, on_device(): grams = lax.all_to_all(gram, everyone, 0, 0, tiled=True)  4.23 us
    all_to_all x1, starting transfers between devices, on_device(): grams = lax.all_to_all(gram, everyone, 0, 0, tiled=True)  3.73 us
    all_to_all x1, starting transfers between devices, on_device(): parts = lax.all_to_all(term, slab, 0, 0, tiled=True)  3.39 us
    pallas_call x1, Pallas kernels, on_device(): call(factor_kernel, (f32(44, rows_local), f32(44, 44)), (pltpu.VMEM((16,...  2.32 us
    pallas_call x1, Pallas kernels, on_device(): call(pair_late_kernel, (big, sides, f32(12 * highs, LOW)), (pltpu.VMEM((2...  2.3 us
  transfers between devices with their start and end apart: 18, of which 7 were waited for; matrix products, arithmetic and copies ran while one was open for 0% of the time, Pallas kernels for 16%

profile of v7, /device:TPU:0, one launch (start us, length us, event | category | flops | bytes accessed | tf_op | source)
XLA Modules:
  0.0 58.3 jit_solution(10100958313272110656)
XLA Ops:
  0.6 1.3 %shard_map.94 = (f32[19,2,16,128]{3,2,1,0:T(8,128)S(1)}, f32[2,16,128]{2,1,0:T(8,128)S(1)}, f32[3,8,128]{2,1,0:T(8,128)S(1)}, f32[3,8,128]{2,1,0:T(8,128)S(1)}, ...) custom-call(f32[8]{0:T(128)} %table_hbm.1, f32[19,2,16,128]{3,2,1,0:T(8,128)} %ratio_hbm.1, ...), custom_call_target="tpu_custom_call" | custom-call | tf_op jit(solution)/shard_map/pallas_call | solution.py:652
  2.0 3.1 %collective-permute-start.2 = (f32[40,8,128]{2,1,0:T(8,128)S(1)}, f32[40,8,128]{2,1,0:T(8,128)S(1)}, u32[]{:S(2)}, u32[]{:S(2)}) collective-permute-start(f32[40,8,128]{2,1,0:T(8,128)S(1)} %get-tuple-element.42), channel_id=1, source_target_pairs={{0,4},{1,5},{2,6},{3,7},{4,0},{5,1},{6,2},{7,3},{8,12},{9,13},{10,... | collective-permute-start | bytes 491528 | tf_op jit(solution)/shard_map/ppermute | solution.py:632
  5.0 1.7 %collective-permute-start.1 = (f32[3,8,128]{2,1,0:T(8,128)S(1)}, f32[3,8,128]{2,1,0:T(8,128)S(1)}, u32[]{:S(2)}, u32[]{:S(2)}) collective-permute-start(f32[3,8,128]{2,1,0:T(8,128)S(1)} %get-tuple-element.39), channel_id=1, source_target_pairs={{0,3},{1,0},{2,1},{3,2},{4,7},{5,4},{6,5},{7,6},{8,11},{9,8},{10,9... | collective-permute-start | bytes 36872 | tf_op jit(solution)/shard_map/ppermute | solution.py:624
  6.8 2.6 %collective-permute-start.4 = (f32[2,8,128]{2,1,0:T(8,128)S(1)}, f32[2,8,128]{2,1,0:T(8,128)S(1)}, u32[]{:S(2)}, u32[]{:S(2)}) collective-permute-start(f32[2,8,128]{2,1,0:T(8,128)S(1)} %get-tuple-element.44), channel_id=1, source_target_pairs={{0,7},{1,4},{2,5},{3,6},{4,3},{5,0},{6,1},{7,2},{8,15},{9,12},{10,... | collective-permute-start | bytes 24584 | tf_op jit(solution)/shard_map/ppermute | solution.py:632
  9.8 0.9 %collective-permute-done.3.cr = f32[2,8,128]{2,1,0:T(8,128)S(1)} collective-permute-done((f32[2,8,128]{2,1,0:T(8,128)S(1)}, f32[2,8,128]{2,1,0:T(8,128)S(1)}, u32[]{:S(2)}, u32[]{:S(2)}) %collective-permute-start.3) | collective-permute-done | bytes 8224 | tf_op jit(solution)/shard_map/ppermute | solution.py:632
  11.1 1.6 %collective-permute-start.5 = (f32[16,8,128]{2,1,0:T(8,128)S(1)}, f32[16,8,128]{2,1,0:T(8,128)S(1)}, u32[]{:S(2)}, u32[]{:S(2)}) collective-permute-start(f32[16,8,128]{2,1,0:T(8,128)S(1)} %get-tuple-element.47), channel_id=1, source_target_pairs={{0,8},{8,16},{16,24},{24,0},{1,9},{9,17},{17,25},{25,1},{2,10},{10... | collective-permute-start | bytes 196616 | tf_op jit(solution)/shard_map/ppermute | solution.py:624
  12.8 2.2 %collective-permute-start.6 = (f32[16,8,128]{2,1,0:T(8,128)S(1)}, f32[16,8,128]{2,1,0:T(8,128)S(1)}, u32[]{:S(2)}, u32[]{:S(2)}) collective-permute-start(f32[16,8,128]{2,1,0:T(8,128)S(1)} %get-tuple-element.48), channel_id=1, source_target_pairs={{0,24},{8,0},{16,8},{24,16},{1,25},{9,1},{17,9},{25,17},{2,26},{10... | collective-permute-start | bytes 196616 | tf_op jit(solution)/shard_map/ppermute | solution.py:624
  15.2 2.3 %collective-permute-done.5.xr = f32[16,8,128]{2,1,0:T(8,128)S(1)} collective-permute-done((f32[16,8,128]{2,1,0:T(8,128)S(1)}, f32[16,8,128]{2,1,0:T(8,128)S(1)}, u32[]{:S(2)}, u32[]{:S(2)}) %collective-permute-start.5) | collective-permute-done | bytes 65568 | tf_op jit(solution)/shard_map/ppermute | solution.py:624
  17.5 1.4 %collective-permute-done.6.xl = f32[16,8,128]{2,1,0:T(8,128)S(1)} collective-permute-done((f32[16,8,128]{2,1,0:T(8,128)S(1)}, f32[16,8,128]{2,1,0:T(8,128)S(1)}, u32[]{:S(2)}, u32[]{:S(2)}) %collective-permute-start.6) | collective-permute-done | bytes 65568 | tf_op jit(solution)/shard_map/ppermute | solution.py:624
  19.6 1.0 %collective-permute-start.7 = (f32[37,8,128]{2,1,0:T(8,128)S(1)}, f32[37,8,128]{2,1,0:T(8,128)S(1)}, u32[]{:S(2)}, u32[]{:S(2)}) collective-permute-start(f32[37,8,128]{2,1,0:T(8,128)S(1)} %get-tuple-element.51), channel_id=1, source_target_pairs={{0,8},{8,16},{16,24},{24,0},{1,9},{9,17},{17,25},{25,1},{2,10},{10... | collective-permute-start | bytes 454664 | tf_op jit(solution)/shard_map/ppermute | solution.py:624
  20.6 2.9 %collective-permute-start.8 = (f32[37,8,128]{2,1,0:T(8,128)S(1)}, f32[37,8,128]{2,1,0:T(8,128)S(1)}, u32[]{:S(2)}, u32[]{:S(2)}) collective-permute-start(f32[37,8,128]{2,1,0:T(8,128)S(1)} %get-tuple-element.52), channel_id=1, source_target_pairs={{0,24},{8,0},{16,8},{24,16},{1,25},{9,1},{17,9},{25,17},{2,26},{10... | collective-permute-start | bytes 454664 | tf_op jit(solution)/shard_map/ppermute | solution.py:624
  23.9 3.6 %collective-permute-done.9 = f32[8,128]{1,0:T(8,128)S(1)} collective-permute-done((f32[8,128]{1,0:T(8,128)S(1)}, f32[8,128]{1,0:T(8,128)S(1)}, u32[]{:S(2)}, u32[]{:S(2)}) %collective-permute-start.9) | collective-permute-done | bytes 4128 | tf_op jit(solution)/shard_map/ppermute | solution.py:624
  27.5 1.0 %collective-permute-start.10 = (f32[8,128]{1,0:T(8,128)S(1)}, f32[8,128]{1,0:T(8,128)S(1)}, u32[]{:S(2)}, u32[]{:S(2)}) collective-permute-start(f32[8,128]{1,0:T(8,128)S(1)} %add.24), channel_id=1, source_target_pairs={{0,2},{1,3},{2,0},{3,1},{4,6},{5,7},{6,4},{7,5},{8,10},{9,11},{10,... | collective-permute-start | bytes 12296 | tf_op jit(solution)/shard_map/ppermute | solution.py:624
  28.5 1.7 %collective-permute-start.12 = (f32[8,128]{1,0:T(8,128)S(1)}, f32[8,128]{1,0:T(8,128)S(1)}, u32[]{:S(2)}, u32[]{:S(2)}) collective-permute-start(f32[8,128]{1,0:T(8,128)S(1)} %add.24), channel_id=1, source_target_pairs={{0,3},{1,0},{2,1},{3,2},{4,7},{5,4},{6,5},{7,6},{8,11},{9,8},{10,9... | collective-permute-start | bytes 12296 | tf_op jit(solution)/shard_map/ppermute | solution.py:624
  30.9 1.0 %shard_map.100.early = f32[192,256]{1,0:T(8,128)S(1)} custom-call(f32[3,2,16,128]{3,2,1,0:T(8,128)S(1)} %get-tuple-element.53.v0, f32[3,2,16,128]{3,2,1,0:T(8,128)S(1)} %get-tuple-element.54.v1, s32[2,16,128]{2,1,0:T(8,128)S(1)} %copy-done, bf16[256,4096]{1,0:T(8,128)(2,1)S(1)} %shard_map.99.right), custom_call_target="tpu_custom_call" | custom-call | tf_op jit(solution)/shard_map/pallas_call | solution.py:701
  31.9 2.3 %shard_map.101 = (f32[19,2,24,256]{3,2,1,0:T(8,128)S(1)}, f32[2,5,24,256]{3,2,1,0:T(8,128)S(1)}, f32[192,256]{1,0:T(8,128)}) custom-call(f32[19,2,24,256]{3,2,1,0:T(8,128)S(1)} %get-tuple-element.49.ahead, f32[2,5,24,256]{3,2,1,0:T(8,128)S(1)} %get-tuple-element.50.going, f32[2,24,256]{2,1,0:T(8,128)S(1)} %get-tuple-element.46.g_ref, ...), custom_call_target="tpu_custom_call" | custom-call | tf_op jit(solution)/shard_map/pallas_call | solution.py:705
  34.2 3.4 %all-to-all-start = ((f32[8,24,256]{2,1,0:T(8,128)}), f32[8,24,256]{2,1,0:T(8,128)S(1)}, u32[]{:S(2)}, u32[]{:S(2)}) async-start(f32[8,24,256]{2,1,0:T(8,128)} %bitcast.1), calls=%async_computation | async-start | bytes 393216 | tf_op jit(solution)/shard_map/all_to_all | solution.py:718
  38.1 3.8 %collective-permute-start.14 = (f32[11,8,128]{2,1,0:T(8,128)S(1)}, f32[11,8,128]{2,1,0:T(8,128)S(1)}, u32[]{:S(2)}, u32[]{:S(2)}) collective-permute-start(f32[11,8,128]{2,1,0:T(8,128)S(1)} %get-tuple-element.60), channel_id=1, source_target_pairs={{0,24},{8,0},{16,8},{24,16},{1,25},{9,1},{17,9},{25,17},{2,26},{10... | collective-permute-start | bytes 135176 | tf_op jit(solution)/shard_map/ppermute | solution.py:624
  41.9 1.8 %all-to-all-done = f32[8,24,256]{2,1,0:T(8,128)S(1)} async-done(((f32[8,24,256]{2,1,0:T(8,128)}), f32[8,24,256]{2,1,0:T(8,128)S(1)}, u32[]{:S(2)}, u32[]{:S(2)}) %all-to-all-start) | async-done | bytes 196640 | tf_op jit(solution)/shard_map/all_to_all | solution.py:718
  43.8 1.0 %shard_map.105 = (f32[16,512]{1,0:T(8,128)S(1)}, f32[128,128]{1,0:T(8,128)}) custom-call(f32[192,256]{1,0:T(8,128)S(1)} %bitcast.9, f32[32,512]{1,0:T(8,128)S(1)} %get-tuple-element.62.scaled), custom_call_target="tpu_custom_call" | custom-call | tf_op jit(solution)/shard_map/pallas_call | solution.py:719
  44.8 3.7 %all-to-all-start.1 = ((f32[32,4,128]{2,1,0:T(4,128)}), f32[32,4,128]{2,1,0:T(4,128)S(1)}, u32[]{:S(2)}, u32[]{:S(2)}) async-start(f32[32,4,128]{2,1,0:T(4,128)} %bitcast.3), calls=%async_computation.1 | async-start | bytes 131072 | tf_op jit(solution)/shard_map/all_to_all | solution.py:725
  48.6 2.3 %shard_map.106 = (f32[32,128]{1,0:T(8,128)S(1)}, f32[32,512]{1,0:T(8,128)S(1)}) custom-call(f32[8,128]{1,0:T(8,128)S(1)} %fusion.1.tile, f32[32,512]{1,0:T(8,128)S(1)} %get-tuple-element.62.scaled), custom_call_target="tpu_custom_call" | custom-call | tf_op jit(solution)/shard_map/pallas_call | solution.py:726
  51.7 4.2 %all-to-all-done.1 = f32[32,4,128]{2,1,0:T(4,128)S(1)} async-done(((f32[32,4,128]{2,1,0:T(4,128)}), f32[32,4,128]{2,1,0:T(4,128)S(1)}, u32[]{:S(2)}, u32[]{:S(2)}) %all-to-all-start.1) | async-done | bytes 65568 | tf_op jit(solution)/shard_map/all_to_all | solution.py:725
  55.9 2.3 %shard_map.107 = (f32[44,512]{1,0:T(8,128)}, f32[44,44]{1,0:T(8,128)}) custom-call(f32[128,128]{1,0:T(8,128)S(1)} %bitcast.10, f32[32,128]{1,0:T(8,128)S(1)} %get-tuple-element.64.factor, f32[32,512]{1,0:T(8,128)S(1)} %get-tuple-element.65.head, f32[16,512]{1,0:T(8,128)S(1)} %get-tuple-element.66.snap), custom_call_target="tpu_custom_call" | custom-call | tf_op jit(solution)/shard_map/pallas_call | solution.py:729
  (36 shorter events, 4.0 us)
Async XLA Ops:
  2.0 8.9 %collective-permute-start.2 = (f32[40,8,128]{2,1,0:T(8,128)S(1)}, f32[40,8,128]{2,1,0:T(8,128)S(1)}, u32[]{:S(2)}, u32[]{:S(2)}) collective-permute-start(f32[40,8,128]{2,1,0:T(8,128)S(1)} %get-tuple-element.42), channel_id=1, source_target_pairs={{0,4},{1,5},{2,6},{3,7},{4,0},{5,1},{6,2},{7,3},{8,12},{9,13},{10,... | collective-permute-start | bytes 491528 | tf_op jit(solution)/shard_map/ppermute | solution.py:632
  5.0 4.4 %collective-permute-start = (f32[3,8,128]{2,1,0:T(8,128)S(1)}, f32[3,8,128]{2,1,0:T(8,128)S(1)}, u32[]{:S(2)}, u32[]{:S(2)}) collective-permute-start(f32[3,8,128]{2,1,0:T(8,128)S(1)} %get-tuple-element.38), channel_id=1, source_target_pairs={{0,1},{1,2},{2,3},{3,0},{4,5},{5,6},{6,7},{7,4},{8,9},{9,10},{10,1... | collective-permute-start | bytes 36872 | tf_op jit(solution)/shard_map/ppermute | solution.py:624
  5.0 4.4 %collective-permute-start.1 = (f32[3,8,128]{2,1,0:T(8,128)S(1)}, f32[3,8,128]{2,1,0:T(8,128)S(1)}, u32[]{:S(2)}, u32[]{:S(2)}) collective-permute-start(f32[3,8,128]{2,1,0:T(8,128)S(1)} %get-tuple-element.39), channel_id=1, source_target_pairs={{0,3},{1,0},{2,1},{3,2},{4,7},{5,4},{6,5},{7,6},{8,11},{9,8},{10,9... | collective-permute-start | bytes 36872 | tf_op jit(solution)/shard_map/ppermute | solution.py:624
  6.8 4.0 %collective-permute-start.3 = (f32[2,8,128]{2,1,0:T(8,128)S(1)}, f32[2,8,128]{2,1,0:T(8,128)S(1)}, u32[]{:S(2)}, u32[]{:S(2)}) collective-permute-start(f32[2,8,128]{2,1,0:T(8,128)S(1)} %get-tuple-element.43), channel_id=1, source_target_pairs={{0,5},{1,6},{2,7},{3,4},{4,1},{5,2},{6,3},{7,0},{8,13},{9,14},{10,... | collective-permute-start | bytes 24584 | tf_op jit(solution)/shard_map/ppermute | solution.py:632
  6.8 4.1 %collective-permute-start.4 = (f32[2,8,128]{2,1,0:T(8,128)S(1)}, f32[2,8,128]{2,1,0:T(8,128)S(1)}, u32[]{:S(2)}, u32[]{:S(2)}) collective-permute-start(f32[2,8,128]{2,1,0:T(8,128)S(1)} %get-tuple-element.44), channel_id=1, source_target_pairs={{0,7},{1,4},{2,5},{3,6},{4,3},{5,0},{6,1},{7,2},{8,15},{9,12},{10,... | collective-permute-start | bytes 24584 | tf_op jit(solution)/shard_map/ppermute | solution.py:632
  9.8 13.7 %copy-start.2 = (f32[32]{0:T(128)S(1)}, f32[32]{0:T(128)}, u32[]{:S(2)}) copy-start(f32[32]{0:T(128)} %param.13) | copy-start | bytes 388
  9.8 13.7 %copy-start.1 = (f32[32,512]{1,0:T(8,128)S(1)}, f32[32,512]{1,0:T(8,128)}, u32[]{:S(2)}) copy-start(f32[32,512]{1,0:T(8,128)} %basis.1) | copy-start | bytes 196612
  10.8 19.4 %copy-start = (s32[2,16,128]{2,1,0:T(8,128)S(1)}, s32[2,16,128]{2,1,0:T(8,128)}, u32[]{:S(2)}) copy-start(s32[2,16,128]{2,1,0:T(8,128)} %row_map.5) | copy-start | bytes 49156
  11.1 6.4 %collective-permute-start.5 = (f32[16,8,128]{2,1,0:T(8,128)S(1)}, f32[16,8,128]{2,1,0:T(8,128)S(1)}, u32[]{:S(2)}, u32[]{:S(2)}) collective-permute-start(f32[16,8,128]{2,1,0:T(8,128)S(1)} %get-tuple-element.47), channel_id=1, source_target_pairs={{0,8},{8,16},{16,24},{24,0},{1,9},{9,17},{17,25},{25,1},{2,10},{10... | collective-permute-start | bytes 196616 | tf_op jit(solution)/shard_map/ppermute | solution.py:624
  12.8 6.2 %collective-permute-start.6 = (f32[16,8,128]{2,1,0:T(8,128)S(1)}, f32[16,8,128]{2,1,0:T(8,128)S(1)}, u32[]{:S(2)}, u32[]{:S(2)}) collective-permute-start(f32[16,8,128]{2,1,0:T(8,128)S(1)} %get-tuple-element.48), channel_id=1, source_target_pairs={{0,24},{8,0},{16,8},{24,16},{1,25},{9,1},{17,9},{25,17},{2,26},{10... | collective-permute-start | bytes 196616 | tf_op jit(solution)/shard_map/ppermute | solution.py:624
  19.6 12.3 %collective-permute-start.7 = (f32[37,8,128]{2,1,0:T(8,128)S(1)}, f32[37,8,128]{2,1,0:T(8,128)S(1)}, u32[]{:S(2)}, u32[]{:S(2)}) collective-permute-start(f32[37,8,128]{2,1,0:T(8,128)S(1)} %get-tuple-element.51), channel_id=1, source_target_pairs={{0,8},{8,16},{16,24},{24,0},{1,9},{9,17},{17,25},{25,1},{2,10},{10... | collective-permute-start | bytes 454664 | tf_op jit(solution)/shard_map/ppermute | solution.py:624
  20.6 11.3 %collective-permute-start.8 = (f32[37,8,128]{2,1,0:T(8,128)S(1)}, f32[37,8,128]{2,1,0:T(8,128)S(1)}, u32[]{:S(2)}, u32[]{:S(2)}) collective-permute-start(f32[37,8,128]{2,1,0:T(8,128)S(1)} %get-tuple-element.52), channel_id=1, source_target_pairs={{0,24},{8,0},{16,8},{24,16},{1,25},{9,1},{17,9},{25,17},{2,26},{10... | collective-permute-start | bytes 454664 | tf_op jit(solution)/shard_map/ppermute | solution.py:624
  23.9 3.6 %collective-permute-start.9 = (f32[8,128]{1,0:T(8,128)S(1)}, f32[8,128]{1,0:T(8,128)S(1)}, u32[]{:S(2)}, u32[]{:S(2)}) collective-permute-start(f32[8,128]{1,0:T(8,128)S(1)} %get-tuple-element.57), channel_id=1, source_target_pairs={{0,4},{4,0},{1,5},{5,1},{2,6},{6,2},{3,7},{7,3},{8,12},{12,8},{9,1... | collective-permute-start | bytes 12296 | tf_op jit(solution)/shard_map/ppermute | solution.py:624
  27.5 10.1 %collective-permute-start.10 = (f32[8,128]{1,0:T(8,128)S(1)}, f32[8,128]{1,0:T(8,128)S(1)}, u32[]{:S(2)}, u32[]{:S(2)}) collective-permute-start(f32[8,128]{1,0:T(8,128)S(1)} %add.24), channel_id=1, source_target_pairs={{0,2},{1,3},{2,0},{3,1},{4,6},{5,7},{6,4},{7,5},{8,10},{9,11},{10,... | collective-permute-start | bytes 12296 | tf_op jit(solution)/shard_map/ppermute | solution.py:624
  28.5 9.1 %collective-permute-start.11 = (f32[8,128]{1,0:T(8,128)S(1)}, f32[8,128]{1,0:T(8,128)S(1)}, u32[]{:S(2)}, u32[]{:S(2)}) collective-permute-start(f32[8,128]{1,0:T(8,128)S(1)} %add.24), channel_id=1, source_target_pairs={{0,1},{1,2},{2,3},{3,0},{4,5},{5,6},{6,7},{7,4},{8,9},{9,10},{10,1... | collective-permute-start | bytes 12296 | tf_op jit(solution)/shard_map/ppermute | solution.py:624
  28.5 9.2 %collective-permute-start.12 = (f32[8,128]{1,0:T(8,128)S(1)}, f32[8,128]{1,0:T(8,128)S(1)}, u32[]{:S(2)}, u32[]{:S(2)}) collective-permute-start(f32[8,128]{1,0:T(8,128)S(1)} %add.24), channel_id=1, source_target_pairs={{0,3},{1,0},{2,1},{3,2},{4,7},{5,4},{6,5},{7,6},{8,11},{9,8},{10,9... | collective-permute-start | bytes 12296 | tf_op jit(solution)/shard_map/ppermute | solution.py:624
  34.2 9.5 %all-to-all-start = ((f32[8,24,256]{2,1,0:T(8,128)}), f32[8,24,256]{2,1,0:T(8,128)S(1)}, u32[]{:S(2)}, u32[]{:S(2)}) async-start(f32[8,24,256]{2,1,0:T(8,128)} %bitcast.1), calls=%async_computation | async-start | bytes 393216 | tf_op jit(solution)/shard_map/all_to_all | solution.py:718
  38.0 10.5 %collective-permute-start.13 = (f32[11,8,128]{2,1,0:T(8,128)S(1)}, f32[11,8,128]{2,1,0:T(8,128)S(1)}, u32[]{:S(2)}, u32[]{:S(2)}) collective-permute-start(f32[11,8,128]{2,1,0:T(8,128)S(1)} %get-tuple-element.59), channel_id=1, source_target_pairs={{0,8},{8,16},{16,24},{24,0},{1,9},{9,17},{17,25},{25,1},{2,10},{10... | collective-permute-start | bytes 135176 | tf_op jit(solution)/shard_map/ppermute | solution.py:624
  38.1 10.5 %collective-permute-start.14 = (f32[11,8,128]{2,1,0:T(8,128)S(1)}, f32[11,8,128]{2,1,0:T(8,128)S(1)}, u32[]{:S(2)}, u32[]{:S(2)}) collective-permute-start(f32[11,8,128]{2,1,0:T(8,128)S(1)} %get-tuple-element.60), channel_id=1, source_target_pairs={{0,24},{8,0},{16,8},{24,16},{1,25},{9,1},{17,9},{25,17},{2,26},{10... | collective-permute-start | bytes 135176 | tf_op jit(solution)/shard_map/ppermute | solution.py:624
  41.9 6.6 %collective-permute-start.15 = (f32[8,128]{1,0:T(8,128)S(1)}, f32[8,128]{1,0:T(8,128)S(1)}, u32[]{:S(2)}, u32[]{:S(2)}) collective-permute-start(f32[8,128]{1,0:T(8,128)S(1)} %add_add_fusion.rider), channel_id=1, source_target_pairs={{0,16},{8,24},{16,0},{24,8},{1,17},{9,25},{17,1},{25,9},{2,18},{10... | collective-permute-start | bytes 12296 | tf_op jit(solution)/shard_map/ppermute | solution.py:624
  44.8 11.1 %all-to-all-start.1 = ((f32[32,4,128]{2,1,0:T(4,128)}), f32[32,4,128]{2,1,0:T(4,128)S(1)}, u32[]{:S(2)}, u32[]{:S(2)}) async-start(f32[32,4,128]{2,1,0:T(4,128)} %bitcast.3), calls=%async_computation.1 | async-start | bytes 131072 | tf_op jit(solution)/shard_map/all_to_all | solution.py:725
